TPU v7x, 32 devices: a whole 2x2x4 slice. The times are simulated.
32 devices in a mesh: harm: 2 (over y), sx: 4 (over z), sy: 4 (over x, core).
Axes of the slice: x: 2, y: 2, z: 4, core: 2. Of those that a mesh axis runs over, the one named last changes fastest.
Arguments:
- potential_start: float32 [32, 16, 256, 512], P('harm', None, 'sx', 'sy'), may hold values from -6 to 6
- material: int32 [16, 256, 512], P(None, 'sx', 'sy'), may hold values from 0 to 2
- coil_amps: int32 [32], P('harm'), may hold values from -4 to 4
- nu_low: float32 [3], replicated, may hold values from 0.2 to 1
- nu_rise: float32 [3], replicated, may hold values from 0.5 to 2
- conductivity: float32 [3], replicated, may hold values from 0.5 to 4
Outputs:
- potential: float32 [32, 16, 256, 512], P('harm', None, 'sx', 'sy')
- heat_density: float32 [16, 256, 512], P('harm', 'sx', 'sy')
All inputs are finite; a program needn't handle non-finite values.
Results may differ from a plain program's by a relative error of at most 0.0003.
Values sent between devices are 32-bit elements; how exact they have to be, the bound alone decides.
No kernel may reach another device: no remote copies, remote signals or barrier semaphores. Data moves between devices by JAX's collectives and lax.ppermute only.
A program may use at most 256 MiB of HBM per device.

v0:
```python
import math

import jax
import jax.numpy as jnp
from jax import lax
from jax.sharding import PartitionSpec as P

NT = 128
ITERS = 3


relax_factor = 0.5
omega_base = 0.25
saturation = 3.0
coil_scale = 0.5


def passed_along(value, axis, by):
    length = lax.axis_size(axis)
    pairs = [(i, i + by) for i in range(length) if 0 <= i + by < length]
    return lax.ppermute(value, axis, pairs)


def basis_table(count, samples):
    coef_index = jnp.arange(count, dtype=jnp.int32)
    harmonic = 2 * (coef_index // 2) + 1
    sample_index = jnp.arange(samples, dtype=jnp.int32)
    turns = harmonic[:, None] * sample_index[None, :] % samples
    angle_grid = turns.astype(jnp.float32) * (2.0 * math.pi / samples)
    return jnp.where((coef_index % 2 == 0)[:, None], jnp.cos(angle_grid), jnp.sin(angle_grid))


def frequencies(first, count):
    coef_index = first + jnp.arange(count, dtype=jnp.int32)
    return omega_base * (2 * (coef_index // 2) + 1).astype(jnp.float32)


def lookup(values, material):
    return jnp.where(material == 0, values[0], jnp.where(material == 1, values[1], values[2]))


def reluctivity(field_x, field_y, low_cell, rise_cell):
    scaled = jnp.sqrt(1.0 + (field_x * field_x + field_y * field_y) / (saturation * saturation))
    langevin = 1.0 / jnp.tanh(scaled) - 1.0 / scaled
    return low_cell + rise_cell * (1.0 - 3.0 * langevin / scaled)


def time_rate(potential, frequency):
    shape = potential.shape
    paired = potential.reshape((shape[0] // 2, 2) + shape[1:])
    turned = jnp.stack([paired[:, 1], -paired[:, 0]], axis=1).reshape(shape)
    return turned * frequency[:, None, None, None]


def sample_grid(basis, spectrum):
    return jnp.einsum("ct,czxy->tzxy", basis, spectrum, precision=lax.Precision.HIGHEST)


def sample_rim(basis, spectrum):
    return jnp.einsum("ct,czy->tzy", basis, spectrum, precision=lax.Precision.HIGHEST)


def project(basis, sampled):
    scale = 2.0 / sampled.shape[0]
    return scale * jnp.einsum("ct,tzxy->czxy", basis, sampled, precision=lax.Precision.HIGHEST)


def local(potential_start, material, coil_amps, nu_low, nu_rise, conductivity):
    group_size = lax.axis_size("harm")
    harm_place = lax.axis_index("harm")
    own_count = potential_start.shape[0]
    layers = potential_start.shape[1]
    all_coefs = own_count * group_size
    slab_depth = layers // group_size
    basis = basis_table(all_coefs, NT)
    frequency = frequencies(harm_place * own_count, own_count)
    low_cell = lookup(nu_low, material)
    rise_cell = lookup(nu_rise, material)
    sigma_cell = lookup(conductivity, material)
    slab_material = lax.dynamic_slice_in_dim(material, harm_place * slab_depth, slab_depth, 0)
    low_slab = lookup(nu_low, slab_material)[None]
    rise_slab = lookup(nu_rise, slab_material)[None]
    sigma_slab = lookup(conductivity, slab_material)
    source = (
        coil_amps.astype(jnp.float32)[:, None, None, None]
        * jnp.where(material == 1, coil_scale, 0.0)[None]
    )
    precond = 4.0 * (low_cell + rise_cell)[None] + sigma_cell[None] * frequency[:, None, None, None]
    potential = potential_start
    for sweep in range(ITERS):
        rim_x = passed_along(potential[:, :, 0, :], "sx", -1)
        rim_y = passed_along(potential[:, :, :, 0], "sy", -1)
        arrived, rims_x, rims_y = (
            lax.all_to_all(potential, "harm", split_axis=1, concat_axis=0, tiled=True),
            lax.all_to_all(rim_x, "harm", split_axis=1, concat_axis=0, tiled=True),
            lax.all_to_all(rim_y, "harm", split_axis=1, concat_axis=0, tiled=True),
        )
        sampled = sample_grid(basis, arrived)
        rim_rows = sample_rim(basis, rims_x)
        rim_cols = sample_rim(basis, rims_y)
        ahead_x = jnp.concatenate([sampled[:, :, 1:, :], rim_rows[:, :, None, :]], axis=2)
        ahead_y = jnp.concatenate([sampled[:, :, :, 1:], rim_cols[:, :, :, None]], axis=3)
        sample_x = ahead_y - sampled
        sample_y = sampled - ahead_x
        recip = reluctivity(sample_x, sample_y, low_slab, rise_slab)
        product_x = recip * sample_x
        product_y = recip * sample_y
        inten_x = project(basis, product_x)
        inten_y = project(basis, product_y)
        own_x, own_y = (
            lax.all_to_all(inten_x, "harm", split_axis=0, concat_axis=1, tiled=True),
            lax.all_to_all(inten_y, "harm", split_axis=0, concat_axis=1, tiled=True),
        )
        back_rows = passed_along(own_y[:, :, -1, :], "sx", 1)
        back_cols = passed_along(own_x[:, :, :, -1], "sy", 1)
        behind_x = jnp.concatenate([back_rows[:, :, None, :], own_y[:, :, :-1, :]], axis=2)
        behind_y = jnp.concatenate([back_cols[:, :, :, None], own_x[:, :, :, :-1]], axis=3)
        curl_h = own_y - behind_x - (own_x - behind_y)
        residual = curl_h + sigma_cell[None] * time_rate(potential, frequency) - source
        potential = potential - relax_factor * residual / precond
    final_rate = time_rate(potential, frequency)
    gathered_rate = lax.all_to_all(final_rate, "harm", split_axis=1, concat_axis=0, tiled=True)
    current = sample_grid(basis, gathered_rate)
    heat_density = sigma_slab * jnp.mean(current * current, axis=0) / all_coefs
    return (potential, heat_density)


def solution(mesh):
    in_specs = (P("harm", None, "sx", "sy"), P(None, "sx", "sy"), P("harm"), P(), P(), P())
    out_specs = (P("harm", None, "sx", "sy"), P("harm", "sx", "sy"))
    return jax.shard_map(local, mesh=mesh, in_specs=in_specs, out_specs=out_specs, check_vma=False)
```

profile of v0, /device:TPU:16, one launch (start us, length us, event | category | flops | bytes accessed | tf_op | source)
XLA Modules:
  0.0 1888.4 jit_solution(10159678809375592771)
XLA Ops:
  23.3 8.4 copy.157
  51.1 81.0 %all-to-all-done = f32[16,16,64,128]{3,2,0,1:T(8,128)} async-done(((f32[16,16,64,128]{3,2,0,1:T(8,128)}), f32[16,16,64,128]{3,2,0,1:T(8,128)}, u32[]{:S(2)}, u32[]{:S(2)}) %all-to-all-start) | async-done | bytes 8388640 | tf_op jit(solution)/shard_map/all_to_all | solution.py:94
  132.1 11.5 copy.158
  143.6 65.5 %fusion.62 = f32[128,8,64,128]{0,3,2,1:T(8,128)S(1)} fusion(f32[32,8,64,128]{3,0,2,1:T(8,128)} %bitcast.237, s32[32]{0:T(128)S(1)} %fusion.69, pred[32]{0:T(512)(128)(4,1)S(1)} %fusion.67), kind=kOutput, calls=%fused_computation.113 | convolution fusion | flops 3221286912 | bytes 41943200 | tf_op jit(solution)/shard_map/ct,czxy->tzxy/dot_general | solution.py:56
  209.1 13.7 slice.174
  222.8 11.8 slice.173
  240.8 64.4 %broadcast_multiply_fusion.6 = f32[32,8,64,128]{3,0,2,1:T(8,128)} fusion(f32[128,8,64,128]{0,3,2,1:T(8,128)S(1)} %fusion.62, f32[128,8,1,128]{0,3,2,1:T(8,128)S(1)} %copy-done.29, f32[128,8,63,128]{0,3,2,1:T(8,128)} %slice.174, f32[8,64,128]{2,1,0:T(8,128)S(1)} %copy-done.33, f32[8,64,128]{2,1,0:T(8,128)S(1)} %copy-done.45, ...), kind=kOutput, calls=%fused_computation.67 | convolution fusion | flops 3374317568 | bytes 109592576 | tf_op jit(solution)/shard_map/ct,tzxy->czxy/dot_general | solution.py:65
  305.2 11.5 copy.166
  323.9 71.1 %broadcast_multiply_fusion.5 = f32[32,8,64,128]{3,0,2,1:T(8,128)S(1)} fusion(f32[128,8,64,128]{0,3,2,1:T(8,128)} %copy-done.1, f32[128,8,64,1]{0,3,2,1:T(1,128)S(1)} %bitcast.269, f32[128,8,64,127]{0,3,2,1:T(8,128)} %slice.173, f32[8,64,128]{2,1,0:T(8,128)S(1)} %copy-done.34, f32[8,64,128]{2,1,0:T(8,128)S(1)} %copy-done.46, ...), kind=kOutput, calls=%fused_computation.66 | convolution fusion | flops 3374317568 | bytes 109592576 | tf_op jit(solution)/shard_map/ct,tzxy->czxy/dot_general | solution.py:65
  395.0 8.2 copy.169
  403.2 13.9 all-to-all-done.3
  440.4 8.7 copy.261
  461.6 55.0 %all-to-all-done.4 = f32[32,8,64,128]{3,2,1,0:T(8,128)} async-done(((f32[32,8,64,128]{3,2,1,0:T(8,128)}), f32[32,8,64,128]{3,2,1,0:T(8,128)}, u32[]{:S(2)}, u32[]{:S(2)}) %all-to-all-start.4) | async-done | bytes 8388640 | tf_op jit(solution)/shard_map/all_to_all | solution.py:111
  516.6 8.2 copy.260
  556.7 27.6 %fusion.14 = f32[16,16,64,128]{3,1,0,2:T(8,128)S(1)} fusion(f32[16,16,63,128]{3,1,0,2:T(8,128)} %slice.176, f32[16,16,1,128]{3,1,0,2:T(8,128)S(1)} %bitcast.272, f32[16,16,64,127]{3,1,0,2:T(8,128)} %bitcast.236, f32[16,16,64,1]{3,1,0,2:T(8,128)} %copy.172, f32[16,16,64,128]{3,2,1,0:T(8,128)} %param.6, f32[16,16,64,128]{3,1,0,2:T(8,128)} %bitcast.240, ...), kind=kLoop, calls=%fused_computation.27 | loop fusion | flops 31457280 | bytes 60293248 | tf_op jit(solution)/shard_map/sub | solution.py:120
  611.4 9.4 copy.179
  632.9 88.7 %all-to-all-done.5 = f32[16,16,64,128]{3,0,2,1:T(8,128)} async-done(((f32[16,16,64,128]{3,0,2,1:T(8,128)}), f32[16,16,64,128]{3,0,2,1:T(8,128)}, u32[]{:S(2)}, u32[]{:S(2)}) %all-to-all-start.5) | async-done | bytes 8388640 | tf_op jit(solution)/shard_map/all_to_all | solution.py:94
  729.4 56.2 %fusion.58 = f32[128,8,64,128]{0,3,2,1:T(8,128)S(1)} fusion(f32[32,8,64,128]{3,0,2,1:T(8,128)} %bitcast.238, s32[32]{0:T(128)S(1)} %copy-done.52, pred[32]{0:T(512)(128)(4,1)S(1)} %copy-done.56), kind=kOutput, calls=%fused_computation.109 | convolution fusion | flops 3221286912 | bytes 41943200 | tf_op jit(solution)/shard_map/ct,czxy->tzxy/dot_general | solution.py:56
  785.7 13.7 slice.183
  799.3 11.8 slice.181
  817.4 64.4 %broadcast_multiply_fusion.4 = f32[32,8,64,128]{3,0,2,1:T(8,128)} fusion(f32[128,8,64,128]{0,3,2,1:T(8,128)S(1)} %fusion.58, f32[128,8,1,128]{0,3,2,1:T(8,128)S(1)} %copy-done.31, f32[128,8,63,128]{0,3,2,1:T(8,128)} %slice.183, f32[8,64,128]{2,1,0:T(8,128)S(1)} %copy-done.35, f32[8,64,128]{2,1,0:T(8,128)S(1)} %copy-done.47, ...), kind=kOutput, calls=%fused_computation.65 | convolution fusion | flops 3374317568 | bytes 109592576 | tf_op jit(solution)/shard_map/ct,tzxy->czxy/dot_general | solution.py:65
  881.8 11.5 copy.189
  900.5 71.3 %broadcast_multiply_fusion.3 = f32[32,8,64,128]{3,0,2,1:T(8,128)S(1)} fusion(f32[128,8,64,128]{0,3,2,1:T(8,128)} %copy-done.2, f32[128,8,64,1]{0,3,2,1:T(1,128)S(1)} %bitcast.271, f32[128,8,64,127]{0,3,2,1:T(8,128)} %slice.181, f32[8,64,128]{2,1,0:T(8,128)S(1)} %copy-done.36, f32[8,64,128]{2,1,0:T(8,128)S(1)} %copy-done.48, ...), kind=kOutput, calls=%fused_computation.64 | convolution fusion | flops 3374317568 | bytes 109592576 | tf_op jit(solution)/shard_map/ct,tzxy->czxy/dot_general | solution.py:65
  971.8 8.2 copy.192
  980.0 13.3 all-to-all-done.8
  1000.6 8.3 fusion.142
  1008.9 8.2 copy.259
  1024.4 68.1 %all-to-all-done.9 = f32[32,8,64,128]{3,2,1,0:T(8,128)} async-done(((f32[32,8,64,128]{3,2,1,0:T(8,128)}), f32[32,8,64,128]{3,2,1,0:T(8,128)}, u32[]{:S(2)}, u32[]{:S(2)}) %all-to-all-start.9) | async-done | bytes 8388640 | tf_op jit(solution)/shard_map/all_to_all | solution.py:111
  1092.6 8.2 copy.258
  1140.4 22.7 %fusion.17 = f32[16,16,64,128]{3,1,0,2:T(8,128)S(1)} fusion(f32[16,16,64,128]{3,1,0,2:T(8,128)} %copy-done.4, f32[16,16,63,128]{3,1,0,2:T(8,128)} %slice.186, f32[16,16,1,128]{3,1,0,2:T(8,128)S(1)} %bitcast.274, f32[16,16,64,127]{3,1,0,2:T(8,128)} %bitcast.234, f32[16,16,64,1]{3,1,0,2:T(8,128)} %copy.195, f32[16,16,64,128]{3,1,0,2:T(8,128)} %bitcast.242, ...), kind=kLoop, calls=%fused_computation.30 | loop fusion | flops 31457280 | bytes 60293248 | tf_op jit(solution)/shard_map/sub | solution.py:120
  1189.7 9.4 copy.196
  1211.2 88.6 %all-to-all-done.10 = f32[16,16,64,128]{3,0,2,1:T(8,128)} async-done(((f32[16,16,64,128]{3,0,2,1:T(8,128)}), f32[16,16,64,128]{3,0,2,1:T(8,128)}, u32[]{:S(2)}, u32[]{:S(2)}) %all-to-all-start.10) | async-done | bytes 8388640 | tf_op jit(solution)/shard_map/all_to_all | solution.py:94
  1307.7 56.3 %fusion.54 = f32[128,8,64,128]{0,3,2,1:T(8,128)S(1)} fusion(f32[32,8,64,128]{3,0,2,1:T(8,128)} %bitcast.239, s32[32]{0:T(128)S(1)} %copy-done.53, pred[32]{0:T(512)(128)(4,1)S(1)} %copy-done.57), kind=kOutput, calls=%fused_computation.105 | convolution fusion | flops 3221286912 | bytes 41943200 | tf_op jit(solution)/shard_map/ct,czxy->tzxy/dot_general | solution.py:56
  1364.0 13.7 slice.193
  1377.7 11.8 slice.191
  1395.7 64.4 %broadcast_multiply_fusion.2 = f32[32,8,64,128]{3,0,2,1:T(8,128)} fusion(f32[128,8,64,128]{0,3,2,1:T(8,128)S(1)} %fusion.54, f32[128,8,1,128]{0,3,2,1:T(8,128)S(1)} %copy-done.27, f32[128,8,63,128]{0,3,2,1:T(8,128)} %slice.193, f32[8,64,128]{2,1,0:T(8,128)S(1)} %copy-done.37, f32[8,64,128]{2,1,0:T(8,128)S(1)} %copy-done.49, ...), kind=kOutput, calls=%fused_computation.63 | convolution fusion | flops 3374317568 | bytes 109592576 | tf_op jit(solution)/shard_map/ct,tzxy->czxy/dot_general | solution.py:65
  1460.1 11.5 copy.206
  1478.8 71.2 %broadcast_multiply_fusion.1 = f32[32,8,64,128]{3,0,2,1:T(8,128)S(1)} fusion(f32[128,8,64,128]{0,3,2,1:T(8,128)} %copy-done, f32[128,8,64,1]{0,3,2,1:T(1,128)S(1)} %bitcast.267, f32[128,8,64,127]{0,3,2,1:T(8,128)} %slice.191, f32[8,64,128]{2,1,0:T(8,128)S(1)} %copy-done.38, f32[8,64,128]{2,1,0:T(8,128)S(1)} %copy-done.50, ...), kind=kOutput, calls=%fused_computation.62 | convolution fusion | flops 3374317568 | bytes 109592576 | tf_op jit(solution)/shard_map/ct,tzxy->czxy/dot_general | solution.py:65
  1550.1 8.2 copy.209
  1558.3 13.3 all-to-all-done.13
  1578.8 8.3 fusion.141
  1587.1 8.2 copy.257
  1602.2 68.5 %all-to-all-done.14 = f32[32,8,64,128]{3,2,1,0:T(8,128)} async-done(((f32[32,8,64,128]{3,2,1,0:T(8,128)}), f32[32,8,64,128]{3,2,1,0:T(8,128)}, u32[]{:S(2)}, u32[]{:S(2)}) %all-to-all-start.14) | async-done | bytes 8388640 | tf_op jit(solution)/shard_map/all_to_all | solution.py:111
  1670.7 8.2 copy.256
  1719.2 22.7 %fusion.20 = f32[16,16,64,128]{3,1,0,2:T(8,128)S(1)} fusion(f32[16,16,64,128]{3,1,0,2:T(8,128)} %copy-done.3, f32[16,16,63,128]{3,1,0,2:T(8,128)} %slice.196, f32[16,16,1,128]{3,1,0,2:T(8,128)S(1)} %bitcast.273, f32[16,16,64,127]{3,1,0,2:T(8,128)} %bitcast.231, f32[16,16,64,1]{3,1,0,2:T(8,128)} %copy.212, f32[16,16,64,128]{3,1,0,2:T(8,128)} %bitcast.241, ...), kind=kLoop, calls=%fused_computation.33 | loop fusion | flops 31457280 | bytes 60293248 | tf_op jit(solution)/shard_map/sub | solution.py:120
  1760.5 11.6 copy.215
  1772.1 80.1 %all-to-all-done.15 = f32[16,16,64,128]{3,0,2,1:T(8,128)} async-done(((f32[16,16,64,128]{3,0,2,1:T(8,128)}), f32[16,16,64,128]{3,0,2,1:T(8,128)}, u32[]{:S(2)}, u32[]{:S(2)}) %all-to-all-start.15) | async-done | bytes 8388640 | tf_op jit(solution)/shard_map/all_to_all | solution.py:122
  1856.7 28.9 %multiply_reduce_fusion = f32[8,64,128]{2,1,0:T(8,128)S(1)} fusion(f32[32,8,64,128]{3,0,2,1:T(8,128)S(1)} %bitcast.250, s32[32]{0:T(128)S(1)} %copy-done.54, pred[32]{0:T(512)(128)(4,1)S(1)} %copy-done.58), kind=kOutput, calls=%fused_computation.6 | convolution fusion | flops 3237998592 | bytes 8650912 | tf_op jit(solution)/shard_map/ct,czxy->tzxy/dot_general | solution.py:56
  (272 shorter events, 376.7 us)
Async XLA Ops:
  2.0 17.9 collective-permute-start.1
  9.8 3.2 collective-permute-start
  19.9 11.8 all-to-all-start.2
  31.7 100.3 %all-to-all-start = ((f32[16,16,64,128]{3,2,0,1:T(8,128)}), f32[16,16,64,128]{3,2,0,1:T(8,128)}, u32[]{:S(2)}, u32[]{:S(2)}) async-start(f32[16,16,64,128]{3,2,0,1:T(8,128)} %copy.157), calls=%async_computation | async-start | bytes 16777216 | tf_op jit(solution)/shard_map/all_to_all | solution.py:94
  38.9 104.7 %copy-start.51 = (s32[32]{0:T(128)}, s32[32]{0:T(128)S(1)}, u32[]{:S(2)}) copy-start(s32[32]{0:T(128)S(1)} %fusion.69) | copy-start | bytes 388
  39.0 104.7 %copy-start.55 = (pred[32]{0:T(512)(128)(4,1)}, pred[32]{0:T(512)(128)(4,1)S(1)}, u32[]{:S(2)}) copy-start(pred[32]{0:T(512)(128)(4,1)S(1)} %fusion.67) | copy-start | bytes 100
  209.1 31.7 %copy-start.1 = (f32[128,8,64,128]{0,3,2,1:T(8,128)}, f32[128,8,64,128]{0,3,2,1:T(8,128)S(1)}, u32[]{:S(2)}) copy-start(f32[128,8,64,128]{0,3,2,1:T(8,128)S(1)} %fusion.62) | copy-start | bytes 100663296
  222.8 18.0 copy-start.33
  222.8 18.0 copy-start.41
  222.8 18.0 copy-start.45
  316.8 100.3 %all-to-all-start.3 = ((f32[32,8,64,128]{3,2,1,0:T(8,128)}), f32[32,8,64,128]{3,2,1,0:T(8,128)}, u32[]{:S(2)}, u32[]{:S(2)}) async-start(f32[32,8,64,128]{3,2,1,0:T(8,128)} %copy.166), calls=%async_computation.3 | async-start | bytes 16777216 | tf_op jit(solution)/shard_map/all_to_all | solution.py:112
  417.1 99.5 %all-to-all-start.4 = ((f32[32,8,64,128]{3,2,1,0:T(8,128)}), f32[32,8,64,128]{3,2,1,0:T(8,128)}, u32[]{:S(2)}, u32[]{:S(2)}) async-start(f32[32,8,64,128]{3,2,1,0:T(8,128)} %copy.169), calls=%async_computation.4 | async-start | bytes 16777216 | tf_op jit(solution)/shard_map/all_to_all | solution.py:111
  440.4 20.8 %copy-start.71 = (s32[16]{0:T(128)S(1)}, s32[16]{0:T(128)}, u32[]{:S(2)}) copy-start(s32[16]{0:T(128)} %param.8) | copy-start | bytes 196
  452.5 104.2 %collective-permute-start.2 = (f32[16,16,128]{2,1,0:T(8,128)S(1)}, f32[16,16,128]{2,1,0:T(8,128)S(1)}, u32[]{:S(2)}, u32[]{:S(2)}) collective-permute-start(f32[16,16,128]{2,1,0:T(8,128)S(1)} %slice_bitcast_fusion.4), channel_id=1, source_target_pairs={{0,4},{4,8},{8,12},{1,5},{5,9},{9,13},{2,6},{6,10},{10,14},{3,7},{... | collective-permute-start | bytes 393224 | tf_op jit(solution)/shard_map/ppermute | solution.py:21
  460.9 95.8 %copy-start.12 = (f32[16,64,128]{2,0,1:T(8,128)}, f32[16,64,128]{2,0,1:T(8,128)S(1)}, u32[]{:S(2)}) copy-start(f32[16,64,128]{2,0,1:T(8,128)S(1)} %copy.177) | copy-start | bytes 1572868
  461.2 95.5 %copy-start.15 = (f32[16,64,128]{2,0,1:T(8,128)}, f32[16,64,128]{2,0,1:T(8,128)S(1)}, u32[]{:S(2)}) copy-start(f32[16,64,128]{2,0,1:T(8,128)S(1)} %copy.176) | copy-start | bytes 1572868
  461.2 95.5 %copy-start.68 = (f32[16]{0:T(128)}, f32[16]{0:T(128)S(1)}, u32[]{:S(2)}) copy-start(f32[16]{0:T(128)S(1)} %convert_element_type.45) | copy-start | bytes 196
  461.5 95.2 %copy-start.18 = (f32[16,64,128]{2,0,1:T(8,128)}, f32[16,64,128]{2,0,1:T(8,128)S(1)}, u32[]{:S(2)}) copy-start(f32[16,64,128]{2,0,1:T(8,128)S(1)} %copy.173) | copy-start | bytes 1572868
  540.1 9.0 collective-permute-start.3
  587.8 16.2 collective-permute-start.5
  596.6 3.2 collective-permute-start.4
  600.6 7.4 all-to-all-start.6
  608.0 12.8 all-to-all-start.7
  620.8 100.7 %all-to-all-start.5 = ((f32[16,16,64,128]{3,0,2,1:T(8,128)}), f32[16,16,64,128]{3,0,2,1:T(8,128)}, u32[]{:S(2)}, u32[]{:S(2)}) async-start(f32[16,16,64,128]{3,0,2,1:T(8,128)} %copy.179), calls=%async_computation.5 | async-start | bytes 16777216 | tf_op jit(solution)/shard_map/all_to_all | solution.py:94
  785.7 31.7 %copy-start.2 = (f32[128,8,64,128]{0,3,2,1:T(8,128)}, f32[128,8,64,128]{0,3,2,1:T(8,128)S(1)}, u32[]{:S(2)}) copy-start(f32[128,8,64,128]{0,3,2,1:T(8,128)S(1)} %fusion.58) | copy-start | bytes 100663296
  799.3 18.0 copy-start.35
  799.3 18.0 copy-start.43
  799.3 18.0 copy-start.47
  893.3 100.0 %all-to-all-start.8 = ((f32[32,8,64,128]{3,2,1,0:T(8,128)}), f32[32,8,64,128]{3,2,1,0:T(8,128)}, u32[]{:S(2)}, u32[]{:S(2)}) async-start(f32[32,8,64,128]{3,2,1,0:T(8,128)} %copy.189), calls=%async_computation.8 | async-start | bytes 16777216 | tf_op jit(solution)/shard_map/all_to_all | solution.py:112
  993.3 99.2 %all-to-all-start.9 = ((f32[32,8,64,128]{3,2,1,0:T(8,128)}), f32[32,8,64,128]{3,2,1,0:T(8,128)}, u32[]{:S(2)}, u32[]{:S(2)}) async-start(f32[32,8,64,128]{3,2,1,0:T(8,128)} %copy.192), calls=%async_computation.9 | async-start | bytes 16777216 | tf_op jit(solution)/shard_map/all_to_all | solution.py:111
  1020.5 119.9 %collective-permute-start.6 = (f32[16,16,128]{2,1,0:T(8,128)S(1)}, f32[16,16,128]{2,1,0:T(8,128)S(1)}, u32[]{:S(2)}, u32[]{:S(2)}) collective-permute-start(f32[16,16,128]{2,1,0:T(8,128)S(1)} %slice_bitcast_fusion.2), channel_id=1, source_target_pairs={{0,4},{4,8},{8,12},{1,5},{5,9},{9,13},{2,6},{6,10},{10,14},{3,7},{... | collective-permute-start | bytes 393224 | tf_op jit(solution)/shard_map/ppermute | solution.py:21
  1116.0 16.6 collective-permute-start.7
  1166.5 15.7 collective-permute-start.9
  1174.9 3.2 collective-permute-start.8
  1179.0 7.4 all-to-all-start.11
  1186.4 12.8 all-to-all-start.12
  1199.2 100.7 %all-to-all-start.10 = ((f32[16,16,64,128]{3,0,2,1:T(8,128)}), f32[16,16,64,128]{3,0,2,1:T(8,128)}, u32[]{:S(2)}, u32[]{:S(2)}) async-start(f32[16,16,64,128]{3,0,2,1:T(8,128)} %copy.196), calls=%async_computation.10 | async-start | bytes 16777216 | tf_op jit(solution)/shard_map/all_to_all | solution.py:94
  1364.0 31.7 %copy-start = (f32[128,8,64,128]{0,3,2,1:T(8,128)}, f32[128,8,64,128]{0,3,2,1:T(8,128)S(1)}, u32[]{:S(2)}) copy-start(f32[128,8,64,128]{0,3,2,1:T(8,128)S(1)} %fusion.54) | copy-start | bytes 100663296
  1377.7 18.0 copy-start.37
  1377.7 18.0 copy-start.39
  1377.7 18.0 copy-start.49
  1471.7 99.9 %all-to-all-start.13 = ((f32[32,8,64,128]{3,2,1,0:T(8,128)}), f32[32,8,64,128]{3,2,1,0:T(8,128)}, u32[]{:S(2)}, u32[]{:S(2)}) async-start(f32[32,8,64,128]{3,2,1,0:T(8,128)} %copy.206), calls=%async_computation.13 | async-start | bytes 16777216 | tf_op jit(solution)/shard_map/all_to_all | solution.py:112
  1571.6 99.2 %all-to-all-start.14 = ((f32[32,8,64,128]{3,2,1,0:T(8,128)}), f32[32,8,64,128]{3,2,1,0:T(8,128)}, u32[]{:S(2)}, u32[]{:S(2)}) async-start(f32[32,8,64,128]{3,2,1,0:T(8,128)} %copy.209), calls=%async_computation.14 | async-start | bytes 16777216 | tf_op jit(solution)/shard_map/all_to_all | solution.py:111
  1598.6 120.6 %collective-permute-start.10 = (f32[16,16,128]{2,1,0:T(8,128)S(1)}, f32[16,16,128]{2,1,0:T(8,128)S(1)}, u32[]{:S(2)}, u32[]{:S(2)}) collective-permute-start(f32[16,16,128]{2,1,0:T(8,128)S(1)} %slice_bitcast_fusion), channel_id=1, source_target_pairs={{0,4},{4,8},{8,12},{1,5},{5,9},{9,13},{2,6},{6,10},{10,14},{3,7},{... | collective-permute-start | bytes 393224 | tf_op jit(solution)/shard_map/ppermute | solution.py:21
  1694.3 17.0 collective-permute-start.11
  1753.3 98.9 %all-to-all-start.15 = ((f32[16,16,64,128]{3,0,2,1:T(8,128)}), f32[16,16,64,128]{3,0,2,1:T(8,128)}, u32[]{:S(2)}, u32[]{:S(2)}) async-start(f32[16,16,64,128]{3,0,2,1:T(8,128)} %copy.213), calls=%async_computation.15 | async-start | bytes 16777216 | tf_op jit(solution)/shard_map/all_to_all | solution.py:122
  1856.6 28.9 %copy-start.24 = (pred[8,64,128]{2,1,0:T(8,128)(4,1)S(1)}, pred[8,64,128]{2,1,0:T(8,128)(4,1)}, u32[]{:S(2)}) copy-start(pred[8,64,128]{2,1,0:T(8,128)(4,1)} %copy-done.23) | copy-start | bytes 196612
  1856.6 28.9 %copy-start.26 = (pred[8,64,128]{2,1,0:T(8,128)(4,1)S(1)}, pred[8,64,128]{2,1,0:T(8,128)(4,1)}, u32[]{:S(2)}) copy-start(pred[8,64,128]{2,1,0:T(8,128)(4,1)} %copy-done.25) | copy-start | bytes 196612
  (51 other events, 353.2 us)
where the time goes:
time: 1900 us; the launch traced here: 1890 us
  matrix products  623 us (33%)
  waiting for transfers between devices  583 us (31%)
  local copies, waits for them, and re-layouts  425 us (22%)
  other arithmetic  134 us (7%)
  starting transfers between devices  115 us (6%)
    dot_general x6, matrix products, project(): jnp.einsum('ct,tzxy->czxy', basis, sampled, precision=lax.Precision.HIGHEST)  407 us
    all_to_all x3, waiting for transfers between devices, local(): lax.all_to_all(potential, 'harm', split_axis=1, concat_axis=0, tiled=True)  258 us
    dot_general x4, matrix products, sample_grid(): jnp.einsum('ct,czxy->tzxy', basis, spectrum, precision=lax.Precision.HIGH...  207 us
    all_to_all x3, waiting for transfers between devices, local(): lax.all_to_all(inten_x, 'harm', split_axis=0, concat_axis=1, tiled=True)  192 us
    all_to_all x1, waiting for transfers between devices, local(): lax.all_to_all(final_rate, 'harm', split_axis=1, concat_axis=0, tiled=True)  80.1 us
    unnamed x155, local copies, waits for them, and re-layouts  77.7 us
    sub x3, other arithmetic, local(): potential = potential - relax_factor * residual / precond  73.1 us
    mul x6, local copies, waits for them, and re-layouts, project(): scale * jnp.einsum('ct,tzxy->czxy', basis, sampled, precision=lax.Precisi...  59.2 us
  transfers between devices with their start and end apart: 27, of which 15 were waited for; matrix products, arithmetic and copies ran while one was open for 27% of the time, Pallas kernels for 0%

commit v1 on v0

v1 whole, which is shorter than its diff:
```python
import functools
import math

import jax
import jax.numpy as jnp
from jax import lax
from jax.experimental import pallas as pl
from jax.experimental.pallas import tpu as pltpu
from jax.sharding import PartitionSpec as P


NT = 128
ITERS = 3
HALF = NT // 2
LANES = 128
RIM = 4
STEP = 2

relax_factor = 0.5
omega_base = 0.25
saturation = 3.0
coil_scale = 0.5


def lookup(values, material):
    return jnp.where(material == 0, values[0], jnp.where(material == 1, values[1], values[2]))


def split(value):
    high = value.astype(jnp.bfloat16)
    low = (value - high.astype(jnp.float32)).astype(jnp.bfloat16)
    return high, low


def split_table(value):
    high = lax.reduce_precision(value, 8, 7)
    return high.astype(jnp.bfloat16), (value - high).astype(jnp.bfloat16)


def shifted(value, axis, by):
    length = lax.axis_size(axis)
    return lax.ppermute(value, axis, [(i, i + by) for i in range(length) if 0 <= i + by < length])


def turned(value, by):
    length = lax.axis_size("harm")
    return lax.ppermute(value, "harm", [(i, (i + by) % length) for i in range(length)])


def turned_and_shifted(value, turn, by):
    groups, length = lax.axis_size("harm"), lax.axis_size("sx")
    pairs = []
    for g in range(groups):
        for i in range(length):
            if 0 <= i + by < length:
                pairs.append((g * length + i, (g + turn) % groups * length + i + by))
    return lax.ppermute(value, ("harm", "sx"), pairs)


def gather_kernel(groups, own, layers, parts, rows, columns, place_ref, *refs):
    mains, tops, bottoms = refs[:groups], refs[groups : 2 * groups], refs[2 * groups : 3 * groups]
    image_ref, left_ref, right_ref, stage_ref = refs[3 * groups :]
    span = rows // parts
    for at in range(-RIM, span + RIM):
        pieces = []
        for g in range(groups):
            for layer in range(layers):
                for part in range(parts):
                    x = span * part + at
                    if x < 0:
                        pieces.append(tops[g][:, layer, RIM + x, :])
                    elif x >= rows:
                        pieces.append(bottoms[g][:, layer, x - rows, :])
                    else:
                        pieces.append(mains[g][:, layer, x, :])
        if own % 8 == 0:
            stacked = jnp.concatenate(pieces, axis=0)
        else:
            for k, piece in enumerate(pieces):
                stage_ref[k * own : (k + 1) * own, :] = piece
            stacked = stage_ref[...]
        flipped = jnp.transpose(stacked)
        image_ref[at + RIM] = flipped
        left_ref[at + RIM] = flipped[:8]
        right_ref[at + RIM] = flipped[columns - 8 :]


def solve_kernel(
    groups, own, layers, parts, rows, columns,
    image_ref, ahead_ref, behind_ref, code_ref, table_ref, fwd_ref, inv_ref, weight_ref, heat_scale_ref,
    *refs,
):
    outs, heat_ref = refs[:groups], refs[groups]
    pot, nu_all, nu_sat, gain, turn_gain, feed, samples_0, samples_1, products_0, products_1, last_row, back_x = refs[groups + 1 :]
    samples, products = (samples_0, samples_1), (products_0, products_1)
    span = rows // parts
    total = span + 2 * RIM
    wide = columns + 8

    def load(x, carry):
        code = code_ref[x]
        chosen = jnp.concatenate([jnp.where(code == m, 1.0, 0.0) for m in (1.0, 2.0, 3.0)] * 3, axis=0)
        picked = lax.dot_general(
            chosen.astype(jnp.bfloat16), table_ref[...], (((0,), (0,)), ((), ())), preferred_element_type=jnp.float32)
        for k, ref in enumerate((nu_all, nu_sat, gain, turn_gain, feed)):
            ref[x] = picked[:wide, k * LANES : (k + 1) * LANES]
        pot[x, 0:columns, :] = image_ref[x]
        edge = lax.broadcasted_iota(jnp.int32, (8, LANES), 0) < RIM
        pot[x, columns:wide, :] = jnp.where(edge, ahead_ref[x], behind_ref[x])
        pot[x, wide : wide + 8, :] = image_ref[x, 0:8, :]
        return carry

    lax.fori_loop(0, total, load, 0, unroll=4)
    for k in range(4 * STEP):
        pot[total + k] = jnp.zeros((wide + 8, LANES), jnp.float32)
    even = lax.broadcasted_iota(jnp.int32, (wide, LANES), 1) % 2 == 0

    def fields_at(base):
        here = [pot[base + k, 0:wide, :] for k in range(STEP + 1)]
        field_x = [pot[base + k, 1 : wide + 1, :] - here[k] for k in range(STEP)]
        field_y = [here[k] - here[k + 1] for k in range(STEP)]
        return here, field_x, field_y

    def to_samples(base, slot):
        _, field_x, field_y = fields_at(base)
        fields = jnp.concatenate([f for pair in zip(field_x, field_y) for f in pair], axis=0)
        high, low = split(fields)
        samples[slot][...] = jnp.dot(
            jnp.concatenate([high, low, high], axis=1), fwd_ref[...], preferred_element_type=jnp.float32)

    def saturate(slot):
        for k in range(STEP):
            sample_x = samples[slot][2 * k * wide : (2 * k + 1) * wide, :]
            sample_y = samples[slot][(2 * k + 1) * wide : (2 * k + 2) * wide, :]
            square = 1.0 + (sample_x * sample_x + sample_y * sample_y)
            scaled = square * lax.rsqrt(square)
            slope = jnp.tanh(scaled)
            factor = (scaled - slope) / (square * slope)
            high, low = split(jnp.concatenate([factor * sample_x, factor * sample_y], axis=0))
            products[slot][2 * k * wide : (2 * k + 2) * wide, 0 : 2 * LANES] = high
            products[slot][2 * k * wide : (2 * k + 2) * wide, 2 * LANES :] = low

    def update(base, slot):
        here, field_x, field_y = fields_at(base)
        pair = jnp.dot(products[slot][...], inv_ref[...], preferred_element_type=jnp.float32)
        back = pair[:, :LANES] + pair[:, LANES:]
        above = last_row[...]
        for k in range(STEP):
            at = base + k
            linear, bent = nu_all[at], nu_sat[at]
            inten_x = linear * field_x[k] - bent * back[2 * k * wide : (2 * k + 1) * wide]
            inten_y = linear * field_y[k] - bent * back[(2 * k + 1) * wide : (2 * k + 2) * wide]
            back_x[k, 8 : wide + 8, :] = inten_x
            back_x[k, 0:8, :] = inten_x[columns:]
            curl = (inten_y - above) - (inten_x - back_x[k, 7 : wide + 7, :])
            above = inten_y
            rotated = jnp.where(even, pltpu.roll(here[k], LANES - 1, 1), pltpu.roll(here[k], 1, 1))
            fresh = here[k] + feed[at] - gain[at] * curl - turn_gain[at] * rotated
            pot[at, 0:wide, :] = fresh
            pot[at, wide : wide + 8, :] = fresh[0:8]
        last_row[...] = above

    def sweep(index, carry):
        first = jnp.where(index == 0, 0, STEP)
        last = jnp.where(index == ITERS - 1, total - 2 * STEP, total - STEP)
        last_row[...] = jnp.zeros((wide, LANES), jnp.float32)
        to_samples(first, 0)
        saturate(0)
        to_samples(first + STEP, 1)

        def advance(step, carry):
            base = first + step * 2 * STEP
            for slot in range(2):
                saturate(1 - slot)
                update(base + slot * STEP, slot)
                to_samples(base + (slot + 2) * STEP, slot)
            return carry

        return lax.fori_loop(0, pl.cdiv(last - first, 2 * STEP), advance, carry)

    lax.fori_loop(0, ITERS, sweep, 0)

    lanes_each = layers * parts * own
    weight = weight_ref[...]

    def finish(block, carry):
        for k in range(8):
            at = pl.multiple_of(block * 8, 8) + k
            flipped = jnp.transpose(pot[block * 8 + k + RIM, 0:columns, :])
            powers = flipped * flipped * weight
            for layer in range(layers):
                for part in range(parts):
                    where = part * span + at
                    power = jnp.zeros((1, columns), jnp.float32)
                    for g in range(groups):
                        begin = g * lanes_each + (layer * parts + part) * own
                        outs[g][:, layer, pl.ds(where, 1), :] = flipped[begin : begin + own].reshape(own, 1, columns)
                        power = power + jnp.sum(powers[begin : begin + own], axis=0, keepdims=True)
                    heat_ref[layer, pl.ds(where, 1), :] = power * heat_scale_ref[layer, pl.ds(where, 1), :]
        return carry

    lax.fori_loop(0, span // 8, finish, 0)


def local(potential_start, material, coil_amps, nu_low, nu_rise, conductivity):
    groups = lax.axis_size("harm")
    place = lax.axis_index("harm")
    own, depth, rows, columns = potential_start.shape
    coefs = own * groups
    slab = depth // groups
    layers = max(d for d in (1, 2) if slab % d == 0)
    parts = LANES // (coefs * layers)
    chunks = slab // layers
    span = rows // parts
    total = span + 2 * RIM
    wide = columns + 8
    cells = layers * parts

    lane = jnp.arange(LANES, dtype=jnp.int32)
    lane_group = lane // (cells * own)
    lane_cell = lane // own % cells
    coef = (place + lane_group) % groups * own + lane % own
    harmonic = 2 * (coef // 2) + 1
    omega = omega_base * harmonic.astype(jnp.float32)
    sign = jnp.where(coef % 2 == 0, 1.0, -1.0)
    slot = jnp.arange(cells * HALF, dtype=jnp.int32)
    turns = harmonic[:, None] * (slot % HALF)[None, :] % NT
    angle = turns.astype(jnp.float32) * (2.0 * math.pi / NT)
    wave = jnp.where((coef % 2 == 0)[:, None], jnp.cos(angle), jnp.sin(angle))
    basis = jnp.where(lane_cell[:, None] == (slot // HALF)[None, :], wave, 0.0)
    fwd_high, fwd_low = split_table(basis / saturation)
    fwd = jnp.concatenate([fwd_high, fwd_high, fwd_low], axis=0)
    inv_high, inv_low = split_table((3.0 * saturation * 2.0 / HALF) * basis.T)
    inv = jnp.concatenate(
        [jnp.concatenate([inv_high, inv_low], axis=1), jnp.concatenate([inv_high, jnp.zeros_like(inv_low)], axis=1)], axis=0)
    amps = coil_amps.astype(jnp.float32)
    amps = jnp.stack([amps] + [turned(amps, -g) for g in range(1, groups)])[lane_group, lane % own]
    precond = 4.0 * (nu_low + nu_rise)[:, None] + conductivity[:, None] * omega[None, :]
    gain = relax_factor / precond
    turn_gain = gain * (conductivity[:, None] * (omega * sign)[None, :])
    feed = gain * jnp.where(jnp.arange(3) == 1, coil_scale, 0.0)[:, None] * amps[None, :]
    constants = jnp.stack(
        [jnp.broadcast_to((nu_low + nu_rise)[:, None], (3, LANES)), jnp.broadcast_to(nu_rise[:, None], (3, LANES)),
         gain, turn_gain, feed], axis=1)
    mine_only = jnp.arange(8)[:, None] == lane_cell[None, :]
    constants = jnp.where(mine_only[None, :, None, :], constants[:, None], 0.0).reshape(24, 5 * LANES)
    top = lax.reduce_precision(constants, 8, 7)
    middle = lax.reduce_precision(constants - top, 8, 7)
    table = jnp.concatenate([top, middle, constants - top - middle], axis=0).astype(jnp.bfloat16)
    weight = jnp.broadcast_to((omega * omega)[:, None], (LANES, columns))

    def part_of(value, group, start, count):
        return lax.dynamic_slice_in_dim(value, group * slab + start, count, 1)

    tops, bottoms = [], []
    arrivals = [[] for _ in range(chunks)]
    for k in range(chunks):
        for g in range(1, groups):
            arrivals[k].append(turned(part_of(potential_start, (place - g) % groups, k * layers, layers), -g))
    for g in range(groups):
        whose = (place - g) % groups
        mine = part_of(potential_start, whose, 0, slab)
        tops.append(turned_and_shifted(mine[:, :, rows - RIM :, :], -g, 1))
        bottoms.append(turned_and_shifted(mine[:, :, :RIM, :], -g, -1))

    slab_material = lax.dynamic_slice_in_dim(material, place * slab, slab, 0)
    heat_scale = lookup(conductivity, slab_material) * (0.5 / coefs)
    code = (slab_material + 1).astype(jnp.float32)
    code = jnp.concatenate(
        [shifted(code[:, rows - RIM :, :], "sx", 1), code, shifted(code[:, :RIM, :], "sx", -1)], axis=1)
    code = jnp.concatenate(
        [code, shifted(code[:, :, :RIM], "sy", -1), shifted(code[:, :, columns - RIM :], "sy", 1)], axis=2)
    code = jnp.stack([code[:, part * span : part * span + total] for part in range(parts)], axis=1)
    code = code.reshape(chunks, cells, total, wide).transpose(0, 2, 1, 3)
    code = jnp.pad(code, ((0, 0), (0, 0), (0, 8 - cells), (0, 0)))

    any_space = pl.BlockSpec(memory_space=pltpu.VMEM)
    gather = pl.pallas_call(
        functools.partial(gather_kernel, groups, own, layers, parts, rows, columns),
        grid_spec=pltpu.PrefetchScalarGridSpec(
            num_scalar_prefetch=1,
            grid=(1,),
            in_specs=[pl.BlockSpec((own, layers, rows, columns), lambda i, s: (0, s[0], 0, 0))]
            + [pl.BlockSpec((own, layers, rows, columns), lambda i, s: (0, 0, 0, 0))] * (groups - 1)
            + [pl.BlockSpec((own, layers, RIM, columns), lambda i, s: (0, s[1], 0, 0))] * (2 * groups),
            out_specs=[
                pl.BlockSpec((total, columns, LANES), lambda i, s: (0, 0, 0)),
                pl.BlockSpec((total, 8, LANES), lambda i, s: (0, 0, 0)),
                pl.BlockSpec((total, 8, LANES), lambda i, s: (0, 0, 0)),
            ],
            scratch_shapes=[pltpu.VMEM((LANES, columns), jnp.float32)],
        ),
        out_shape=[
            jax.ShapeDtypeStruct((total, columns, LANES), jnp.float32),
            jax.ShapeDtypeStruct((total, 8, LANES), jnp.float32),
            jax.ShapeDtypeStruct((total, 8, LANES), jnp.float32),
        ],
        cost_estimate=pl.CostEstimate(flops=0, bytes_accessed=4 * total * columns * LANES * 2, transcendentals=0),
    )
    solve = pl.pallas_call(
        functools.partial(solve_kernel, groups, own, layers, parts, rows, columns),
        in_specs=[any_space] * 9,
        out_specs=[any_space] * (groups + 1),
        out_shape=[jax.ShapeDtypeStruct((own, layers, rows, columns), jnp.float32)] * groups
        + [jax.ShapeDtypeStruct((layers, rows, columns), jnp.float32)],
        scratch_shapes=[pltpu.VMEM((total + 4 * STEP, wide + 8, LANES), jnp.float32)]
        + [pltpu.VMEM((total, wide, LANES), jnp.float32)] * 5
        + [pltpu.VMEM((2 * STEP * wide, 2 * LANES), jnp.float32)] * 2
        + [pltpu.VMEM((2 * STEP * wide, 4 * LANES), jnp.bfloat16)] * 2
        + [pltpu.VMEM((wide, LANES), jnp.float32), pltpu.VMEM((STEP, wide + 8, LANES), jnp.float32)],
        cost_estimate=pl.CostEstimate(
            flops=6 * total * wide * 256 * 256 * 8, bytes_accessed=4 * total * wide * LANES * 4, transcendentals=0),
    )

    potential = jnp.zeros_like(potential_start)
    heats = []
    for k in range(chunks):
        where = jnp.stack([place * chunks + k, jnp.int32(k)]).astype(jnp.int32)
        image, left, right = gather(where, potential_start, *arrivals[k], *tops, *bottoms)
        ahead = shifted(left, "sy", -1)
        behind = shifted(right, "sy", 1)
        *fresh, heat = solve(
            image, ahead, behind, code[k], table, fwd, inv, weight,
            heat_scale[k * layers : (k + 1) * layers])
        heats.append(heat)
        potential = lax.dynamic_update_slice_in_dim(potential, fresh[0], place * slab + k * layers, 1)
        for g in range(1, groups):
            sent = turned(fresh[g], g)
            potential = lax.dynamic_update_slice_in_dim(potential, sent, (place - g) % groups * slab + k * layers, 1)
    return potential, jnp.concatenate(heats, axis=0)


def solution(mesh):
    in_specs = (P("harm", None, "sx", "sy"), P(None, "sx", "sy"), P("harm"), P(), P(), P())
    out_specs = (P("harm", None, "sx", "sy"), P("harm", "sx", "sy"))

    return jax.shard_map(local, mesh=mesh, in_specs=in_specs, out_specs=out_specs, check_vma=False)
```

time: 1900 us -> 344 us (0.18)
  matrix products: 623 us -> 0 us
  waiting for transfers between devices: 583 us -> 56.8 us
  local copies, waits for them, and re-layouts: 425 us -> 20 us
  Pallas kernels: 0 us -> 192 us
  other arithmetic: 134 us -> 9.91 us
  starting transfers between devices: 115 us -> 62.5 us
    dot_general x16 -> x0, matrix products: 623 us -> none  [the longest x6 407 us: project(): jnp.einsum('ct,tzxy->czxy', basis, sampled, precision=lax.Precision.HIGHEST)]
    all_to_all x15 -> x0, waiting for transfers between devices: 577 us -> none  [the longest x3 258 us: local(): lax.all_to_all(potential, 'harm', split_axis=1, concat_axis=0, tiled=True)]
    pallas_call x0 -> x8, Pallas kernels: none -> 192 us  [the longest x4 171 us: local(): solve(image, ahead, behind, code[k], table, fwd, inv, weight, heat_scale[...]
    slice x19 -> x4, local copies, waits for them, and re-layouts: 153 us -> 3.38 us  [the longest x1 2.51 us: local(): bottoms.append(turned_and_shifted(mine[:, :, :RIM, :], -g, -1))]
    all_to_all x15 -> x0, starting transfers between devices: 88.2 us -> none  [the longest x3 21.7 us: local(): lax.all_to_all(inten_x, 'harm', split_axis=0, concat_axis=1, tiled=True)]
    all_to_all x17 -> x0, local copies, waits for them, and re-layouts: 82.1 us -> none  [the longest x3 27.3 us: local(): lax.all_to_all(potential, 'harm', split_axis=1, concat_axis=0, tiled=True)]
    sub x3 -> x0, other arithmetic: 73.1 us -> none  [local(): potential = potential - relax_factor * residual / precond]
    unnamed x155 -> x52, local copies, waits for them, and re-layouts: 77.7 us -> 4.89 us
  transfers between devices with their start and end apart: 27 -> 25, of which waited for: 15 -> 8; matrix products, arithmetic and copies ran while one was open for 27% -> 6% of each run, Pallas kernels for 0% -> 56%
where the time goes in v1:
time: 344 us; the launch traced here: 342 us
  Pallas kernels  192 us (56%)
  starting transfers between devices  62.5 us (18%)
  waiting for transfers between devices  56.8 us (17%)
  local copies, waits for them, and re-layouts  20 us (6%)
  other arithmetic  9.91 us (3%)
    pallas_call x4, Pallas kernels, local(): solve(image, ahead, behind, code[k], table, fwd, inv, weight, heat_scale[...  171 us
    ppermute x9, waiting for transfers between devices, turned(): lax.ppermute(value, 'harm', [(i, (i + by) % length) for i in range(length)])  43.1 us
    ppermute x12, starting transfers between devices, shifted(): lax.ppermute(value, axis, [(i, i + by) for i in range(length) if 0 <= i +...  40.5 us
    pallas_call x4, Pallas kernels, local(): gather(where, potential_start, *arrivals[k], *tops, *bottoms)  21 us
    ppermute x4, starting transfers between devices, turned_and_shifted(): return lax.ppermute(value, ('harm', 'sx'), pairs)  11.1 us
    ppermute x9, starting transfers between devices, turned(): lax.ppermute(value, 'harm', [(i, (i + by) % length) for i in range(length)])  11 us
    ppermute x4, waiting for transfers between devices, turned_and_shifted(): return lax.ppermute(value, ('harm', 'sx'), pairs)  11 us
  transfers between devices with their start and end apart: 25, of which 8 were waited for; matrix products, arithmetic and copies ran while one was open for 6% of the time, Pallas kernels for 56%

profile of v1, /device:TPU:16, one launch (start us, length us, event | category | flops | bytes accessed | tf_op | source)
XLA Modules:
  0.0 342.4 jit_solution(1566457748856816372)
XLA Ops:
  0.7 4.1 %constant_dynamic-slice_fusion.2 = (f32[16,2,64,128]{3,2,1,0:T(8,128)S(1)}, f32[16,2,64,128]{3,2,1,0:T(8,128)}, f32[16,2,64,128]{3,2,1,0:T(8,128)}, f32[16,2,64,128]{3,2,1,0:T(8,128)}) fusion(f32[16,16,64,128]{3,2,1,0:T(8,128)} %refs_0_.7, s32[]{:T(128)S(6)} %select_n.338, s32[]{:T(128)S(6)} %select_n.336, s32[]{:T(128)S(6)} %select_n.334, s32[]{:T(128)S(6)} %select_n.305), kind=kLoop, calls=%fused_computation.56 | loop fusion | bytes 8388624 | tf_op jit(solution)/shard_map/dynamic_slice | solution.py:253
  4.9 1.5 collective-permute-start
  6.4 2.5 constant_dynamic-slice_fusion.5
  8.9 3.5 %collective-permute-start.1 = (f32[16,8,4,128]{3,2,1,0:T(4,128)}, f32[16,8,4,128]{3,2,1,0:T(4,128)S(1)}, u32[]{:S(2)}, u32[]{:S(2)}) collective-permute-start(f32[16,8,4,128]{3,2,1,0:T(4,128)} %get-tuple-element.60), channel_id=1, source_target_pairs={{0,4},{4,8},{8,12},{16,20},{20,24},{24,28},{1,5},{5,9},{9,13},{17,... | collective-permute-start | bytes 786440 | tf_op jit(solution)/shard_map/ppermute | solution.py:57
  12.4 1.9 collective-permute-start.2
  14.4 3.9 %collective-permute-start.8 = (f32[8,4,128]{2,1,0:T(4,128)S(1)}, f32[8,4,128]{2,1,0:T(4,128)S(1)}, u32[]{:S(2)}, u32[]{:S(2)}) collective-permute-start(f32[8,4,128]{2,1,0:T(4,128)S(1)} %get-tuple-element.75), channel_id=1, source_target_pairs={{4,0},{8,4},{12,8},{5,1},{9,5},{13,9},{6,2},{10,6},{14,10},{7,3},{... | collective-permute-start | bytes 49160 | tf_op jit(solution)/shard_map/ppermute | solution.py:42
  18.3 1.6 collective-permute-start.11
  21.9 2.0 select_multiply_fusion
  23.9 0.7 fusion.31
  25.9 0.7 fusion.5.inv_ref
  28.6 7.2 %collective-permute-done.11 = f32[16]{0:T(128)S(1)} collective-permute-done((f32[16]{0:T(128)S(1)}, f32[16]{0:T(128)S(1)}, u32[]{:S(2)}, u32[]{:S(2)}) %collective-permute-start.11) | collective-permute-done | bytes 96 | tf_op jit(solution)/shard_map/ppermute | solution.py:47
  35.7 3.5 %collective-permute-start.7 = (f32[8,4,128]{2,1,0:T(4,128)S(1)}, f32[8,4,128]{2,1,0:T(4,128)S(1)}, u32[]{:S(2)}, u32[]{:S(2)}) collective-permute-start(f32[8,4,128]{2,1,0:T(4,128)S(1)} %get-tuple-element.74), channel_id=1, source_target_pairs={{0,4},{4,8},{8,12},{1,5},{5,9},{9,13},{2,6},{6,10},{10,14},{3,7},{... | collective-permute-start | bytes 49160 | tf_op jit(solution)/shard_map/ppermute | solution.py:42
  39.2 1.5 gather_fusion
  41.5 1.3 collective-permute-start.10
  42.8 1.3 collective-permute-start.9
  44.2 1.6 collective-permute-start.13
  45.8 2.2 collective-permute-done.9
  48.0 1.5 collective-permute-start.17
  50.3 2.4 collective-permute-start.3
  53.4 5.2 %collective-permute-done.3.refs_4_ = f32[16,8,4,128]{3,2,1,0:T(4,128)S(1)} collective-permute-done((f32[16,8,4,128]{3,2,1,0:T(4,128)S(1)}, f32[16,8,4,128]{3,2,1,0:T(4,128)S(1)}, u32[]{:S(2)}, u32[]{:S(2)}) %collective-permute-start.3) | collective-permute-done | bytes 262176 | tf_op jit(solution)/shard_map/ppermute | solution.py:57
  58.6 3.3 collective-permute-start.4
  62.1 5.7 %collective-permute-done.4.refs_5_ = f32[16,8,4,128]{3,2,1,0:T(4,128)S(1)} collective-permute-done((f32[16,8,4,128]{3,2,1,0:T(4,128)S(1)}, f32[16,8,4,128]{3,2,1,0:T(4,128)S(1)}, u32[]{:S(2)}, u32[]{:S(2)}) %collective-permute-start.4) | collective-permute-done | bytes 262176 | tf_op jit(solution)/shard_map/ppermute | solution.py:57
  68.5 5.2 %shard_map.77 = (f32[40,128,128]{2,1,0:T(8,128)}, f32[40,8,128]{2,1,0:T(8,128)}, f32[40,8,128]{2,1,0:T(8,128)}) custom-call(s32[2]{0:T(128)} %pad_add_fusion.place_ref, f32[16,16,64,128]{3,2,1,0:T(8,128)} %refs_0_.7, f32[16,2,64,128]{3,2,1,0:T(8,128)} %collective-permute-done.refs_1_, f32[16,8,4,128]{3,2,1,0:T(4,128)} %copy-done.1, ...), custom_call_target="tpu_custom_call" | custom-call | bytes 5242880 | tf_op jit(solution)/shard_map/pallas_call | solution.py:319
  73.7 1.3 collective-permute-start.5
  75.0 5.5 %collective-permute-start.6 = (f32[40,8,128]{2,1,0:T(8,128)}, f32[40,8,128]{2,1,0:T(8,128)S(1)}, u32[]{:S(2)}, u32[]{:S(2)}) collective-permute-start(f32[40,8,128]{2,1,0:T(8,128)} %get-tuple-element.28), channel_id=1, source_target_pairs={{0,1},{1,2},{2,3},{4,5},{5,6},{6,7},{8,9},{9,10},{10,11},{12,13},{... | collective-permute-start | bytes 491528 | tf_op jit(solution)/shard_map/ppermute | solution.py:42
  80.9 1.1 fusion.4
  82.0 5.3 %shard_map.79 = (f32[40,128,128]{2,1,0:T(8,128)}, f32[40,8,128]{2,1,0:T(8,128)}, f32[40,8,128]{2,1,0:T(8,128)}) custom-call(s32[2]{0:T(128)} %pad_add_fusion.1.place_ref, f32[16,16,64,128]{3,2,1,0:T(8,128)} %refs_0_.7, f32[16,2,64,128]{3,2,1,0:T(8,128)} %collective-permute-done.13.refs_1_, f32[16,8,4,128]{3,2,1,0:T(4,128)} %copy-done.1, ...), custom_call_target="tpu_custom_call" | custom-call | bytes 5242880 | tf_op jit(solution)/shard_map/pallas_call | solution.py:319
  87.3 1.3 collective-permute-start.14
  88.6 6.7 %collective-permute-done.17.refs_1_ = f32[16,2,64,128]{3,2,1,0:T(8,128)} collective-permute-done((f32[16,2,64,128]{3,2,1,0:T(8,128)}, f32[16,2,64,128]{3,2,1,0:T(8,128)}, u32[]{:S(2)}, u32[]{:S(2)}) %collective-permute-start.17) | collective-permute-done | bytes 1048608 | tf_op jit(solution)/shard_map/ppermute | solution.py:47
  95.3 8.9 %collective-permute-start.15 = (f32[40,8,128]{2,1,0:T(8,128)}, f32[40,8,128]{2,1,0:T(8,128)S(1)}, u32[]{:S(2)}, u32[]{:S(2)}) collective-permute-start(f32[40,8,128]{2,1,0:T(8,128)} %get-tuple-element.33), channel_id=1, source_target_pairs={{0,1},{1,2},{2,3},{4,5},{5,6},{6,7},{8,9},{9,10},{10,11},{12,13},{... | collective-permute-start | bytes 491528 | tf_op jit(solution)/shard_map/ppermute | solution.py:42
  104.2 5.3 %shard_map.81 = (f32[40,128,128]{2,1,0:T(8,128)}, f32[40,8,128]{2,1,0:T(8,128)}, f32[40,8,128]{2,1,0:T(8,128)}) custom-call(s32[2]{0:T(128)} %pad_add_fusion.2.place_ref, f32[16,16,64,128]{3,2,1,0:T(8,128)} %refs_0_.7, f32[16,2,64,128]{3,2,1,0:T(8,128)} %collective-permute-done.17.refs_1_, f32[16,8,4,128]{3,2,1,0:T(4,128)} %copy-done.1, ...), custom_call_target="tpu_custom_call" | custom-call | bytes 5242880 | tf_op jit(solution)/shard_map/pallas_call | solution.py:319
  109.4 8.3 %collective-permute-done.21.refs_1_ = f32[16,2,64,128]{3,2,1,0:T(8,128)} collective-permute-done((f32[16,2,64,128]{3,2,1,0:T(8,128)S(1)}, f32[16,2,64,128]{3,2,1,0:T(8,128)}, u32[]{:S(2)}, u32[]{:S(2)}) %collective-permute-start.21) | collective-permute-done | bytes 1048608 | tf_op jit(solution)/shard_map/ppermute | solution.py:47
  117.8 1.3 collective-permute-start.18
  119.1 5.2 %shard_map.83 = (f32[40,128,128]{2,1,0:T(8,128)}, f32[40,8,128]{2,1,0:T(8,128)}, f32[40,8,128]{2,1,0:T(8,128)}) custom-call(s32[2]{0:T(128)} %pad_add_fusion.3.place_ref, f32[16,16,64,128]{3,2,1,0:T(8,128)} %refs_0_.7, f32[16,2,64,128]{3,2,1,0:T(8,128)} %collective-permute-done.21.refs_1_, f32[16,8,4,128]{3,2,1,0:T(4,128)} %copy-done.1, ...), custom_call_target="tpu_custom_call" | custom-call | bytes 5242880 | tf_op jit(solution)/shard_map/pallas_call | solution.py:319
  124.3 6.5 %collective-permute-start.19 = (f32[40,8,128]{2,1,0:T(8,128)S(1)}, f32[40,8,128]{2,1,0:T(8,128)}, u32[]{:S(2)}, u32[]{:S(2)}) collective-permute-start(f32[40,8,128]{2,1,0:T(8,128)S(1)} %copy-done.21), channel_id=1, source_target_pairs={{0,1},{1,2},{2,3},{4,5},{5,6},{6,7},{8,9},{9,10},{10,11},{12,13},{... | collective-permute-start | bytes 491528 | tf_op jit(solution)/shard_map/ppermute | solution.py:42
  130.8 1.5 collective-permute-start.22
  132.9 42.7 %shard_map.78 = (f32[16,2,64,128]{3,2,1,0:T(8,128)}, f32[16,2,64,128]{3,2,1,0:T(8,128)}, f32[2,64,128]{2,1,0:T(8,128)}) custom-call(f32[40,128,128]{2,1,0:T(8,128)} %get-tuple-element.26.image_ref, f32[40,8,128]{2,1,0:T(8,128)} %copy-done.17, f32[40,8,128]{2,1,0:T(8,128)} %copy-done.18, f32[40,8,136]{2,1,0:T(8,128)} %get-tuple-element.65.code_ref, ...), custom_call_target="tpu_custom_call" | custom-call | flops 17112760320 | bytes 11141120 | tf_op jit(solution)/shard_map/pallas_call | solution.py:322
  175.7 4.5 %collective-permute-start.23 = (f32[40,8,128]{2,1,0:T(8,128)S(1)}, f32[40,8,128]{2,1,0:T(8,128)S(1)}, u32[]{:S(2)}, u32[]{:S(2)}) collective-permute-start(f32[40,8,128]{2,1,0:T(8,128)S(1)} %copy-done.16), channel_id=1, source_target_pairs={{0,1},{1,2},{2,3},{4,5},{5,6},{6,7},{8,9},{9,10},{10,11},{12,13},{... | collective-permute-start | bytes 491528 | tf_op jit(solution)/shard_map/ppermute | solution.py:42
  180.2 1.6 collective-permute-start.12
  181.8 42.6 %shard_map.80 = (f32[16,2,64,128]{3,2,1,0:T(8,128)}, f32[16,2,64,128]{3,2,1,0:T(8,128)}, f32[2,64,128]{2,1,0:T(8,128)}) custom-call(f32[40,128,128]{2,1,0:T(8,128)} %get-tuple-element.31.image_ref, f32[40,8,128]{2,1,0:T(8,128)} %copy-done.20, f32[40,8,128]{2,1,0:T(8,128)} %copy-done.23, f32[40,8,136]{2,1,0:T(8,128)} %get-tuple-element.63.code_ref, ...), custom_call_target="tpu_custom_call" | custom-call | flops 17112760320 | bytes 11141120 | tf_op jit(solution)/shard_map/pallas_call | solution.py:322
  225.1 42.7 %shard_map.82 = (f32[16,2,64,128]{3,2,1,0:T(8,128)}, f32[16,2,64,128]{3,2,1,0:T(8,128)}, f32[2,64,128]{2,1,0:T(8,128)}) custom-call(f32[40,128,128]{2,1,0:T(8,128)} %get-tuple-element.36.image_ref, f32[40,8,128]{2,1,0:T(8,128)} %copy-done.22, f32[40,8,128]{2,1,0:T(8,128)} %collective-permute-done.19.behind_ref, f32[40,8,136]{2,1,0:T(8,128)} %get-tuple-element.64.code_ref, ...), custom_call_target="tpu_custom_call" | custom-call | flops 17112760320 | bytes 11141120 | tf_op jit(solution)/shard_map/pallas_call | solution.py:322
  267.7 1.4 collective-permute-start.20
  269.9 42.8 %shard_map.84 = (f32[16,2,64,128]{3,2,1,0:T(8,128)}, f32[16,2,64,128]{3,2,1,0:T(8,128)}, f32[2,64,128]{2,1,0:T(8,128)}) custom-call(f32[40,128,128]{2,1,0:T(8,128)} %get-tuple-element.41.image_ref, f32[40,8,128]{2,1,0:T(8,128)} %copy-done.19, f32[40,8,128]{2,1,0:T(8,128)} %copy-done.24, f32[40,8,136]{2,1,0:T(8,128)} %get-tuple-element.62.code_ref, ...), custom_call_target="tpu_custom_call" | custom-call | flops 17112760320 | bytes 11141120 | tf_op jit(solution)/shard_map/pallas_call | solution.py:322
  313.3 1.6 pad_maximum_fusion.3
  314.9 1.1 broadcast_in_dim.94
  316.6 1.3 constant_dynamic-update-slice_fusion.2
  318.0 20.9 %collective-permute-done.24 = f32[16,2,64,128]{3,2,1,0:T(8,128)S(1)} collective-permute-done((f32[16,2,64,128]{3,2,1,0:T(8,128)}, f32[16,2,64,128]{3,2,1,0:T(8,128)S(1)}, u32[]{:S(2)}, u32[]{:S(2)}) %collective-permute-start.24) | collective-permute-done | bytes 1048608 | tf_op jit(solution)/shard_map/ppermute | solution.py:47
  339.0 3.4 copy-done
  (115 shorter events, 12.3 us)
Async XLA Ops:
  0.6 13.7 %copy-start.9 = (s32[16,64,128]{2,1,0:T(8,128)S(1)}, s32[16,64,128]{2,1,0:T(8,128)}, u32[]{:S(2)}) copy-start(s32[16,64,128]{2,1,0:T(8,128)} %param.7) | copy-start | bytes 1572868
  0.6 17.6 %copy-start.25 = (s32[16]{0:T(128)S(1)}, s32[16]{0:T(128)}, u32[]{:S(2)}) copy-start(s32[16]{0:T(128)} %param.8) | copy-start | bytes 196
  0.7 20.6 %copy-start.13 = (f32[3]{0:T(128)S(1)}, f32[3]{0:T(128)}, u32[]{:S(2)}) copy-start(f32[3]{0:T(128)} %param.11) | copy-start | bytes 40
  0.7 24.5 %copy-start.15 = (f32[3]{0:T(128)S(1)}, f32[3]{0:T(128)}, u32[]{:S(2)}) copy-start(f32[3]{0:T(128)} %param.9) | copy-start | bytes 40
  0.7 24.5 %copy-start.14 = (f32[3]{0:T(128)S(1)}, f32[3]{0:T(128)}, u32[]{:S(2)}) copy-start(f32[3]{0:T(128)} %param.10) | copy-start | bytes 40
  4.9 63.0 %collective-permute-start = (f32[16,2,64,128]{3,2,1,0:T(8,128)}, f32[16,2,64,128]{3,2,1,0:T(8,128)}, u32[]{:S(2)}, u32[]{:S(2)}) collective-permute-start(f32[16,2,64,128]{3,2,1,0:T(8,128)} %get-tuple-element.57), channel_id=1, source_target_pairs={{0,16},{16,0},{1,17},{17,1},{2,18},{18,2},{3,19},{19,3},{4,20},{20... | collective-permute-start | bytes 3145736 | tf_op jit(solution)/shard_map/ppermute | solution.py:47
  8.9 40.6 %collective-permute-start.1 = (f32[16,8,4,128]{3,2,1,0:T(4,128)}, f32[16,8,4,128]{3,2,1,0:T(4,128)S(1)}, u32[]{:S(2)}, u32[]{:S(2)}) collective-permute-start(f32[16,8,4,128]{3,2,1,0:T(4,128)} %get-tuple-element.60), channel_id=1, source_target_pairs={{0,4},{4,8},{8,12},{16,20},{20,24},{24,28},{1,5},{5,9},{9,13},{17,... | collective-permute-start | bytes 786440 | tf_op jit(solution)/shard_map/ppermute | solution.py:57
  12.4 37.9 %collective-permute-start.2 = (f32[16,8,4,128]{3,2,1,0:T(4,128)S(1)}, f32[16,8,4,128]{3,2,1,0:T(4,128)S(1)}, u32[]{:S(2)}, u32[]{:S(2)}) collective-permute-start(f32[16,8,4,128]{3,2,1,0:T(4,128)S(1)} %get-tuple-element.59), channel_id=1, source_target_pairs={{0,20},{4,24},{8,28},{16,4},{20,8},{24,12},{1,21},{5,25},{9,29},{1... | collective-permute-start | bytes 786440 | tf_op jit(solution)/shard_map/ppermute | solution.py:57
  14.4 26.4 %collective-permute-start.8 = (f32[8,4,128]{2,1,0:T(4,128)S(1)}, f32[8,4,128]{2,1,0:T(4,128)S(1)}, u32[]{:S(2)}, u32[]{:S(2)}) collective-permute-start(f32[8,4,128]{2,1,0:T(4,128)S(1)} %get-tuple-element.75), channel_id=1, source_target_pairs={{4,0},{8,4},{12,8},{5,1},{9,5},{13,9},{6,2},{10,6},{14,10},{7,3},{... | collective-permute-start | bytes 49160 | tf_op jit(solution)/shard_map/ppermute | solution.py:42
  18.3 17.4 %collective-permute-start.11 = (f32[16]{0:T(128)S(1)}, f32[16]{0:T(128)S(1)}, u32[]{:S(2)}, u32[]{:S(2)}) collective-permute-start(f32[16]{0:T(128)S(1)} %get-tuple-element.87), channel_id=1, source_target_pairs={{0,16},{16,0},{1,17},{17,1},{2,18},{18,2},{3,19},{19,3},{4,20},{20... | collective-permute-start | bytes 200 | tf_op jit(solution)/shard_map/ppermute | solution.py:47
  35.7 5.6 %collective-permute-start.7 = (f32[8,4,128]{2,1,0:T(4,128)S(1)}, f32[8,4,128]{2,1,0:T(4,128)S(1)}, u32[]{:S(2)}, u32[]{:S(2)}) collective-permute-start(f32[8,4,128]{2,1,0:T(4,128)S(1)} %get-tuple-element.74), channel_id=1, source_target_pairs={{0,4},{4,8},{8,12},{1,5},{5,9},{9,13},{2,6},{6,10},{10,14},{3,7},{... | collective-permute-start | bytes 49160 | tf_op jit(solution)/shard_map/ppermute | solution.py:42
  41.5 2.7 collective-permute-start.10
  42.8 5.2 %collective-permute-start.9 = (f32[8,72,4]{2,1,0:T(8,128)S(1)}, f32[8,72,4]{2,1,0:T(8,128)S(1)}, u32[]{:S(2)}, u32[]{:S(2)}) collective-permute-start(f32[8,72,4]{2,1,0:T(8,128)S(1)} %get-tuple-element.68), channel_id=1, source_target_pairs={{1,0},{2,1},{3,2},{5,4},{6,5},{7,6},{9,8},{10,9},{11,10},{13,12},{... | collective-permute-start | bytes 27656 | tf_op jit(solution)/shard_map/ppermute | solution.py:42
  44.2 37.8 %collective-permute-start.13 = (f32[16,2,64,128]{3,2,1,0:T(8,128)}, f32[16,2,64,128]{3,2,1,0:T(8,128)}, u32[]{:S(2)}, u32[]{:S(2)}) collective-permute-start(f32[16,2,64,128]{3,2,1,0:T(8,128)} %get-tuple-element.56), channel_id=1, source_target_pairs={{0,16},{16,0},{1,17},{17,1},{2,18},{18,2},{3,19},{19,3},{4,20},{20... | collective-permute-start | bytes 3145736 | tf_op jit(solution)/shard_map/ppermute | solution.py:47
  48.0 47.3 %collective-permute-start.17 = (f32[16,2,64,128]{3,2,1,0:T(8,128)}, f32[16,2,64,128]{3,2,1,0:T(8,128)}, u32[]{:S(2)}, u32[]{:S(2)}) collective-permute-start(f32[16,2,64,128]{3,2,1,0:T(8,128)} %get-tuple-element.55), channel_id=1, source_target_pairs={{0,16},{16,0},{1,17},{17,1},{2,18},{18,2},{3,19},{19,3},{4,20},{20... | collective-permute-start | bytes 3145736 | tf_op jit(solution)/shard_map/ppermute | solution.py:47
  49.5 18.3 %copy-start.1 = (f32[16,8,4,128]{3,2,1,0:T(4,128)}, f32[16,8,4,128]{3,2,1,0:T(4,128)S(1)}, u32[]{:S(2)}) copy-start(f32[16,8,4,128]{3,2,1,0:T(4,128)S(1)} %collective-permute-done.1.refs_2_) | copy-start | bytes 786436
  49.5 68.2 %collective-permute-start.21 = (f32[16,2,64,128]{3,2,1,0:T(8,128)S(1)}, f32[16,2,64,128]{3,2,1,0:T(8,128)}, u32[]{:S(2)}, u32[]{:S(2)}) collective-permute-start(f32[16,2,64,128]{3,2,1,0:T(8,128)S(1)} %get-tuple-element.54), channel_id=1, source_target_pairs={{0,16},{16,0},{1,17},{17,1},{2,18},{18,2},{3,19},{19,3},{4,20},{20... | collective-permute-start | bytes 3145736 | tf_op jit(solution)/shard_map/ppermute | solution.py:47
  50.3 17.5 %copy-start.2 = (f32[16,8,4,128]{3,2,1,0:T(4,128)}, f32[16,8,4,128]{3,2,1,0:T(4,128)S(1)}, u32[]{:S(2)}) copy-start(f32[16,8,4,128]{3,2,1,0:T(4,128)S(1)} %collective-permute-done.2.refs_3_) | copy-start | bytes 786436
  50.3 8.3 %collective-permute-start.3 = (f32[16,8,4,128]{3,2,1,0:T(4,128)S(1)}, f32[16,8,4,128]{3,2,1,0:T(4,128)S(1)}, u32[]{:S(2)}, u32[]{:S(2)}) collective-permute-start(f32[16,8,4,128]{3,2,1,0:T(4,128)S(1)} %get-tuple-element.61), channel_id=1, source_target_pairs={{4,0},{8,4},{12,8},{20,16},{24,20},{28,24},{5,1},{9,5},{13,9},{21,... | collective-permute-start | bytes 786440 | tf_op jit(solution)/shard_map/ppermute | solution.py:57
  58.6 9.3 %copy-start.3 = (f32[16,8,4,128]{3,2,1,0:T(4,128)}, f32[16,8,4,128]{3,2,1,0:T(4,128)S(1)}, u32[]{:S(2)}) copy-start(f32[16,8,4,128]{3,2,1,0:T(4,128)S(1)} %collective-permute-done.3.refs_4_) | copy-start | bytes 786436
  58.6 9.3 %collective-permute-start.4 = (f32[16,8,4,128]{3,2,1,0:T(4,128)S(1)}, f32[16,8,4,128]{3,2,1,0:T(4,128)S(1)}, u32[]{:S(2)}, u32[]{:S(2)}) collective-permute-start(f32[16,8,4,128]{3,2,1,0:T(4,128)S(1)} %get-tuple-element.58), channel_id=1, source_target_pairs={{4,16},{8,20},{12,24},{20,0},{24,4},{28,8},{5,17},{9,21},{13,25},{... | collective-permute-start | bytes 786440 | tf_op jit(solution)/shard_map/ppermute | solution.py:57
  67.8 0.7 copy-start.4
  73.7 50.6 %collective-permute-start.5 = (f32[40,8,128]{2,1,0:T(8,128)}, f32[40,8,128]{2,1,0:T(8,128)S(1)}, u32[]{:S(2)}, u32[]{:S(2)}) collective-permute-start(f32[40,8,128]{2,1,0:T(8,128)} %get-tuple-element.27), channel_id=1, source_target_pairs={{1,0},{2,1},{3,2},{5,4},{6,5},{7,6},{9,8},{10,9},{11,10},{13,12},{... | collective-permute-start | bytes 491528 | tf_op jit(solution)/shard_map/ppermute | solution.py:42
  75.0 55.7 %collective-permute-start.6 = (f32[40,8,128]{2,1,0:T(8,128)}, f32[40,8,128]{2,1,0:T(8,128)S(1)}, u32[]{:S(2)}, u32[]{:S(2)}) collective-permute-start(f32[40,8,128]{2,1,0:T(8,128)} %get-tuple-element.28), channel_id=1, source_target_pairs={{0,1},{1,2},{2,3},{4,5},{5,6},{6,7},{8,9},{9,10},{10,11},{12,13},{... | collective-permute-start | bytes 491528 | tf_op jit(solution)/shard_map/ppermute | solution.py:42
  87.3 88.3 %collective-permute-start.14 = (f32[40,8,128]{2,1,0:T(8,128)}, f32[40,8,128]{2,1,0:T(8,128)S(1)}, u32[]{:S(2)}, u32[]{:S(2)}) collective-permute-start(f32[40,8,128]{2,1,0:T(8,128)} %get-tuple-element.32), channel_id=1, source_target_pairs={{1,0},{2,1},{3,2},{5,4},{6,5},{7,6},{9,8},{10,9},{11,10},{13,12},{... | collective-permute-start | bytes 491528 | tf_op jit(solution)/shard_map/ppermute | solution.py:42
  95.3 84.9 %collective-permute-start.15 = (f32[40,8,128]{2,1,0:T(8,128)}, f32[40,8,128]{2,1,0:T(8,128)S(1)}, u32[]{:S(2)}, u32[]{:S(2)}) collective-permute-start(f32[40,8,128]{2,1,0:T(8,128)} %get-tuple-element.33), channel_id=1, source_target_pairs={{0,1},{1,2},{2,3},{4,5},{5,6},{6,7},{8,9},{9,10},{10,11},{12,13},{... | collective-permute-start | bytes 491528 | tf_op jit(solution)/shard_map/ppermute | solution.py:42
  109.4 14.9 %copy-start.21 = (f32[40,8,128]{2,1,0:T(8,128)S(1)}, f32[40,8,128]{2,1,0:T(8,128)}, u32[]{:S(2)}) copy-start(f32[40,8,128]{2,1,0:T(8,128)} %get-tuple-element.38) | copy-start | bytes 491524
  117.8 106.6 %collective-permute-start.18 = (f32[40,8,128]{2,1,0:T(8,128)}, f32[40,8,128]{2,1,0:T(8,128)S(1)}, u32[]{:S(2)}, u32[]{:S(2)}) collective-permute-start(f32[40,8,128]{2,1,0:T(8,128)} %get-tuple-element.37), channel_id=1, source_target_pairs={{1,0},{2,1},{3,2},{5,4},{6,5},{7,6},{9,8},{10,9},{11,10},{13,12},{... | collective-permute-start | bytes 491528 | tf_op jit(solution)/shard_map/ppermute | solution.py:42
  124.3 8.6 %copy-start.17 = (f32[40,8,128]{2,1,0:T(8,128)}, f32[40,8,128]{2,1,0:T(8,128)S(1)}, u32[]{:S(2)}) copy-start(f32[40,8,128]{2,1,0:T(8,128)S(1)} %collective-permute-done.5.ahead_ref) | copy-start | bytes 491524
  124.3 100.7 %collective-permute-start.19 = (f32[40,8,128]{2,1,0:T(8,128)S(1)}, f32[40,8,128]{2,1,0:T(8,128)}, u32[]{:S(2)}, u32[]{:S(2)}) collective-permute-start(f32[40,8,128]{2,1,0:T(8,128)S(1)} %copy-done.21), channel_id=1, source_target_pairs={{0,1},{1,2},{2,3},{4,5},{5,6},{6,7},{8,9},{9,10},{10,11},{12,13},{... | collective-permute-start | bytes 491528 | tf_op jit(solution)/shard_map/ppermute | solution.py:42
  130.8 2.2 copy-start.18
  130.8 138.4 %collective-permute-start.22 = (f32[40,8,128]{2,1,0:T(8,128)}, f32[40,8,128]{2,1,0:T(8,128)S(1)}, u32[]{:S(2)}, u32[]{:S(2)}) collective-permute-start(f32[40,8,128]{2,1,0:T(8,128)} %get-tuple-element.42), channel_id=1, source_target_pairs={{1,0},{2,1},{3,2},{5,4},{6,5},{7,6},{9,8},{10,9},{11,10},{13,12},{... | collective-permute-start | bytes 491528 | tf_op jit(solution)/shard_map/ppermute | solution.py:42
  132.9 42.7 %copy-start.16 = (f32[40,8,128]{2,1,0:T(8,128)S(1)}, f32[40,8,128]{2,1,0:T(8,128)}, u32[]{:S(2)}) copy-start(f32[40,8,128]{2,1,0:T(8,128)} %get-tuple-element.43) | copy-start | bytes 491524
  175.6 6.1 %copy-start.20 = (f32[40,8,128]{2,1,0:T(8,128)}, f32[40,8,128]{2,1,0:T(8,128)S(1)}, u32[]{:S(2)}) copy-start(f32[40,8,128]{2,1,0:T(8,128)S(1)} %collective-permute-done.14.ahead_ref) | copy-start | bytes 491524
  175.7 93.5 %collective-permute-start.23 = (f32[40,8,128]{2,1,0:T(8,128)S(1)}, f32[40,8,128]{2,1,0:T(8,128)S(1)}, u32[]{:S(2)}, u32[]{:S(2)}) collective-permute-start(f32[40,8,128]{2,1,0:T(8,128)S(1)} %copy-done.16), channel_id=1, source_target_pairs={{0,1},{1,2},{2,3},{4,5},{5,6},{6,7},{8,9},{9,10},{10,11},{12,13},{... | collective-permute-start | bytes 491528 | tf_op jit(solution)/shard_map/ppermute | solution.py:42
  180.2 1.6 copy-start.23
  180.2 135.9 %collective-permute-start.12 = (f32[16,2,64,128]{3,2,1,0:T(8,128)}, f32[16,2,64,128]{3,2,1,0:T(8,128)S(1)}, u32[]{:S(2)}, u32[]{:S(2)}) collective-permute-start(f32[16,2,64,128]{3,2,1,0:T(8,128)} %get-tuple-element.30), channel_id=1, source_target_pairs={{0,16},{16,0},{1,17},{17,1},{2,18},{18,2},{3,19},{19,3},{4,20},{20... | collective-permute-start | bytes 3145736 | tf_op jit(solution)/shard_map/ppermute | solution.py:47
  224.4 91.9 %collective-permute-start.16 = (f32[16,2,64,128]{3,2,1,0:T(8,128)}, f32[16,2,64,128]{3,2,1,0:T(8,128)S(1)}, u32[]{:S(2)}, u32[]{:S(2)}) collective-permute-start(f32[16,2,64,128]{3,2,1,0:T(8,128)} %get-tuple-element.35), channel_id=1, source_target_pairs={{0,16},{16,0},{1,17},{17,1},{2,18},{18,2},{3,19},{19,3},{4,20},{20... | collective-permute-start | bytes 3145736 | tf_op jit(solution)/shard_map/ppermute | solution.py:47
  267.7 48.8 %collective-permute-start.20 = (f32[16,2,64,128]{3,2,1,0:T(8,128)}, f32[16,2,64,128]{3,2,1,0:T(8,128)}, u32[]{:S(2)}, u32[]{:S(2)}) collective-permute-start(f32[16,2,64,128]{3,2,1,0:T(8,128)} %get-tuple-element.40), channel_id=1, source_target_pairs={{0,16},{16,0},{1,17},{17,1},{2,18},{18,2},{3,19},{19,3},{4,20},{20... | collective-permute-start | bytes 3145736 | tf_op jit(solution)/shard_map/ppermute | solution.py:47
  269.9 43.4 %copy-start.10 = (f32[2,64,128]{2,1,0:T(8,128)S(1)}, f32[2,64,128]{2,1,0:T(8,128)}, u32[]{:S(2)}) copy-start(f32[2,64,128]{2,1,0:T(8,128)} %get-tuple-element.46) | copy-start | bytes 196612
  269.9 43.4 %copy-start.11 = (f32[2,64,128]{2,1,0:T(8,128)S(1)}, f32[2,64,128]{2,1,0:T(8,128)}, u32[]{:S(2)}) copy-start(f32[2,64,128]{2,1,0:T(8,128)} %get-tuple-element.47) | copy-start | bytes 196612
  269.9 43.4 %copy-start.12 = (f32[2,64,128]{2,1,0:T(8,128)S(1)}, f32[2,64,128]{2,1,0:T(8,128)}, u32[]{:S(2)}) copy-start(f32[2,64,128]{2,1,0:T(8,128)} %get-tuple-element.48) | copy-start | bytes 196612
  312.6 3.3 copy-start.5
  312.6 3.5 %copy-start.6 = (f32[16,2,64,128]{3,2,1,0:T(8,128)S(1)}, f32[16,2,64,128]{3,2,1,0:T(8,128)}, u32[]{:S(2)}) copy-start(f32[16,2,64,128]{3,2,1,0:T(8,128)} %get-tuple-element.34) | copy-start | bytes 3145732
  312.6 26.2 %collective-permute-start.24 = (f32[16,2,64,128]{3,2,1,0:T(8,128)}, f32[16,2,64,128]{3,2,1,0:T(8,128)S(1)}, u32[]{:S(2)}, u32[]{:S(2)}) collective-permute-start(f32[16,2,64,128]{3,2,1,0:T(8,128)} %get-tuple-element.45), channel_id=1, source_target_pairs={{0,16},{16,0},{1,17},{17,1},{2,18},{18,2},{3,19},{19,3},{4,20},{20... | collective-permute-start | bytes 3145736 | tf_op jit(solution)/shard_map/ppermute | solution.py:47
  314.9 1.6 copy-start.7
  315.9 2.0 copy-start.8
  339.0 3.4 copy-start
  (3 other events, 2.0 us)

commit v2 on v1

v2 whole, which is shorter than its diff:
```python
import functools
import math

import jax
import jax.numpy as jnp
import numpy as np
from jax import lax
from jax.experimental import pallas as pl
from jax.experimental.pallas import tpu as pltpu
from jax.sharding import PartitionSpec as P


NT = 128
ITERS = 3
HALF = NT // 2
LANES = 128
RIM = 4
STEP = 1
UNROLL = 12
SPARE = UNROLL + 4

relax_factor = 0.5
omega_base = 0.25
saturation = 3.0
coil_scale = 0.5


def lookup(values, material):
    return jnp.where(material == 0, values[0], jnp.where(material == 1, values[1], values[2]))


def split(value):
    high = value.astype(jnp.bfloat16)
    low = (value - high.astype(jnp.float32)).astype(jnp.bfloat16)
    return high, low


def shifted(value, axis, by):
    length = lax.axis_size(axis)
    return lax.ppermute(value, axis, [(i, i + by) for i in range(length) if 0 <= i + by < length])


def turned(value, by):
    length = lax.axis_size("harm")
    return lax.ppermute(value, "harm", [(i, (i + by) % length) for i in range(length)])


def turned_and_shifted(value, turn, by):
    groups, length = lax.axis_size("harm"), lax.axis_size("sx")
    pairs = []
    for g in range(groups):
        for i in range(length):
            if 0 <= i + by < length:
                pairs.append((g * length + i, (g + turn) % groups * length + i + by))
    return lax.ppermute(value, ("harm", "sx"), pairs)


def gather_kernel(groups, own, layers, parts, rows, columns, place_ref, *refs):
    mains, tops, bottoms = refs[:groups], refs[groups : 2 * groups], refs[2 * groups : 3 * groups]
    image_ref, left_ref, right_ref, stage_ref = refs[3 * groups :]
    span = rows // parts
    for at in range(-RIM, span + RIM):
        pieces = []
        for g in range(groups):
            for layer in range(layers):
                for part in range(parts):
                    x = span * part + at
                    if x < 0:
                        pieces.append(tops[g][0:own, layer, RIM + x, :])
                    elif x >= rows:
                        pieces.append(bottoms[g][0:own, layer, x - rows, :])
                    else:
                        pieces.append(mains[g][:, layer, x, :])
        if own % 8 == 0:
            stacked = jnp.concatenate(pieces, axis=0)
        else:
            for k, piece in enumerate(pieces):
                stage_ref[k * own : (k + 1) * own, :] = piece
            stacked = stage_ref[...]
        flipped = jnp.transpose(stacked)
        image_ref[0, at + RIM] = flipped
        left_ref[0, at + RIM] = flipped[:8]
        right_ref[0, at + RIM] = flipped[columns - 8 :]


def solve_kernel(
    groups, own, layers, parts, rows, columns,
    chained, place_ref, image_ref, ahead_ref, behind_ref, code_ref, table_ref, fwd_ref, inv_ref, weight_ref, heat_scale_ref,
    *refs,
):
    refs = refs[chained:]
    outs, heat_ref = refs[:groups], refs[groups]
    pot, nu_all, nu_sat, gain, turn_gain, feed, samples_0, samples_1, products_0, products_1, last_row, back_x = refs[groups + 1 :]
    samples, products = (samples_0, samples_1), (products_0, products_1)
    span = rows // parts
    total = span + 2 * RIM
    wide = columns + 8

    def load(x, carry):
        code = code_ref[0, x]
        chosen = jnp.concatenate([jnp.where(code == m, 1.0, 0.0) for m in (1.0, 2.0, 3.0)] * 3, axis=0)
        picked = lax.dot_general(
            chosen.astype(jnp.bfloat16), table_ref[...], (((0,), (0,)), ((), ())), preferred_element_type=jnp.float32)
        for k, ref in enumerate((nu_all, nu_sat, gain, turn_gain, feed)):
            ref[x] = picked[:wide, k * LANES : (k + 1) * LANES]
        pot[x, 0:columns, :] = image_ref[0, x]
        edge = lax.broadcasted_iota(jnp.int32, (8, LANES), 0) < RIM
        pot[x, columns:wide, :] = jnp.where(edge, ahead_ref[0, x], behind_ref[0, x])
        pot[x, wide : wide + 8, :] = image_ref[0, x, 0:8, :]
        return carry

    lax.fori_loop(0, total, load, 0, unroll=4)
    for k in range(SPARE):
        pot[total + k] = jnp.zeros((wide + 8, LANES), jnp.float32)
    even = lax.broadcasted_iota(jnp.int32, (wide, LANES), 1) % 2 == 0

    def fields_at(base):
        here = [pot[base + k, 0:wide, :] for k in range(STEP + 1)]
        field_x = [pot[base + k, 1 : wide + 1, :] - here[k] for k in range(STEP)]
        field_y = [here[k] - here[k + 1] for k in range(STEP)]
        return here, field_x, field_y

    def to_samples(base, slot):
        _, field_x, field_y = fields_at(base)
        fields = jnp.concatenate([f for pair in zip(field_x, field_y) for f in pair], axis=0)
        high, low = split(fields)
        samples[slot][...] = jnp.dot(
            jnp.concatenate([high, low, high], axis=1), fwd_ref[0], preferred_element_type=jnp.float32)

    def saturate(slot):
        for k in range(STEP):
            sample_x = samples[slot][2 * k * wide : (2 * k + 1) * wide, :]
            sample_y = samples[slot][(2 * k + 1) * wide : (2 * k + 2) * wide, :]
            square = 1.0 + (sample_x * sample_x + sample_y * sample_y)
            inverse = lax.rsqrt(square)
            scaled = square * inverse
            factor = inverse * (1.0 / jnp.tanh(scaled) - inverse)
            high, low = split(jnp.concatenate([factor * sample_x, factor * sample_y], axis=0))
            products[slot][2 * k * wide : (2 * k + 2) * wide, 0 : 2 * LANES] = high
            products[slot][2 * k * wide : (2 * k + 2) * wide, 2 * LANES :] = low

    def update(base, slot):
        here, field_x, field_y = fields_at(base)
        pair = jnp.dot(products[slot][...], inv_ref[0], preferred_element_type=jnp.float32)
        back = pair[:, :LANES] + pair[:, LANES:]
        above = last_row[...]
        for k in range(STEP):
            at = base + k
            linear, bent = nu_all[at], nu_sat[at]
            inten_x = linear * field_x[k] - bent * back[2 * k * wide : (2 * k + 1) * wide]
            inten_y = linear * field_y[k] - bent * back[(2 * k + 1) * wide : (2 * k + 2) * wide]
            back_x[k, 8 : wide + 8, :] = inten_x
            back_x[k, 0:8, :] = inten_x[columns:]
            curl = (inten_y - above) - (inten_x - back_x[k, 7 : wide + 7, :])
            above = inten_y
            rotated = jnp.where(even, pltpu.roll(here[k], LANES - 1, 1), pltpu.roll(here[k], 1, 1))
            fresh = here[k] + feed[at] - gain[at] * curl - turn_gain[at] * rotated
            pot[at, 0:wide, :] = fresh
            pot[at, wide : wide + 8, :] = fresh[0:8]
        last_row[...] = above

    def sweep(index, carry):
        first = index + 2
        last = total - 2 - index
        to_samples(first - 1, 1)
        saturate(1)
        to_samples(first, 0)
        pair = jnp.dot(products[1][wide:], inv_ref[0], preferred_element_type=jnp.float32)
        fall = pot[first - 1, 0:wide, :] - pot[first, 0:wide, :]
        last_row[...] = nu_all[first - 1] * fall - nu_sat[first - 1] * (pair[:, :LANES] + pair[:, LANES:])
        saturate(0)
        to_samples(first + STEP, 1)

        def advance(step, carry):
            base = first + step * UNROLL * STEP
            for part in range(UNROLL):
                slot = part % 2
                saturate(1 - slot)
                update(base + part * STEP, slot)
                to_samples(base + (part + 2) * STEP, slot)
            return carry

        return lax.fori_loop(0, pl.cdiv(last - first, UNROLL * STEP), advance, carry)

    lax.fori_loop(0, ITERS, sweep, 0)

    lanes_each = layers * parts * own
    weight = weight_ref[0]

    def finish(block, carry):
        for k in range(8):
            at = pl.multiple_of(block * 8, 8) + k
            flipped = jnp.transpose(pot[block * 8 + k + RIM, 0:columns, :])
            powers = flipped * flipped * weight
            for layer in range(layers):
                for part in range(parts):
                    where = part * span + at
                    power = jnp.zeros((1, columns), jnp.float32)
                    for g in range(groups):
                        begin = g * lanes_each + (layer * parts + part) * own
                        outs[g][:, layer, pl.ds(where, 1), :] = flipped[begin : begin + own].reshape(own, 1, columns)
                        power = power + jnp.sum(powers[begin : begin + own], axis=0, keepdims=True)
                    heat_ref[layer, pl.ds(where, 1), :] = power * heat_scale_ref[layer, pl.ds(where, 1), :]
        return carry

    lax.fori_loop(0, span // 8, finish, 0)


def place_kernel(where_ref, value_ref, whole_ref, out_ref):
    out_ref[...] = value_ref[...]


def lane_tables(groups, own, cells):
    lane = np.arange(LANES)
    cell = lane // own % cells
    slot = np.arange(cells * HALF)
    tables = []
    for place in range(groups):
        coef = (place + lane // (cells * own)) % groups * own + lane % own
        harmonic = 2 * (coef // 2) + 1
        angle = harmonic[:, None] * (slot % HALF)[None, :] % NT * (2.0 * math.pi / NT)
        wave = np.where((coef % 2 == 0)[:, None], np.cos(angle), np.sin(angle))
        basis = np.where(cell[:, None] == (slot // HALF)[None, :], wave, 0.0)

        def halves(value):
            high = value.astype(jnp.bfloat16)
            return high, (value - high.astype(np.float64)).astype(jnp.bfloat16)

        fwd_high, fwd_low = halves(basis / saturation)
        inv_high, inv_low = halves((3.0 * saturation * 2.0 / HALF) * basis.T)
        omega = omega_base * harmonic
        tables.append((
            np.concatenate([fwd_high, fwd_high, fwd_low], axis=0),
            np.block([[inv_high, inv_low], [inv_high, np.zeros_like(inv_low)]]),
            np.repeat((omega * omega).astype(np.float32)[:, None], LANES, axis=1),
            np.stack([omega, omega * np.where(coef % 2 == 0, 1.0, -1.0)]).astype(np.float32),
        ))
    return [np.stack(each) for each in zip(*tables)]


def local(potential_start, material, coil_amps, nu_low, nu_rise, conductivity):
    groups = lax.axis_size("harm")
    place = lax.axis_index("harm")
    own, depth, rows, columns = potential_start.shape
    coefs = own * groups
    slab = depth // groups
    layers = max(d for d in (1, 2) if slab % d == 0)
    parts = LANES // (coefs * layers)
    chunks = slab // layers
    span = rows // parts
    total = span + 2 * RIM
    wide = columns + 8
    cells = layers * parts

    fwd, inv, weight, omegas = lane_tables(groups, own, cells)
    omegas = lax.dynamic_index_in_dim(jnp.asarray(omegas), place, 0, keepdims=False)
    amps = coil_amps.astype(jnp.float32)
    amps = jnp.stack([amps] + [turned(amps, -g) for g in range(1, groups)])
    amps = jnp.broadcast_to(amps[:, None, :], (groups, cells, own)).reshape(1, LANES)
    precond = 4.0 * (nu_low + nu_rise)[:, None] + conductivity[:, None] * omegas[:1]
    gain = relax_factor / precond
    turn_gain = gain * (conductivity[:, None] * omegas[1:])
    feed = gain * jnp.where(jnp.arange(3) == 1, coil_scale, 0.0)[:, None] * amps
    constants = jnp.stack(
        [jnp.broadcast_to((nu_low + nu_rise)[:, None], (3, LANES)), jnp.broadcast_to(nu_rise[:, None], (3, LANES)),
         gain, turn_gain, feed], axis=1)
    mine_only = jnp.arange(8)[:, None] == (jnp.arange(LANES) // own % cells)[None, :]
    constants = jnp.where(mine_only[None, :, None, :], constants[:, None], 0.0).reshape(24, 5 * LANES)
    top = lax.reduce_precision(constants, 8, 7)
    middle = lax.reduce_precision(constants - top, 8, 7)
    table = jnp.concatenate([top, middle, constants - top - middle], axis=0).astype(jnp.bfloat16)

    def part_of(value, group, start, count):
        return lax.dynamic_slice_in_dim(value, group * slab + start, count, 1)

    slab_material = lax.dynamic_slice_in_dim(material, place * slab, slab, 0)
    heat_scale = lookup(conductivity, slab_material) * (0.5 / coefs)
    code = (slab_material + 1).astype(jnp.float32)
    batches = [b for b in ((0, 1), (1, 1), (2, chunks - 2)) if b[0] < chunks]
    tops, bottoms, arrivals = [], [], []
    for start, count in batches:
        arrivals.append([
            turned(part_of(potential_start, (place - g) % groups, start * layers, count * layers), -g)
            for g in range(1, groups)])
    sides = jnp.concatenate(
        [shifted(code[:, :, :RIM], "sy", -1), shifted(code[:, :, columns - RIM :], "sy", 1)], axis=2)
    riders = jnp.stack([code, jnp.pad(sides, ((0, 0), (0, 0), (0, columns - 2 * RIM)))])
    for g in range(groups):
        mine = part_of(potential_start, (place - g) % groups, 0, slab)
        high, low = mine[:, :, rows - RIM :, :], mine[:, :, :RIM, :]
        if g == 0:
            high = jnp.concatenate([high, riders[:, :, rows - RIM :, :]], axis=0)
            low = jnp.concatenate([low, riders[:, :, :RIM, :]], axis=0)
        tops.append(turned_and_shifted(high, -g, 1))
        bottoms.append(turned_and_shifted(low, -g, -1))

    code = jnp.concatenate([tops[0][own:], riders, bottoms[0][own:]], axis=2)
    code = jnp.concatenate([code[0], code[1, :, :, : 2 * RIM]], axis=2)
    code = jnp.stack([code[:, part * span : part * span + total] for part in range(parts)], axis=1)
    code = code.reshape(chunks, cells, total, wide).transpose(0, 2, 1, 3)
    code = jnp.pad(code, ((0, 0), (0, 0), (0, 8 - cells), (0, 0)))

    index = jnp.stack([place, place * chunks]).astype(jnp.int32)

    def gather(start, count, arrived):
        at = (lambda i, s: (0, i, 0, 0))
        return pl.pallas_call(
            functools.partial(gather_kernel, groups, own, layers, parts, rows, columns),
            grid_spec=pltpu.PrefetchScalarGridSpec(
                num_scalar_prefetch=1,
                grid=(count,),
                in_specs=[pl.BlockSpec((own, layers, rows, columns), lambda i, s: (0, s[1] + start + i, 0, 0))]
                + [pl.BlockSpec((own, layers, rows, columns), at)] * (groups - 1)
                + ([pl.BlockSpec((own + 2, layers, RIM, columns), lambda i, s: (0, start + i, 0, 0))]
                   + [pl.BlockSpec((own, layers, RIM, columns), lambda i, s: (0, start + i, 0, 0))] * (groups - 1)) * 2,
                out_specs=[
                    pl.BlockSpec((1, total, columns, LANES), lambda i, s: (i, 0, 0, 0)),
                    pl.BlockSpec((1, total, 8, LANES), lambda i, s: (i, 0, 0, 0)),
                    pl.BlockSpec((1, total, 8, LANES), lambda i, s: (i, 0, 0, 0)),
                ],
                scratch_shapes=[pltpu.VMEM((LANES, columns), jnp.float32)],
            ),
            out_shape=[
                jax.ShapeDtypeStruct((count, total, columns, LANES), jnp.float32),
                jax.ShapeDtypeStruct((count, total, 8, LANES), jnp.float32),
                jax.ShapeDtypeStruct((count, total, 8, LANES), jnp.float32),
            ],
            cost_estimate=pl.CostEstimate(
                flops=0, bytes_accessed=count * 4 * total * columns * LANES * 2, transcendentals=0),
        )(index, potential_start, *arrived, *tops, *bottoms)

    def solve(k, at, image, ahead, behind, potential):
        chained = potential is not None
        fixed = lambda i, s: (0, 0)
        chosen = lambda i, s: (s[0], 0, 0)
        part = lambda i, s: (at, 0, 0, 0)
        whole = jax.ShapeDtypeStruct(potential_start.shape, jnp.float32)
        return pl.pallas_call(
            functools.partial(solve_kernel, groups, own, layers, parts, rows, columns, int(chained)),
            grid_spec=pltpu.PrefetchScalarGridSpec(
                num_scalar_prefetch=1,
                grid=(1,),
                in_specs=[
                    pl.BlockSpec((1, total, columns, LANES), part),
                    pl.BlockSpec((1, total, 8, LANES), part),
                    pl.BlockSpec((1, total, 8, LANES), part),
                    pl.BlockSpec((1, total, 8, wide), lambda i, s: (k, 0, 0, 0)),
                    pl.BlockSpec((72, 5 * LANES), fixed),
                    pl.BlockSpec((1, 3 * LANES, 2 * LANES), chosen),
                    pl.BlockSpec((1, 4 * LANES, 2 * LANES), chosen),
                    pl.BlockSpec((1, LANES, LANES), chosen),
                    pl.BlockSpec((layers, rows, columns), lambda i, s: (k, 0, 0)),
                ] + [pl.BlockSpec(memory_space=pl.ANY)] * chained,
                out_specs=[pl.BlockSpec((own, layers, rows, columns), lambda i, s: (0, s[1] + k, 0, 0))]
                + [pl.BlockSpec((own, layers, rows, columns), lambda i, s: (0, 0, 0, 0))] * (groups - 1)
                + [pl.BlockSpec((layers, rows, columns), lambda i, s: (0, 0, 0))],
                scratch_shapes=[pltpu.VMEM((total + SPARE, wide + 8, LANES), jnp.float32)]
                + [pltpu.VMEM((total + SPARE, wide, LANES), jnp.float32)] * 5
                + [pltpu.VMEM((2 * STEP * wide, 2 * LANES), jnp.float32)] * 2
                + [pltpu.VMEM((2 * STEP * wide, 4 * LANES), jnp.bfloat16)] * 2
                + [pltpu.VMEM((wide, LANES), jnp.float32), pltpu.VMEM((STEP, wide + 8, LANES), jnp.float32)],
            ),
            out_shape=[whole]
            + [jax.ShapeDtypeStruct((own, layers, rows, columns), jnp.float32)] * (groups - 1)
            + [jax.ShapeDtypeStruct((layers, rows, columns), jnp.float32)],
            input_output_aliases={10: 0} if chained else {},
            cost_estimate=pl.CostEstimate(
                flops=6 * total * wide * 256 * 256 * 8, bytes_accessed=4 * total * wide * LANES * 4, transcendentals=0),
        )(index, image, ahead, behind, code, table, fwd, inv, weight, heat_scale, *([potential] if chained else []))

    def place_into(potential, value, block):
        return pl.pallas_call(
            place_kernel,
            grid_spec=pltpu.PrefetchScalarGridSpec(
                num_scalar_prefetch=1,
                grid=(1,),
                in_specs=[pl.BlockSpec((own, layers, rows, columns), lambda i, s: (0, 0, 0, 0)),
                          pl.BlockSpec(memory_space=pl.ANY)],
                out_specs=pl.BlockSpec((own, layers, rows, columns), lambda i, s: (0, s[0], 0, 0)),
            ),
            out_shape=jax.ShapeDtypeStruct(potential.shape, jnp.float32),
            input_output_aliases={2: 0},
            cost_estimate=pl.CostEstimate(
                flops=0, bytes_accessed=8 * own * layers * rows * columns, transcendentals=0),
        )(block, value, potential)

    ready = []
    for k, (start, count) in enumerate(batches):
        image, left, right = gather(start, count, arrivals[k])
        ahead = shifted(left, "sy", -1)
        behind = shifted(right, "sy", 1)
        ready += [(at, image, ahead, behind) for at in range(count)]
    blocks = [(((place - g) % groups) * chunks).astype(jnp.int32) for g in range(groups)]
    potential, heats, coming = None, [], []
    for k in range(chunks):
        potential, *others, heat = solve(k, *ready[k], potential)
        heats.append(heat)
        for value, block in coming:
            potential = place_into(potential, value, block)
        coming = []
        for g in range(1, groups):
            coming.append((turned(others[g - 1], g), blocks[g].reshape(1) + k))
    for value, block in coming:
        potential = place_into(potential, value, block)
    return potential, jnp.concatenate(heats, axis=0)


def solution(mesh):
    in_specs = (P("harm", None, "sx", "sy"), P(None, "sx", "sy"), P("harm"), P(), P(), P())
    out_specs = (P("harm", None, "sx", "sy"), P("harm", "sx", "sy"))

    return jax.shard_map(local, mesh=mesh, in_specs=in_specs, out_specs=out_specs, check_vma=False)
```

time: 344 us -> 295 us (0.86)
  starting transfers between devices: 62.5 us -> 39.5 us
  Pallas kernels: 192 us -> 177 us
  waiting for transfers between devices: 56.8 us -> 43.6 us
    ppermute x12 -> x8, starting transfers between devices: 40.5 us -> 18.6 us  [shifted(): lax.ppermute(value, axis, [(i, i + by) for i in range(length) if 0 <= i +...]
    pallas_call x8 -> x11, Pallas kernels: 192 us -> 177 us  [the longest x4 151 us: solve(): pl.pallas_call(functools.partial(solve_kernel, groups, own, layers, parts...]
    ppermute x9 -> x8, waiting for transfers between devices: 43.1 us -> 34.7 us  [turned(): lax.ppermute(value, 'harm', [(i, (i + by) % length) for i in range(length)])]
    unnamed x52 -> x44, local copies, waits for them, and re-layouts: 4.89 us -> 6.98 us
    ppermute x9 -> x8, starting transfers between devices: 11 us -> 9.3 us  [turned(): lax.ppermute(value, 'harm', [(i, (i + by) % length) for i in range(length)])]
  transfers between devices with their start and end apart: 25 -> 20, of which waited for: 8 -> 5; matrix products, arithmetic and copies ran while one was open for 6% -> 8% of each run, Pallas kernels for 56% -> 60%
where the time goes in v2:
time: 295 us; the launch traced here: 292 us
  Pallas kernels  177 us (60%)
  waiting for transfers between devices  43.6 us (15%)
  starting transfers between devices  39.5 us (13%)
  local copies, waits for them, and re-layouts  19.1 us (6%)
  other arithmetic  12 us (4%)
    pallas_call x4, Pallas kernels, solve(): pl.pallas_call(functools.partial(solve_kernel, groups, own, layers, parts...  151 us
    ppermute x8, waiting for transfers between devices, turned(): lax.ppermute(value, 'harm', [(i, (i + by) % length) for i in range(length)])  34.7 us
    ppermute x8, starting transfers between devices, shifted(): lax.ppermute(value, axis, [(i, i + by) for i in range(length) if 0 <= i +...  18.6 us
    pallas_call x3, Pallas kernels, gather(): pl.pallas_call(functools.partial(gather_kernel, groups, own, layers, part...  17.4 us
    ppermute x4, starting transfers between devices, turned_and_shifted(): return lax.ppermute(value, ('harm', 'sx'), pairs)  11.5 us
    ppermute x8, starting transfers between devices, turned(): lax.ppermute(value, 'harm', [(i, (i + by) % length) for i in range(length)])  9.3 us
    pallas_call x4, Pallas kernels, place_into(): pl.pallas_call(place_kernel, grid_spec=pltpu.PrefetchScalarGridSpec(num_s...  9.05 us
    ppermute x4, waiting for transfers between devices, turned_and_shifted(): return lax.ppermute(value, ('harm', 'sx'), pairs)  8.92 us
  transfers between devices with their start and end apart: 20, of which 5 were waited for; matrix products, arithmetic and copies ran while one was open for 8% of the time, Pallas kernels for 60%

profile of v2, /device:TPU:16, one launch (start us, length us, event | category | flops | bytes accessed | tf_op | source)
XLA Modules:
  0.0 292.2 jit_solution(15482040053061027104)
XLA Ops:
  0.7 1.0 add_convert_fusion
  2.6 1.3 collective-permute-start.1
  3.9 3.7 %collective-permute-start.2 = (f32[8,64,4]{2,1,0:T(8,128)}, f32[8,64,4]{2,1,0:T(8,128)}, u32[]{:S(2)}, u32[]{:S(2)}) collective-permute-start(f32[8,64,4]{2,1,0:T(8,128)} %get-tuple-element.59), channel_id=1, source_target_pairs={{0,1},{1,2},{2,3},{4,5},{5,6},{6,7},{8,9},{9,10},{10,11},{12,13},{... | collective-permute-start | bytes 24584 | tf_op jit(solution)/shard_map/ppermute | solution.py:40
  7.6 3.1 %constant_dynamic-slice_fusion.2 = (f32[16,2,64,128]{3,2,1,0:T(8,128)}, f32[16,2,64,128]{3,2,1,0:T(8,128)}) fusion(f32[16,16,64,128]{3,2,1,0:T(8,128)} %refs_0_.5, s32[]{:T(128)S(6)} %select_n.87, s32[]{:T(128)S(6)} %select_n.96), kind=kLoop, calls=%fused_computation.30 | loop fusion | bytes 4194312 | tf_op jit(solution)/shard_map/dynamic_slice | solution.py:274
  10.7 1.5 collective-permute-start.13
  12.2 2.6 constant_dynamic-slice_fusion.5
  14.8 3.4 %collective-permute-start.4 = (f32[16,8,4,128]{3,2,1,0:T(4,128)}, f32[16,8,4,128]{3,2,1,0:T(4,128)S(1)}, u32[]{:S(2)}, u32[]{:S(2)}) collective-permute-start(f32[16,8,4,128]{3,2,1,0:T(4,128)} %get-tuple-element.51), channel_id=1, source_target_pairs={{0,20},{4,24},{8,28},{16,4},{20,8},{24,12},{1,21},{5,25},{9,29},{1... | collective-permute-start | bytes 786440 | tf_op jit(solution)/shard_map/ppermute | solution.py:55
  18.9 1.5 collective-permute-start.9
  20.4 1.0 fusion.10
  22.1 1.7 constant_dynamic-slice_fusion.7
  24.5 2.7 select_multiply_fusion.heat_scale_ref
  27.2 15.0 %collective-permute-done.9 = f32[16]{0:T(128)S(1)} collective-permute-done((f32[16]{0:T(128)S(1)}, f32[16]{0:T(128)S(1)}, u32[]{:S(2)}, u32[]{:S(2)}) %collective-permute-start.9) | collective-permute-done | bytes 96 | tf_op jit(solution)/shard_map/ppermute | solution.py:45
  42.2 1.5 collective-permute-start.10
  44.1 1.2 fusion.5
  45.3 1.1 fusion.3
  46.4 3.5 %collective-permute-start.3 = (f32[18,8,4,128]{3,2,1,0:T(4,128)S(1)}, f32[18,8,4,128]{3,2,1,0:T(4,128)S(1)}, u32[]{:S(2)}, u32[]{:S(2)}) collective-permute-start(f32[18,8,4,128]{3,2,1,0:T(4,128)S(1)} %get-tuple-element.57), channel_id=1, source_target_pairs={{0,4},{4,8},{8,12},{16,20},{20,24},{24,28},{1,5},{5,9},{9,13},{17,... | collective-permute-start | bytes 884744 | tf_op jit(solution)/shard_map/ppermute | solution.py:55
  49.9 2.4 collective-permute-start.5
  52.9 3.6 %collective-permute-done.3.refs_2_ = f32[18,8,4,128]{3,2,1,0:T(4,128)S(1)} collective-permute-done((f32[18,8,4,128]{3,2,1,0:T(4,128)S(1)}, f32[18,8,4,128]{3,2,1,0:T(4,128)S(1)}, u32[]{:S(2)}, u32[]{:S(2)}) %collective-permute-start.3) | collective-permute-done | bytes 294944 | tf_op jit(solution)/shard_map/ppermute | solution.py:55
  56.5 2.3 collective-permute-start.6
  58.9 0.9 collective-permute-done.5.refs_4_
  62.0 4.4 %collective-permute-done.6.refs_5_ = f32[16,8,4,128]{3,2,1,0:T(4,128)S(1)} collective-permute-done((f32[16,8,4,128]{3,2,1,0:T(4,128)}, f32[16,8,4,128]{3,2,1,0:T(4,128)S(1)}, u32[]{:S(2)}, u32[]{:S(2)}) %collective-permute-start.6) | collective-permute-done | bytes 262176 | tf_op jit(solution)/shard_map/ppermute | solution.py:55
  67.1 5.2 %shard_map.115 = (f32[1,40,128,128]{3,2,1,0:T(8,128)}, f32[1,40,8,128]{3,2,1,0:T(8,128)}, f32[1,40,8,128]{3,2,1,0:T(8,128)}) custom-call(s32[2]{0:T(128)} %pad_add_fusion.place_ref, f32[16,16,64,128]{3,2,1,0:T(8,128)} %refs_0_.5, f32[16,2,64,128]{3,2,1,0:T(8,128)} %collective-permute-done.13.refs_1_, f32[18,8,4,128]{3,2,1,0:T(4,128)} %copy-done, ...), custom_call_target="tpu_custom_call" | custom-call | bytes 5242880 | tf_op jit(solution)/shard_map/pallas_call | solution.py:307
  72.4 1.3 collective-permute-start.14
  73.7 3.0 %collective-permute-start.15 = (f32[1,40,8,128]{3,2,1,0:T(8,128)}, f32[1,40,8,128]{3,2,1,0:T(8,128)S(1)}, u32[]{:S(2)}, u32[]{:S(2)}) collective-permute-start(f32[1,40,8,128]{3,2,1,0:T(8,128)} %get-tuple-element.31), channel_id=1, source_target_pairs={{0,1},{1,2},{2,3},{4,5},{5,6},{6,7},{8,9},{9,10},{10,11},{12,13},{... | collective-permute-start | bytes 491528 | tf_op jit(solution)/shard_map/ppermute | solution.py:40
  76.7 1.2 fusion.1
  78.3 1.2 pad.9.code_ref
  79.5 5.3 %shard_map.114 = (f32[1,40,128,128]{3,2,1,0:T(8,128)}, f32[1,40,8,128]{3,2,1,0:T(8,128)}, f32[1,40,8,128]{3,2,1,0:T(8,128)}) custom-call(s32[2]{0:T(128)} %pad_add_fusion.place_ref, f32[16,16,64,128]{3,2,1,0:T(8,128)} %refs_0_.5, f32[16,2,64,128]{3,2,1,0:T(8,128)} %collective-permute-done.10.refs_1_, f32[18,8,4,128]{3,2,1,0:T(4,128)} %copy-done, ...), custom_call_target="tpu_custom_call" | custom-call | bytes 5242880 | tf_op jit(solution)/shard_map/pallas_call | solution.py:307
  84.8 1.3 collective-permute-start.11
  86.1 3.0 %collective-permute-start.12 = (f32[1,40,8,128]{3,2,1,0:T(8,128)}, f32[1,40,8,128]{3,2,1,0:T(8,128)S(1)}, u32[]{:S(2)}, u32[]{:S(2)}) collective-permute-start(f32[1,40,8,128]{3,2,1,0:T(8,128)} %get-tuple-element.28), channel_id=1, source_target_pairs={{0,1},{1,2},{2,3},{4,5},{5,6},{6,7},{8,9},{9,10},{10,11},{12,13},{... | collective-permute-start | bytes 491528 | tf_op jit(solution)/shard_map/ppermute | solution.py:40
  89.9 37.6 %shard_map.116 = (f32[16,16,64,128]{3,2,1,0:T(8,128)}, f32[16,2,64,128]{3,2,1,0:T(8,128)}, f32[2,64,128]{2,1,0:T(8,128)}) custom-call(s32[2]{0:T(128)} %pad_add_fusion.place_ref, f32[1,40,128,128]{3,2,1,0:T(8,128)} %get-tuple-element.29.image_ref, f32[1,40,8,128]{3,2,1,0:T(8,128)} %copy-done.20, f32[1,40,8,128]{3,2,1,0:T(8,128)} %copy-done.21, ...), custom_call_target="tpu_custom_call" | custom-call | flops 17112760320 | bytes 11141120 | tf_op jit(solution)/shard_map/pallas_call | solution.py:338
  128.0 6.8 %shard_map.113 = (f32[2,40,128,128]{3,2,1,0:T(8,128)}, f32[2,40,8,128]{3,2,1,0:T(8,128)}, f32[2,40,8,128]{3,2,1,0:T(8,128)}) custom-call(s32[2]{0:T(128)} %pad_add_fusion.place_ref, f32[16,16,64,128]{3,2,1,0:T(8,128)} %refs_0_.5, f32[16,4,64,128]{3,2,1,0:T(8,128)} %collective-permute-done.refs_1_, f32[18,8,4,128]{3,2,1,0:T(4,128)} %copy-done, ...), custom_call_target="tpu_custom_call" | custom-call | bytes 10485760 | tf_op jit(solution)/shard_map/pallas_call | solution.py:307
  134.8 1.5 collective-permute-start.7
  136.3 3.5 %collective-permute-start.8 = (f32[2,40,8,128]{3,2,1,0:T(8,128)}, f32[2,40,8,128]{3,2,1,0:T(8,128)S(1)}, u32[]{:S(2)}, u32[]{:S(2)}) collective-permute-start(f32[2,40,8,128]{3,2,1,0:T(8,128)} %get-tuple-element.25), channel_id=1, source_target_pairs={{0,1},{1,2},{2,3},{4,5},{5,6},{6,7},{8,9},{9,10},{10,11},{12,13},{... | collective-permute-start | bytes 983048 | tf_op jit(solution)/shard_map/ppermute | solution.py:40
  140.5 37.7 %shard_map.117 = (f32[16,16,64,128]{3,2,1,0:T(8,128)}, f32[16,2,64,128]{3,2,1,0:T(8,128)}, f32[2,64,128]{2,1,0:T(8,128)}) custom-call(s32[2]{0:T(128)} %pad_add_fusion.place_ref, f32[1,40,128,128]{3,2,1,0:T(8,128)} %get-tuple-element.26.image_ref, f32[1,40,8,128]{3,2,1,0:T(8,128)} %copy-done.18, ...), custom_call_target="tpu_custom_call", output_to_operand_aliasing={{0}: (10, {})} | custom-call | flops 17112760320 | bytes 11141120 | tf_op jit(solution)/shard_map/pallas_call | solution.py:338
  178.1 1.5 collective-permute-start.16
  179.7 1.0 copy-done.5
  180.7 2.3 shard_map.118.refs_0_
  183.8 37.6 %shard_map.119 = (f32[16,16,64,128]{3,2,1,0:T(8,128)}, f32[16,2,64,128]{3,2,1,0:T(8,128)}, f32[2,64,128]{2,1,0:T(8,128)}) custom-call(s32[2]{0:T(128)} %pad_add_fusion.place_ref, f32[2,40,128,128]{3,2,1,0:T(8,128)} %get-tuple-element.23.image_ref, f32[2,40,8,128]{3,2,1,0:T(8,128)} %copy-done.16, ...), custom_call_target="tpu_custom_call", output_to_operand_aliasing={{0}: (10, {})} | custom-call | flops 17112760320 | bytes 11141120 | tf_op jit(solution)/shard_map/pallas_call | solution.py:338
  221.9 1.0 copy-done.7
  222.9 2.3 shard_map.120.refs_0_
  225.1 37.7 %shard_map.121 = (f32[16,16,64,128]{3,2,1,0:T(8,128)}, f32[16,2,64,128]{3,2,1,0:T(8,128)}, f32[2,64,128]{2,1,0:T(8,128)}) custom-call(s32[2]{0:T(128)} %pad_add_fusion.place_ref, f32[2,40,128,128]{3,2,1,0:T(8,128)} %get-tuple-element.23.image_ref, f32[2,40,8,128]{3,2,1,0:T(8,128)} %copy-done.16, ...), custom_call_target="tpu_custom_call", output_to_operand_aliasing={{0}: (10, {})} | custom-call | flops 17112760320 | bytes 11141120 | tf_op jit(solution)/shard_map/pallas_call | solution.py:338
  262.8 1.5 collective-permute-start.18
  264.4 1.6 pad_maximum_fusion.5
  265.9 1.0 copy-done.6
  266.9 2.3 shard_map.122.whole_ref
  269.2 19.7 %collective-permute-done.18.value_ref = f32[16,2,64,128]{3,2,1,0:T(8,128)S(1)} collective-permute-done((f32[16,2,64,128]{3,2,1,0:T(8,128)}, f32[16,2,64,128]{3,2,1,0:T(8,128)S(1)}, u32[]{:S(2)}, u32[]{:S(2)}) %collective-permute-start.18) | collective-permute-done | bytes 1048608 | tf_op jit(solution)/shard_map/ppermute | solution.py:45
  288.9 1.0 copy-done.8
  289.9 2.3 shard_map.123
  (85 shorter events, 10.5 us)
Async XLA Ops:
  0.6 20.8 %copy-start.15 = (f32[2,2,128]{2,1,0:T(2,128)S(1)}, f32[2,2,128]{2,1,0:T(2,128)}, u32[]{:S(2)}) copy-start(f32[2,2,128]{2,1,0:T(2,128)} %constant.101.clone) | copy-start | bytes 6148
  0.6 23.8 %copy-start.4 = (s32[16,64,128]{2,1,0:T(8,128)S(1)}, s32[16,64,128]{2,1,0:T(8,128)}, u32[]{:S(2)}) copy-start(s32[16,64,128]{2,1,0:T(8,128)} %param.11) | copy-start | bytes 1572868
  0.7 20.8 %copy-start.12 = (f32[3]{0:T(128)S(1)}, f32[3]{0:T(128)}, u32[]{:S(2)}) copy-start(f32[3]{0:T(128)} %param.15) | copy-start | bytes 40
  0.7 23.8 %copy-start.14 = (f32[3]{0:T(128)S(1)}, f32[3]{0:T(128)}, u32[]{:S(2)}) copy-start(f32[3]{0:T(128)} %param.13) | copy-start | bytes 40
  0.7 23.8 %copy-start.13 = (f32[3]{0:T(128)S(1)}, f32[3]{0:T(128)}, u32[]{:S(2)}) copy-start(f32[3]{0:T(128)} %param.14) | copy-start | bytes 40
  2.6 41.5 %collective-permute-start.1 = (f32[8,64,4]{2,1,0:T(8,128)}, f32[8,64,4]{2,1,0:T(8,128)}, u32[]{:S(2)}, u32[]{:S(2)}) collective-permute-start(f32[8,64,4]{2,1,0:T(8,128)} %get-tuple-element.58), channel_id=1, source_target_pairs={{1,0},{2,1},{3,2},{5,4},{6,5},{7,6},{9,8},{10,9},{11,10},{13,12},{... | collective-permute-start | bytes 24584 | tf_op jit(solution)/shard_map/ppermute | solution.py:40
  3.9 40.3 %collective-permute-start.2 = (f32[8,64,4]{2,1,0:T(8,128)}, f32[8,64,4]{2,1,0:T(8,128)}, u32[]{:S(2)}, u32[]{:S(2)}) collective-permute-start(f32[8,64,4]{2,1,0:T(8,128)} %get-tuple-element.59), channel_id=1, source_target_pairs={{0,1},{1,2},{2,3},{4,5},{5,6},{6,7},{8,9},{9,10},{10,11},{12,13},{... | collective-permute-start | bytes 24584 | tf_op jit(solution)/shard_map/ppermute | solution.py:40
  10.7 55.7 %collective-permute-start.13 = (f32[16,2,64,128]{3,2,1,0:T(8,128)}, f32[16,2,64,128]{3,2,1,0:T(8,128)}, u32[]{:S(2)}, u32[]{:S(2)}) collective-permute-start(f32[16,2,64,128]{3,2,1,0:T(8,128)} %get-tuple-element.48), channel_id=1, source_target_pairs={{0,16},{16,0},{1,17},{17,1},{2,18},{18,2},{3,19},{19,3},{4,20},{20... | collective-permute-start | bytes 3145736 | tf_op jit(solution)/shard_map/ppermute | solution.py:45
  14.8 47.2 %collective-permute-start.4 = (f32[16,8,4,128]{3,2,1,0:T(4,128)}, f32[16,8,4,128]{3,2,1,0:T(4,128)S(1)}, u32[]{:S(2)}, u32[]{:S(2)}) collective-permute-start(f32[16,8,4,128]{3,2,1,0:T(4,128)} %get-tuple-element.51), channel_id=1, source_target_pairs={{0,20},{4,24},{8,28},{16,4},{20,8},{24,12},{1,21},{5,25},{9,29},{1... | collective-permute-start | bytes 786440 | tf_op jit(solution)/shard_map/ppermute | solution.py:55
  18.9 23.3 %collective-permute-start.9 = (f32[16]{0:T(128)S(1)}, f32[16]{0:T(128)S(1)}, u32[]{:S(2)}, u32[]{:S(2)}) collective-permute-start(f32[16]{0:T(128)S(1)} %get-tuple-element.69), channel_id=1, source_target_pairs={{0,16},{16,0},{1,17},{17,1},{2,18},{18,2},{3,19},{19,3},{4,20},{20... | collective-permute-start | bytes 200 | tf_op jit(solution)/shard_map/ppermute | solution.py:45
  42.2 37.3 %collective-permute-start.10 = (f32[16,2,64,128]{3,2,1,0:T(8,128)}, f32[16,2,64,128]{3,2,1,0:T(8,128)}, u32[]{:S(2)}, u32[]{:S(2)}) collective-permute-start(f32[16,2,64,128]{3,2,1,0:T(8,128)} %get-tuple-element.49), channel_id=1, source_target_pairs={{0,16},{16,0},{1,17},{17,1},{2,18},{18,2},{3,19},{19,3},{4,20},{20... | collective-permute-start | bytes 3145736 | tf_op jit(solution)/shard_map/ppermute | solution.py:45
  46.4 10.1 %collective-permute-start.3 = (f32[18,8,4,128]{3,2,1,0:T(4,128)S(1)}, f32[18,8,4,128]{3,2,1,0:T(4,128)S(1)}, u32[]{:S(2)}, u32[]{:S(2)}) collective-permute-start(f32[18,8,4,128]{3,2,1,0:T(4,128)S(1)} %get-tuple-element.57), channel_id=1, source_target_pairs={{0,4},{4,8},{8,12},{16,20},{20,24},{24,28},{1,5},{5,9},{9,13},{17,... | collective-permute-start | bytes 884744 | tf_op jit(solution)/shard_map/ppermute | solution.py:55
  49.9 9.9 %collective-permute-start.5 = (f32[18,8,4,128]{3,2,1,0:T(4,128)S(1)}, f32[18,8,4,128]{3,2,1,0:T(4,128)S(1)}, u32[]{:S(2)}, u32[]{:S(2)}) collective-permute-start(f32[18,8,4,128]{3,2,1,0:T(4,128)S(1)} %get-tuple-element.56), channel_id=1, source_target_pairs={{4,0},{8,4},{12,8},{20,16},{24,20},{28,24},{5,1},{9,5},{13,9},{21,... | collective-permute-start | bytes 884744 | tf_op jit(solution)/shard_map/ppermute | solution.py:55
  56.5 9.9 %copy-start = (f32[18,8,4,128]{3,2,1,0:T(4,128)}, f32[18,8,4,128]{3,2,1,0:T(4,128)S(1)}, u32[]{:S(2)}) copy-start(f32[18,8,4,128]{3,2,1,0:T(4,128)S(1)} %collective-permute-done.3.refs_2_) | copy-start | bytes 884740
  56.5 9.9 %collective-permute-start.6 = (f32[16,8,4,128]{3,2,1,0:T(4,128)}, f32[16,8,4,128]{3,2,1,0:T(4,128)S(1)}, u32[]{:S(2)}, u32[]{:S(2)}) collective-permute-start(f32[16,8,4,128]{3,2,1,0:T(4,128)} %get-tuple-element.50), channel_id=1, source_target_pairs={{4,16},{8,20},{12,24},{20,0},{24,4},{28,8},{5,17},{9,21},{13,25},{... | collective-permute-start | bytes 786440 | tf_op jit(solution)/shard_map/ppermute | solution.py:55
  59.8 6.7 %copy-start.1 = (f32[18,8,4,128]{3,2,1,0:T(4,128)}, f32[18,8,4,128]{3,2,1,0:T(4,128)S(1)}, u32[]{:S(2)}) copy-start(f32[18,8,4,128]{3,2,1,0:T(4,128)S(1)} %collective-permute-done.5.refs_4_) | copy-start | bytes 884740
  59.8 68.2 %collective-permute-start = (f32[16,4,64,128]{3,2,1,0:T(8,128)S(1)}, f32[16,4,64,128]{3,2,1,0:T(8,128)}, u32[]{:S(2)}, u32[]{:S(2)}) collective-permute-start(f32[16,4,64,128]{3,2,1,0:T(8,128)S(1)} %constant_dynamic-slice_fusion.7), channel_id=1, source_target_pairs={{0,16},{16,0},{1,17},{17,1},{2,18},{18,2},{3,19},{19,3},{4,20},{20... | collective-permute-start | bytes 6291464 | tf_op jit(solution)/shard_map/ppermute | solution.py:45
  62.0 4.4 %copy-start.2 = (f32[16,8,4,128]{3,2,1,0:T(4,128)}, f32[16,8,4,128]{3,2,1,0:T(4,128)S(1)}, u32[]{:S(2)}) copy-start(f32[16,8,4,128]{3,2,1,0:T(4,128)S(1)} %collective-permute-done.4.refs_3_) | copy-start | bytes 786436
  66.4 0.7 copy-start.3
  72.4 16.8 %collective-permute-start.14 = (f32[1,40,8,128]{3,2,1,0:T(8,128)}, f32[1,40,8,128]{3,2,1,0:T(8,128)S(1)}, u32[]{:S(2)}, u32[]{:S(2)}) collective-permute-start(f32[1,40,8,128]{3,2,1,0:T(8,128)} %get-tuple-element.30), channel_id=1, source_target_pairs={{1,0},{2,1},{3,2},{5,4},{6,5},{7,6},{9,8},{10,9},{11,10},{13,12},{... | collective-permute-start | bytes 491528 | tf_op jit(solution)/shard_map/ppermute | solution.py:40
  73.7 15.5 %collective-permute-start.15 = (f32[1,40,8,128]{3,2,1,0:T(8,128)}, f32[1,40,8,128]{3,2,1,0:T(8,128)S(1)}, u32[]{:S(2)}, u32[]{:S(2)}) collective-permute-start(f32[1,40,8,128]{3,2,1,0:T(8,128)} %get-tuple-element.31), channel_id=1, source_target_pairs={{0,1},{1,2},{2,3},{4,5},{5,6},{6,7},{8,9},{9,10},{10,11},{12,13},{... | collective-permute-start | bytes 491528 | tf_op jit(solution)/shard_map/ppermute | solution.py:40
  84.8 54.9 %collective-permute-start.11 = (f32[1,40,8,128]{3,2,1,0:T(8,128)}, f32[1,40,8,128]{3,2,1,0:T(8,128)S(1)}, u32[]{:S(2)}, u32[]{:S(2)}) collective-permute-start(f32[1,40,8,128]{3,2,1,0:T(8,128)} %get-tuple-element.27), channel_id=1, source_target_pairs={{1,0},{2,1},{3,2},{5,4},{6,5},{7,6},{9,8},{10,9},{11,10},{13,12},{... | collective-permute-start | bytes 491528 | tf_op jit(solution)/shard_map/ppermute | solution.py:40
  86.1 53.7 %collective-permute-start.12 = (f32[1,40,8,128]{3,2,1,0:T(8,128)}, f32[1,40,8,128]{3,2,1,0:T(8,128)S(1)}, u32[]{:S(2)}, u32[]{:S(2)}) collective-permute-start(f32[1,40,8,128]{3,2,1,0:T(8,128)} %get-tuple-element.28), channel_id=1, source_target_pairs={{0,1},{1,2},{2,3},{4,5},{5,6},{6,7},{8,9},{9,10},{10,11},{12,13},{... | collective-permute-start | bytes 491528 | tf_op jit(solution)/shard_map/ppermute | solution.py:40
  89.2 0.7 copy-start.20
  89.2 0.7 copy-start.21
  127.5 52.2 %collective-permute-start.17 = (f32[16,2,64,128]{3,2,1,0:T(8,128)}, f32[16,2,64,128]{3,2,1,0:T(8,128)S(1)}, u32[]{:S(2)}, u32[]{:S(2)}) collective-permute-start(f32[16,2,64,128]{3,2,1,0:T(8,128)} %get-tuple-element.34), channel_id=1, source_target_pairs={{0,16},{16,0},{1,17},{17,1},{2,18},{18,2},{3,19},{19,3},{4,20},{20... | collective-permute-start | bytes 3145736 | tf_op jit(solution)/shard_map/ppermute | solution.py:45
  134.8 48.1 %collective-permute-start.7 = (f32[2,40,8,128]{3,2,1,0:T(8,128)}, f32[2,40,8,128]{3,2,1,0:T(8,128)S(1)}, u32[]{:S(2)}, u32[]{:S(2)}) collective-permute-start(f32[2,40,8,128]{3,2,1,0:T(8,128)} %get-tuple-element.24), channel_id=1, source_target_pairs={{1,0},{2,1},{3,2},{5,4},{6,5},{7,6},{9,8},{10,9},{11,10},{13,12},{... | collective-permute-start | bytes 983048 | tf_op jit(solution)/shard_map/ppermute | solution.py:40
  136.3 46.7 %collective-permute-start.8 = (f32[2,40,8,128]{3,2,1,0:T(8,128)}, f32[2,40,8,128]{3,2,1,0:T(8,128)S(1)}, u32[]{:S(2)}, u32[]{:S(2)}) collective-permute-start(f32[2,40,8,128]{3,2,1,0:T(8,128)} %get-tuple-element.25), channel_id=1, source_target_pairs={{0,1},{1,2},{2,3},{4,5},{5,6},{6,7},{8,9},{9,10},{10,11},{12,13},{... | collective-permute-start | bytes 983048 | tf_op jit(solution)/shard_map/ppermute | solution.py:40
  139.8 0.7 copy-start.18
  139.8 0.7 copy-start.19
  178.1 43.8 %collective-permute-start.16 = (f32[16,2,64,128]{3,2,1,0:T(8,128)}, f32[16,2,64,128]{3,2,1,0:T(8,128)S(1)}, u32[]{:S(2)}, u32[]{:S(2)}) collective-permute-start(f32[16,2,64,128]{3,2,1,0:T(8,128)} %get-tuple-element.33), channel_id=1, source_target_pairs={{0,16},{16,0},{1,17},{17,1},{2,18},{18,2},{3,19},{19,3},{4,20},{20... | collective-permute-start | bytes 3145736 | tf_op jit(solution)/shard_map/ppermute | solution.py:45
  179.7 1.0 copy-start.5
  182.9 0.8 copy-start.16
  182.9 0.9 copy-start.17
  221.4 44.5 %collective-permute-start.19 = (f32[16,2,64,128]{3,2,1,0:T(8,128)}, f32[16,2,64,128]{3,2,1,0:T(8,128)S(1)}, u32[]{:S(2)}, u32[]{:S(2)}) collective-permute-start(f32[16,2,64,128]{3,2,1,0:T(8,128)} %get-tuple-element.38), channel_id=1, source_target_pairs={{0,16},{16,0},{1,17},{17,1},{2,18},{18,2},{3,19},{19,3},{4,20},{20... | collective-permute-start | bytes 3145736 | tf_op jit(solution)/shard_map/ppermute | solution.py:45
  221.9 1.0 copy-start.7
  225.1 39.2 %copy-start.9 = (f32[2,64,128]{2,1,0:T(8,128)S(1)}, f32[2,64,128]{2,1,0:T(8,128)}, u32[]{:S(2)}) copy-start(f32[2,64,128]{2,1,0:T(8,128)} %get-tuple-element.40) | copy-start | bytes 196612
  225.1 39.2 %copy-start.10 = (f32[2,64,128]{2,1,0:T(8,128)S(1)}, f32[2,64,128]{2,1,0:T(8,128)}, u32[]{:S(2)}) copy-start(f32[2,64,128]{2,1,0:T(8,128)} %get-tuple-element.41) | copy-start | bytes 196612
  225.1 39.2 %copy-start.11 = (f32[2,64,128]{2,1,0:T(8,128)S(1)}, f32[2,64,128]{2,1,0:T(8,128)}, u32[]{:S(2)}) copy-start(f32[2,64,128]{2,1,0:T(8,128)} %get-tuple-element.42) | copy-start | bytes 196612
  262.8 26.1 %collective-permute-start.18 = (f32[16,2,64,128]{3,2,1,0:T(8,128)}, f32[16,2,64,128]{3,2,1,0:T(8,128)S(1)}, u32[]{:S(2)}, u32[]{:S(2)}) collective-permute-start(f32[16,2,64,128]{3,2,1,0:T(8,128)} %get-tuple-element.37), channel_id=1, source_target_pairs={{0,16},{16,0},{1,17},{17,1},{2,18},{18,2},{3,19},{19,3},{4,20},{20... | collective-permute-start | bytes 3145736 | tf_op jit(solution)/shard_map/ppermute | solution.py:45
  265.9 1.0 copy-start.6
  288.9 1.0 copy-start.8

commit v3 on v2

--- a/solution.py
+++ b/solution.py
@@ -17,6 +17,7 @@
 RIM = 4
 STEP = 1
 UNROLL = 12
+BLOCK = 4
 SPARE = UNROLL + 4
 
 relax_factor = 0.5
@@ -85,7 +86,7 @@
 
 def solve_kernel(
     groups, own, layers, parts, rows, columns,
-    chained, place_ref, image_ref, ahead_ref, behind_ref, code_ref, table_ref, fwd_ref, inv_ref, weight_ref, heat_scale_ref,
+    chained, place_ref, image_ref, ahead_ref, behind_ref, code_ref, table_ref, fwd_ref, inv_ref, weight_ref, material_ref, sigma_ref,
     *refs,
 ):
     refs = refs[chained:]
@@ -96,68 +97,78 @@
     total = span + 2 * RIM
     wide = columns + 8
 
-    def load(x, carry):
-        code = code_ref[0, x]
+    def load(block, carry):
+        code = code_ref[0, block]
         chosen = jnp.concatenate([jnp.where(code == m, 1.0, 0.0) for m in (1.0, 2.0, 3.0)] * 3, axis=0)
         picked = lax.dot_general(
             chosen.astype(jnp.bfloat16), table_ref[...], (((0,), (0,)), ((), ())), preferred_element_type=jnp.float32)
-        for k, ref in enumerate((nu_all, nu_sat, gain, turn_gain, feed)):
-            ref[x] = picked[:wide, k * LANES : (k + 1) * LANES]
-        pot[x, 0:columns, :] = image_ref[0, x]
         edge = lax.broadcasted_iota(jnp.int32, (8, LANES), 0) < RIM
-        pot[x, columns:wide, :] = jnp.where(edge, ahead_ref[0, x], behind_ref[0, x])
-        pot[x, wide : wide + 8, :] = image_ref[0, x, 0:8, :]
+        for r in range(BLOCK):
+            x = block * BLOCK + r
+            for k, ref in enumerate((nu_all, nu_sat, gain, turn_gain, feed)):
+                ref[x] = picked[r * wide : (r + 1) * wide, k * LANES : (k + 1) * LANES]
+            pot[x, 0:columns, :] = image_ref[0, x]
+            pot[x, columns:wide, :] = jnp.where(edge, ahead_ref[0, x], behind_ref[0, x])
+            pot[x, wide : wide + 8, :] = image_ref[0, x, 0:8, :]
         return carry
 
-    lax.fori_loop(0, total, load, 0, unroll=4)
+    lax.fori_loop(0, total // BLOCK, load, 0, unroll=2)
     for k in range(SPARE):
         pot[total + k] = jnp.zeros((wide + 8, LANES), jnp.float32)
-    even = lax.broadcasted_iota(jnp.int32, (wide, LANES), 1) % 2 == 0
-
-    def fields_at(base):
-        here = [pot[base + k, 0:wide, :] for k in range(STEP + 1)]
-        field_x = [pot[base + k, 1 : wide + 1, :] - here[k] for k in range(STEP)]
-        field_y = [here[k] - here[k + 1] for k in range(STEP)]
-        return here, field_x, field_y
+    tiles = [(8 * t, 16 * t) for t in range(wide // 8)]
+    even = lax.broadcasted_iota(jnp.int32, (8, LANES), 1) % 2 == 0
+
+    def fields_at(base, y):
+        here = pot[base, y : y + 8, :]
+        return here, pot[base, y + 1 : y + 9, :] - here, here - pot[base + 1, y : y + 8, :]
 
     def to_samples(base, slot):
-        _, field_x, field_y = fields_at(base)
-        fields = jnp.concatenate([f for pair in zip(field_x, field_y) for f in pair], axis=0)
-        high, low = split(fields)
+        operand = []
+        for y, _ in tiles:
+            _, field_x, field_y = fields_at(base, y)
+            high, low = split(jnp.concatenate([field_x, field_y], axis=0))
+            operand.append(jnp.concatenate([high, low, high], axis=1))
         samples[slot][...] = jnp.dot(
-            jnp.concatenate([high, low, high], axis=1), fwd_ref[0], preferred_element_type=jnp.float32)
+            jnp.concatenate(operand, axis=0), fwd_ref[0], preferred_element_type=jnp.float32)
 
     def saturate(slot):
-        for k in range(STEP):
-            sample_x = samples[slot][2 * k * wide : (2 * k + 1) * wide, :]
-            sample_y = samples[slot][(2 * k + 1) * wide : (2 * k + 2) * wide, :]
+        for _, m in tiles:
+            sample_x = samples[slot][m : m + 8, :]
+            sample_y = samples[slot][m + 8 : m + 16, :]
             square = 1.0 + (sample_x * sample_x + sample_y * sample_y)
             inverse = lax.rsqrt(square)
-            scaled = square * inverse
-            factor = inverse * (1.0 / jnp.tanh(scaled) - inverse)
+            factor = inverse * (1.0 / jnp.tanh(square * inverse) - inverse)
             high, low = split(jnp.concatenate([factor * sample_x, factor * sample_y], axis=0))
-            products[slot][2 * k * wide : (2 * k + 2) * wide, 0 : 2 * LANES] = high
-            products[slot][2 * k * wide : (2 * k + 2) * wide, 2 * LANES :] = low
-
-    def update(base, slot):
-        here, field_x, field_y = fields_at(base)
+            products[slot][m : m + 16, 0 : 2 * LANES] = high
+            products[slot][m : m + 16, 2 * LANES :] = low
+
+    def intensity(pair, at, y, m, field_x, field_y):
+        back = pair[m : m + 16, :LANES] + pair[m : m + 16, LANES:]
+        linear, bent = nu_all[at, y : y + 8, :], nu_sat[at, y : y + 8, :]
+        return linear * field_x - bent * back[:8], linear * field_y - bent * back[8:]
+
+    def update(at, slot):
         pair = jnp.dot(products[slot][...], inv_ref[0], preferred_element_type=jnp.float32)
-        back = pair[:, :LANES] + pair[:, LANES:]
-        above = last_row[...]
-        for k in range(STEP):
-            at = base + k
-            linear, bent = nu_all[at], nu_sat[at]
-            inten_x = linear * field_x[k] - bent * back[2 * k * wide : (2 * k + 1) * wide]
-            inten_y = linear * field_y[k] - bent * back[(2 * k + 1) * wide : (2 * k + 2) * wide]
-            back_x[k, 8 : wide + 8, :] = inten_x
-            back_x[k, 0:8, :] = inten_x[columns:]
-            curl = (inten_y - above) - (inten_x - back_x[k, 7 : wide + 7, :])
-            above = inten_y
-            rotated = jnp.where(even, pltpu.roll(here[k], LANES - 1, 1), pltpu.roll(here[k], 1, 1))
-            fresh = here[k] + feed[at] - gain[at] * curl - turn_gain[at] * rotated
-            pot[at, 0:wide, :] = fresh
-            pot[at, wide : wide + 8, :] = fresh[0:8]
-        last_row[...] = above
+        for y, m in tiles[-1:] + tiles[:-1]:
+            here, field_x, field_y = fields_at(at, y)
+            inten_x, inten_y = intensity(pair, at, y, m, field_x, field_y)
+            back_x[y + 8 : y + 16, :] = inten_x
+            if y == columns:
+                back_x[0:8, :] = inten_x
+                held = here, inten_x, inten_y
+                continue
+            settle(at, y, here, inten_x, inten_y)
+        settle(at, columns, *held)
+
+    def settle(at, y, here, inten_x, inten_y):
+        curl = (inten_y - last_row[y : y + 8, :]) - (inten_x - back_x[y + 7 : y + 15, :])
+        last_row[y : y + 8, :] = inten_y
+        rotated = jnp.where(even, pltpu.roll(here, LANES - 1, 1), pltpu.roll(here, 1, 1))
+        fresh = (here + feed[at, y : y + 8, :] - gain[at, y : y + 8, :] * curl
+                 - turn_gain[at, y : y + 8, :] * rotated)
+        pot[at, y : y + 8, :] = fresh
+        if y == 0:
+            pot[at, wide : wide + 8, :] = fresh
 
     def sweep(index, carry):
         first = index + 2
@@ -165,9 +176,10 @@
         to_samples(first - 1, 1)
         saturate(1)
         to_samples(first, 0)
-        pair = jnp.dot(products[1][wide:], inv_ref[0], preferred_element_type=jnp.float32)
-        fall = pot[first - 1, 0:wide, :] - pot[first, 0:wide, :]
-        last_row[...] = nu_all[first - 1] * fall - nu_sat[first - 1] * (pair[:, :LANES] + pair[:, LANES:])
+        pair = jnp.dot(products[1][...], inv_ref[0], preferred_element_type=jnp.float32)
+        for y, m in tiles:
+            _, field_x, field_y = fields_at(first - 1, y)
+            last_row[y : y + 8, :] = intensity(pair, first - 1, y, m, field_x, field_y)[1]
         saturate(0)
         to_samples(first + STEP, 1)
 
@@ -200,7 +212,8 @@
                         begin = g * lanes_each + (layer * parts + part) * own
                         outs[g][:, layer, pl.ds(where, 1), :] = flipped[begin : begin + own].reshape(own, 1, columns)
                         power = power + jnp.sum(powers[begin : begin + own], axis=0, keepdims=True)
-                    heat_ref[layer, pl.ds(where, 1), :] = power * heat_scale_ref[layer, pl.ds(where, 1), :]
+                    sigma = lookup([sigma_ref[m] for m in range(3)], material_ref[layer, pl.ds(where, 1), :])
+                    heat_ref[layer, pl.ds(where, 1), :] = power * sigma * (0.5 / (own * groups))
         return carry
 
     lax.fori_loop(0, span // 8, finish, 0)
@@ -274,7 +287,6 @@
         return lax.dynamic_slice_in_dim(value, group * slab + start, count, 1)
 
     slab_material = lax.dynamic_slice_in_dim(material, place * slab, slab, 0)
-    heat_scale = lookup(conductivity, slab_material) * (0.5 / coefs)
     code = (slab_material + 1).astype(jnp.float32)
     batches = [b for b in ((0, 1), (1, 1), (2, chunks - 2)) if b[0] < chunks]
     tops, bottoms, arrivals = [], [], []
@@ -297,9 +309,8 @@
     code = jnp.concatenate([tops[0][own:], riders, bottoms[0][own:]], axis=2)
     code = jnp.concatenate([code[0], code[1, :, :, : 2 * RIM]], axis=2)
     code = jnp.stack([code[:, part * span : part * span + total] for part in range(parts)], axis=1)
-    code = code.reshape(chunks, cells, total, wide).transpose(0, 2, 1, 3)
+    code = code.reshape(chunks, cells, total // BLOCK, BLOCK * wide).transpose(0, 2, 1, 3)
     code = jnp.pad(code, ((0, 0), (0, 0), (0, 8 - cells), (0, 0)))
-
     index = jnp.stack([place, place * chunks]).astype(jnp.int32)
 
     def gather(start, count, arrived):
@@ -344,12 +355,13 @@
                     pl.BlockSpec((1, total, columns, LANES), part),
                     pl.BlockSpec((1, total, 8, LANES), part),
                     pl.BlockSpec((1, total, 8, LANES), part),
-                    pl.BlockSpec((1, total, 8, wide), lambda i, s: (k, 0, 0, 0)),
+                    pl.BlockSpec((1, total // BLOCK, 8, BLOCK * wide), lambda i, s: (k, 0, 0, 0)),
                     pl.BlockSpec((72, 5 * LANES), fixed),
                     pl.BlockSpec((1, 3 * LANES, 2 * LANES), chosen),
                     pl.BlockSpec((1, 4 * LANES, 2 * LANES), chosen),
                     pl.BlockSpec((1, LANES, LANES), chosen),
-                    pl.BlockSpec((layers, rows, columns), lambda i, s: (k, 0, 0)),
+                    pl.BlockSpec((layers, rows, columns), lambda i, s: (s[1] + k, 0, 0)),
+                    pl.BlockSpec(memory_space=pltpu.SMEM),
                 ] + [pl.BlockSpec(memory_space=pl.ANY)] * chained,
                 out_specs=[pl.BlockSpec((own, layers, rows, columns), lambda i, s: (0, s[1] + k, 0, 0))]
                 + [pl.BlockSpec((own, layers, rows, columns), lambda i, s: (0, 0, 0, 0))] * (groups - 1)
@@ -358,15 +370,15 @@
                 + [pltpu.VMEM((total + SPARE, wide, LANES), jnp.float32)] * 5
                 + [pltpu.VMEM((2 * STEP * wide, 2 * LANES), jnp.float32)] * 2
                 + [pltpu.VMEM((2 * STEP * wide, 4 * LANES), jnp.bfloat16)] * 2
-                + [pltpu.VMEM((wide, LANES), jnp.float32), pltpu.VMEM((STEP, wide + 8, LANES), jnp.float32)],
+                + [pltpu.VMEM((wide, LANES), jnp.float32), pltpu.VMEM((wide + 8, LANES), jnp.float32)],
             ),
             out_shape=[whole]
             + [jax.ShapeDtypeStruct((own, layers, rows, columns), jnp.float32)] * (groups - 1)
             + [jax.ShapeDtypeStruct((layers, rows, columns), jnp.float32)],
-            input_output_aliases={10: 0} if chained else {},
+            input_output_aliases={11: 0} if chained else {},
             cost_estimate=pl.CostEstimate(
                 flops=6 * total * wide * 256 * 256 * 8, bytes_accessed=4 * total * wide * LANES * 4, transcendentals=0),
-        )(index, image, ahead, behind, code, table, fwd, inv, weight, heat_scale, *([potential] if chained else []))
+        )(index, image, ahead, behind, code, table, fwd, inv, weight, material, conductivity, *([potential] if chained else []))
 
     def place_into(potential, value, block):
         return pl.pallas_call(
@@ -395,9 +407,6 @@
     for k in range(chunks):
         potential, *others, heat = solve(k, *ready[k], potential)
         heats.append(heat)
-        for value, block in coming:
-            potential = place_into(potential, value, block)
-        coming = []
         for g in range(1, groups):
             coming.append((turned(others[g - 1], g), blocks[g].reshape(1) + k))
     for value, block in coming:

time: 295 us -> 276 us (0.936)
  Pallas kernels: 177 us -> 167 us
  other arithmetic: 12 us -> 7.34 us
    pallas_call x4, Pallas kernels: 151 us -> 141 us  [solve(): pl.pallas_call(functools.partial(solve_kernel, groups, own, layers, parts...]
    unnamed x44 -> x34, local copies, waits for them, and re-layouts: 6.98 us -> 4.58 us
  transfers between devices with their start and end apart: 20 -> 20, of which waited for: 5 -> 5; matrix products, arithmetic and copies ran while one was open for 8% -> 6% of each run, Pallas kernels for 60% -> 60%
where the time goes in v3:
time: 276 us; the launch traced here: 273 us
  Pallas kernels  167 us (61%)
  waiting for transfers between devices  41 us (15%)
  starting transfers between devices  40.4 us (15%)
  local copies, waits for them, and re-layouts  16.3 us (6%)
  other arithmetic  7.34 us (3%)
    pallas_call x4, Pallas kernels, solve(): pl.pallas_call(functools.partial(solve_kernel, groups, own, layers, parts...  141 us
    ppermute x8, waiting for transfers between devices, turned(): lax.ppermute(value, 'harm', [(i, (i + by) % length) for i in range(length)])  32.1 us
    ppermute x8, starting transfers between devices, shifted(): lax.ppermute(value, axis, [(i, i + by) for i in range(length) if 0 <= i +...  19.6 us
    pallas_call x3, Pallas kernels, gather(): pl.pallas_call(functools.partial(gather_kernel, groups, own, layers, part...  17.3 us
    ppermute x4, starting transfers between devices, turned_and_shifted(): return lax.ppermute(value, ('harm', 'sx'), pairs)  11.5 us
    ppermute x8, starting transfers between devices, turned(): lax.ppermute(value, 'harm', [(i, (i + by) % length) for i in range(length)])  9.3 us
    pallas_call x4, Pallas kernels, place_into(): pl.pallas_call(place_kernel, grid_spec=pltpu.PrefetchScalarGridSpec(num_s...  9.05 us
    ppermute x4, waiting for transfers between devices, turned_and_shifted(): return lax.ppermute(value, ('harm', 'sx'), pairs)  8.9 us
  transfers between devices with their start and end apart: 20, of which 5 were waited for; matrix products, arithmetic and copies ran while one was open for 6% of the time, Pallas kernels for 60%

profile of v3, /device:TPU:16, one launch (start us, length us, event | category | flops | bytes accessed | tf_op | source)
XLA Modules:
  0.0 273.2 jit_solution(11487714593069170820)
XLA Ops:
  0.7 1.0 add_convert_fusion
  1.7 0.9 fusion.8
  2.5 1.3 collective-permute-start.1
  3.8 3.7 %collective-permute-start.2 = (f32[8,64,4]{2,1,0:T(8,128)}, f32[8,64,4]{2,1,0:T(8,128)}, u32[]{:S(2)}, u32[]{:S(2)}) collective-permute-start(f32[8,64,4]{2,1,0:T(8,128)} %get-tuple-element.59), channel_id=1, source_target_pairs={{0,1},{1,2},{2,3},{4,5},{5,6},{6,7},{8,9},{9,10},{10,11},{12,13},{... | collective-permute-start | bytes 24584 | tf_op jit(solution)/shard_map/ppermute | solution.py:41
  7.6 3.1 %constant_dynamic-slice_fusion.2 = (f32[16,2,64,128]{3,2,1,0:T(8,128)}, f32[16,2,64,128]{3,2,1,0:T(8,128)}) fusion(f32[16,16,64,128]{3,2,1,0:T(8,128)} %refs_0_.5, s32[]{:T(128)S(6)} %select_n.79, s32[]{:T(128)S(6)} %select_n.86), kind=kLoop, calls=%fused_computation.29 | loop fusion | bytes 4194312 | tf_op jit(solution)/shard_map/dynamic_slice | solution.py:287
  10.7 1.5 collective-permute-start.13
  12.2 2.6 constant_dynamic-slice_fusion.5
  14.8 3.4 %collective-permute-start.4 = (f32[16,8,4,128]{3,2,1,0:T(4,128)}, f32[16,8,4,128]{3,2,1,0:T(4,128)S(1)}, u32[]{:S(2)}, u32[]{:S(2)}) collective-permute-start(f32[16,8,4,128]{3,2,1,0:T(4,128)} %get-tuple-element.51), channel_id=1, source_target_pairs={{0,20},{4,24},{8,28},{16,4},{20,8},{24,12},{1,21},{5,25},{9,29},{1... | collective-permute-start | bytes 786440 | tf_op jit(solution)/shard_map/ppermute | solution.py:56
  18.9 1.5 collective-permute-start.9
  20.4 1.0 fusion.9
  21.5 1.7 constant_dynamic-slice_fusion.7
  23.9 18.3 %collective-permute-done.9 = f32[16]{0:T(128)S(1)} collective-permute-done((f32[16]{0:T(128)S(1)}, f32[16]{0:T(128)S(1)}, u32[]{:S(2)}, u32[]{:S(2)}) %collective-permute-start.9) | collective-permute-done | bytes 96 | tf_op jit(solution)/shard_map/ppermute | solution.py:46
  42.1 1.5 collective-permute-start.10
  44.1 1.1 fusion.5
  45.4 3.5 %collective-permute-start.3 = (f32[18,8,4,128]{3,2,1,0:T(4,128)S(1)}, f32[18,8,4,128]{3,2,1,0:T(4,128)S(1)}, u32[]{:S(2)}, u32[]{:S(2)}) collective-permute-start(f32[18,8,4,128]{3,2,1,0:T(4,128)S(1)} %get-tuple-element.57), channel_id=1, source_target_pairs={{0,4},{4,8},{8,12},{16,20},{20,24},{24,28},{1,5},{5,9},{9,13},{17,... | collective-permute-start | bytes 884744 | tf_op jit(solution)/shard_map/ppermute | solution.py:56
  48.9 2.4 collective-permute-start.5
  51.9 3.6 %collective-permute-done.3.refs_2_ = f32[18,8,4,128]{3,2,1,0:T(4,128)S(1)} collective-permute-done((f32[18,8,4,128]{3,2,1,0:T(4,128)S(1)}, f32[18,8,4,128]{3,2,1,0:T(4,128)S(1)}, u32[]{:S(2)}, u32[]{:S(2)}) %collective-permute-start.3) | collective-permute-done | bytes 294944 | tf_op jit(solution)/shard_map/ppermute | solution.py:56
  55.5 2.3 collective-permute-start.6
  57.8 0.9 collective-permute-done.5.refs_4_
  59.5 0.7 slice_bitcast_fusion
  60.2 0.7 slice_bitcast_fusion.1
  61.0 4.4 %collective-permute-done.6.refs_5_ = f32[16,8,4,128]{3,2,1,0:T(4,128)S(1)} collective-permute-done((f32[16,8,4,128]{3,2,1,0:T(4,128)}, f32[16,8,4,128]{3,2,1,0:T(4,128)S(1)}, u32[]{:S(2)}, u32[]{:S(2)}) %collective-permute-start.6) | collective-permute-done | bytes 262176 | tf_op jit(solution)/shard_map/ppermute | solution.py:56
  66.1 5.2 %shard_map.115 = (f32[1,40,128,128]{3,2,1,0:T(8,128)}, f32[1,40,8,128]{3,2,1,0:T(8,128)}, f32[1,40,8,128]{3,2,1,0:T(8,128)}) custom-call(s32[2]{0:T(128)} %pad_add_fusion.place_ref, f32[16,16,64,128]{3,2,1,0:T(8,128)} %refs_0_.5, f32[16,2,64,128]{3,2,1,0:T(8,128)} %collective-permute-done.13.refs_1_, f32[18,8,4,128]{3,2,1,0:T(4,128)} %copy-done, ...), custom_call_target="tpu_custom_call" | custom-call | bytes 5242880 | tf_op jit(solution)/shard_map/pallas_call | solution.py:318
  71.3 1.3 collective-permute-start.14
  72.6 3.7 %collective-permute-start.15 = (f32[1,40,8,128]{3,2,1,0:T(8,128)}, f32[1,40,8,128]{3,2,1,0:T(8,128)}, u32[]{:S(2)}, u32[]{:S(2)}) collective-permute-start(f32[1,40,8,128]{3,2,1,0:T(8,128)} %get-tuple-element.31), channel_id=1, source_target_pairs={{0,1},{1,2},{2,3},{4,5},{5,6},{6,7},{8,9},{9,10},{10,11},{12,13},{... | collective-permute-start | bytes 491528 | tf_op jit(solution)/shard_map/ppermute | solution.py:41
  76.3 1.2 fusion.1
  78.2 1.0 pad.9.code_ref
  79.2 5.3 %shard_map.114 = (f32[1,40,128,128]{3,2,1,0:T(8,128)}, f32[1,40,8,128]{3,2,1,0:T(8,128)}, f32[1,40,8,128]{3,2,1,0:T(8,128)}) custom-call(s32[2]{0:T(128)} %pad_add_fusion.place_ref, f32[16,16,64,128]{3,2,1,0:T(8,128)} %refs_0_.5, f32[16,2,64,128]{3,2,1,0:T(8,128)} %collective-permute-done.10.refs_1_, f32[18,8,4,128]{3,2,1,0:T(4,128)} %copy-done, ...), custom_call_target="tpu_custom_call" | custom-call | bytes 5242880 | tf_op jit(solution)/shard_map/pallas_call | solution.py:318
  84.4 1.3 collective-permute-start.11
  85.7 3.7 %collective-permute-start.12 = (f32[1,40,8,128]{3,2,1,0:T(8,128)}, f32[1,40,8,128]{3,2,1,0:T(8,128)}, u32[]{:S(2)}, u32[]{:S(2)}) collective-permute-start(f32[1,40,8,128]{3,2,1,0:T(8,128)} %get-tuple-element.28), channel_id=1, source_target_pairs={{0,1},{1,2},{2,3},{4,5},{5,6},{6,7},{8,9},{9,10},{10,11},{12,13},{... | collective-permute-start | bytes 491528 | tf_op jit(solution)/shard_map/ppermute | solution.py:41
  89.5 35.1 %shard_map.116 = (f32[16,16,64,128]{3,2,1,0:T(8,128)}, f32[16,2,64,128]{3,2,1,0:T(8,128)}, f32[2,64,128]{2,1,0:T(8,128)}) custom-call(s32[2]{0:T(128)} %pad_add_fusion.place_ref, f32[1,40,128,128]{3,2,1,0:T(8,128)} %get-tuple-element.29.image_ref, f32[1,40,8,128]{3,2,1,0:T(8,128)} %collective-permute-done.14.ahead_ref, ...), custom_call_target="tpu_custom_call" | custom-call | flops 17112760320 | bytes 11141120 | tf_op jit(solution)/shard_map/pallas_call | solution.py:349
  125.1 6.8 %shard_map.113 = (f32[2,40,128,128]{3,2,1,0:T(8,128)}, f32[2,40,8,128]{3,2,1,0:T(8,128)}, f32[2,40,8,128]{3,2,1,0:T(8,128)}) custom-call(s32[2]{0:T(128)} %pad_add_fusion.place_ref, f32[16,16,64,128]{3,2,1,0:T(8,128)} %refs_0_.5, f32[16,4,64,128]{3,2,1,0:T(8,128)} %collective-permute-done.refs_1_, f32[18,8,4,128]{3,2,1,0:T(4,128)} %copy-done, ...), custom_call_target="tpu_custom_call" | custom-call | bytes 10485760 | tf_op jit(solution)/shard_map/pallas_call | solution.py:318
  132.0 1.3 collective-permute-start.7
  133.3 3.3 %collective-permute-start.8 = (f32[2,40,8,128]{3,2,1,0:T(8,128)}, f32[2,40,8,128]{3,2,1,0:T(8,128)S(1)}, u32[]{:S(2)}, u32[]{:S(2)}) collective-permute-start(f32[2,40,8,128]{3,2,1,0:T(8,128)} %get-tuple-element.25), channel_id=1, source_target_pairs={{0,1},{1,2},{2,3},{4,5},{5,6},{6,7},{8,9},{9,10},{10,11},{12,13},{... | collective-permute-start | bytes 983048 | tf_op jit(solution)/shard_map/ppermute | solution.py:41
  136.6 35.3 %shard_map.117 = (f32[16,16,64,128]{3,2,1,0:T(8,128)}, f32[16,2,64,128]{3,2,1,0:T(8,128)}, f32[2,64,128]{2,1,0:T(8,128)}) custom-call(s32[2]{0:T(128)} %pad_add_fusion.place_ref, f32[1,40,128,128]{3,2,1,0:T(8,128)} %get-tuple-element.26.image_ref, f32[1,40,8,128]{3,2,1,0:T(8,128)} %collective-permute-done.11.ahead_ref, ...), custom_call_target="tpu_custom_call", output_to_operand_aliasing={{0}: (11, {})} | custom-call | flops 17112760320 | bytes 11141120 | tf_op jit(solution)/shard_map/pallas_call | solution.py:349
  171.8 1.5 collective-permute-start.18
  174.2 35.2 %shard_map.118 = (f32[16,16,64,128]{3,2,1,0:T(8,128)}, f32[16,2,64,128]{3,2,1,0:T(8,128)}, f32[2,64,128]{2,1,0:T(8,128)}) custom-call(s32[2]{0:T(128)} %pad_add_fusion.place_ref, f32[2,40,128,128]{3,2,1,0:T(8,128)} %get-tuple-element.23.image_ref, f32[2,40,8,128]{3,2,1,0:T(8,128)} %copy-done.15, ...), custom_call_target="tpu_custom_call", output_to_operand_aliasing={{0}: (11, {})} | custom-call | flops 17112760320 | bytes 11141120 | tf_op jit(solution)/shard_map/pallas_call | solution.py:349
  209.9 35.2 %shard_map.119 = (f32[16,16,64,128]{3,2,1,0:T(8,128)}, f32[16,2,64,128]{3,2,1,0:T(8,128)}, f32[2,64,128]{2,1,0:T(8,128)}) custom-call(s32[2]{0:T(128)} %pad_add_fusion.place_ref, f32[2,40,128,128]{3,2,1,0:T(8,128)} %get-tuple-element.23.image_ref, f32[2,40,8,128]{3,2,1,0:T(8,128)} %copy-done.15, ...), custom_call_target="tpu_custom_call", output_to_operand_aliasing={{0}: (11, {})} | custom-call | flops 17112760320 | bytes 11141120 | tf_op jit(solution)/shard_map/pallas_call | solution.py:349
  245.1 1.5 collective-permute-start.16
  246.6 1.0 copy-done.4
  247.6 2.3 shard_map.120.whole_ref
  249.9 1.0 copy-done.5
  250.9 2.3 shard_map.121.whole_ref
  253.2 0.7 pad_maximum_fusion.5
  253.9 1.0 copy-done.6
  255.0 2.3 shard_map.122.whole_ref
  257.2 13.8 %collective-permute-done.16.value_ref = f32[16,2,64,128]{3,2,1,0:T(8,128)} collective-permute-done((f32[16,2,64,128]{3,2,1,0:T(8,128)}, f32[16,2,64,128]{3,2,1,0:T(8,128)}, u32[]{:S(2)}, u32[]{:S(2)}) %collective-permute-start.16) | collective-permute-done | bytes 1048608 | tf_op jit(solution)/shard_map/ppermute | solution.py:46
  271.0 2.3 shard_map.123
  (74 shorter events, 6.6 us)
Async XLA Ops:
  0.6 20.8 %copy-start.14 = (f32[2,2,128]{2,1,0:T(2,128)S(1)}, f32[2,2,128]{2,1,0:T(2,128)}, u32[]{:S(2)}) copy-start(f32[2,2,128]{2,1,0:T(2,128)} %constant.98.clone) | copy-start | bytes 6148
  0.6 22.6 %copy-start.13 = (f32[3]{0:T(128)S(1)}, f32[3]{0:T(128)}, u32[]{:S(2)}) copy-start(f32[3]{0:T(128)} %param.13) | copy-start | bytes 40
  0.7 22.6 %copy-start.11 = (f32[3]{0:T(128)S(1)}, f32[3]{0:T(128)}, u32[]{:S(2)}) copy-start(f32[3]{0:T(128)} %param.14) | copy-start | bytes 40
  0.7 43.1 %copy-start.12 = (f32[3]{0:T(128)S(1)}, f32[3]{0:T(128)}, u32[]{:S(2)}) copy-start(f32[3]{0:T(128)} %sigma_ref.7) | copy-start | bytes 40
  2.5 41.6 %collective-permute-start.1 = (f32[8,64,4]{2,1,0:T(8,128)}, f32[8,64,4]{2,1,0:T(8,128)S(1)}, u32[]{:S(2)}, u32[]{:S(2)}) collective-permute-start(f32[8,64,4]{2,1,0:T(8,128)} %get-tuple-element.58), channel_id=1, source_target_pairs={{1,0},{2,1},{3,2},{5,4},{6,5},{7,6},{9,8},{10,9},{11,10},{13,12},{... | collective-permute-start | bytes 24584 | tf_op jit(solution)/shard_map/ppermute | solution.py:41
  3.8 40.3 %collective-permute-start.2 = (f32[8,64,4]{2,1,0:T(8,128)}, f32[8,64,4]{2,1,0:T(8,128)}, u32[]{:S(2)}, u32[]{:S(2)}) collective-permute-start(f32[8,64,4]{2,1,0:T(8,128)} %get-tuple-element.59), channel_id=1, source_target_pairs={{0,1},{1,2},{2,3},{4,5},{5,6},{6,7},{8,9},{9,10},{10,11},{12,13},{... | collective-permute-start | bytes 24584 | tf_op jit(solution)/shard_map/ppermute | solution.py:41
  10.7 54.7 %collective-permute-start.13 = (f32[16,2,64,128]{3,2,1,0:T(8,128)}, f32[16,2,64,128]{3,2,1,0:T(8,128)}, u32[]{:S(2)}, u32[]{:S(2)}) collective-permute-start(f32[16,2,64,128]{3,2,1,0:T(8,128)} %get-tuple-element.48), channel_id=1, source_target_pairs={{0,16},{16,0},{1,17},{17,1},{2,18},{18,2},{3,19},{19,3},{4,20},{20... | collective-permute-start | bytes 3145736 | tf_op jit(solution)/shard_map/ppermute | solution.py:46
  14.8 46.2 %collective-permute-start.4 = (f32[16,8,4,128]{3,2,1,0:T(4,128)}, f32[16,8,4,128]{3,2,1,0:T(4,128)S(1)}, u32[]{:S(2)}, u32[]{:S(2)}) collective-permute-start(f32[16,8,4,128]{3,2,1,0:T(4,128)} %get-tuple-element.51), channel_id=1, source_target_pairs={{0,20},{4,24},{8,28},{16,4},{20,8},{24,12},{1,21},{5,25},{9,29},{1... | collective-permute-start | bytes 786440 | tf_op jit(solution)/shard_map/ppermute | solution.py:56
  18.9 23.2 %collective-permute-start.9 = (f32[16]{0:T(128)S(1)}, f32[16]{0:T(128)S(1)}, u32[]{:S(2)}, u32[]{:S(2)}) collective-permute-start(f32[16]{0:T(128)S(1)} %get-tuple-element.66), channel_id=1, source_target_pairs={{0,16},{16,0},{1,17},{17,1},{2,18},{18,2},{3,19},{19,3},{4,20},{20... | collective-permute-start | bytes 200 | tf_op jit(solution)/shard_map/ppermute | solution.py:46
  42.1 37.0 %collective-permute-start.10 = (f32[16,2,64,128]{3,2,1,0:T(8,128)}, f32[16,2,64,128]{3,2,1,0:T(8,128)}, u32[]{:S(2)}, u32[]{:S(2)}) collective-permute-start(f32[16,2,64,128]{3,2,1,0:T(8,128)} %get-tuple-element.49), channel_id=1, source_target_pairs={{0,16},{16,0},{1,17},{17,1},{2,18},{18,2},{3,19},{19,3},{4,20},{20... | collective-permute-start | bytes 3145736 | tf_op jit(solution)/shard_map/ppermute | solution.py:46
  45.4 10.1 %collective-permute-start.3 = (f32[18,8,4,128]{3,2,1,0:T(4,128)S(1)}, f32[18,8,4,128]{3,2,1,0:T(4,128)S(1)}, u32[]{:S(2)}, u32[]{:S(2)}) collective-permute-start(f32[18,8,4,128]{3,2,1,0:T(4,128)S(1)} %get-tuple-element.57), channel_id=1, source_target_pairs={{0,4},{4,8},{8,12},{16,20},{20,24},{24,28},{1,5},{5,9},{9,13},{17,... | collective-permute-start | bytes 884744 | tf_op jit(solution)/shard_map/ppermute | solution.py:56
  48.9 9.9 %collective-permute-start.5 = (f32[18,8,4,128]{3,2,1,0:T(4,128)S(1)}, f32[18,8,4,128]{3,2,1,0:T(4,128)S(1)}, u32[]{:S(2)}, u32[]{:S(2)}) collective-permute-start(f32[18,8,4,128]{3,2,1,0:T(4,128)S(1)} %get-tuple-element.56), channel_id=1, source_target_pairs={{4,0},{8,4},{12,8},{20,16},{24,20},{28,24},{5,1},{9,5},{13,9},{21,... | collective-permute-start | bytes 884744 | tf_op jit(solution)/shard_map/ppermute | solution.py:56
  55.5 9.9 %copy-start = (f32[18,8,4,128]{3,2,1,0:T(4,128)}, f32[18,8,4,128]{3,2,1,0:T(4,128)S(1)}, u32[]{:S(2)}) copy-start(f32[18,8,4,128]{3,2,1,0:T(4,128)S(1)} %collective-permute-done.3.refs_2_) | copy-start | bytes 884740
  55.5 9.9 %collective-permute-start.6 = (f32[16,8,4,128]{3,2,1,0:T(4,128)}, f32[16,8,4,128]{3,2,1,0:T(4,128)S(1)}, u32[]{:S(2)}, u32[]{:S(2)}) collective-permute-start(f32[16,8,4,128]{3,2,1,0:T(4,128)} %get-tuple-element.50), channel_id=1, source_target_pairs={{4,16},{8,20},{12,24},{20,0},{24,4},{28,8},{5,17},{9,21},{13,25},{... | collective-permute-start | bytes 786440 | tf_op jit(solution)/shard_map/ppermute | solution.py:56
  58.7 6.7 %copy-start.1 = (f32[18,8,4,128]{3,2,1,0:T(4,128)}, f32[18,8,4,128]{3,2,1,0:T(4,128)S(1)}, u32[]{:S(2)}) copy-start(f32[18,8,4,128]{3,2,1,0:T(4,128)S(1)} %collective-permute-done.5.refs_4_) | copy-start | bytes 884740
  58.7 66.4 %collective-permute-start = (f32[16,4,64,128]{3,2,1,0:T(8,128)S(1)}, f32[16,4,64,128]{3,2,1,0:T(8,128)}, u32[]{:S(2)}, u32[]{:S(2)}) collective-permute-start(f32[16,4,64,128]{3,2,1,0:T(8,128)S(1)} %constant_dynamic-slice_fusion.7), channel_id=1, source_target_pairs={{0,16},{16,0},{1,17},{17,1},{2,18},{18,2},{3,19},{19,3},{4,20},{20... | collective-permute-start | bytes 6291464 | tf_op jit(solution)/shard_map/ppermute | solution.py:46
  61.0 4.4 %copy-start.2 = (f32[16,8,4,128]{3,2,1,0:T(4,128)}, f32[16,8,4,128]{3,2,1,0:T(4,128)S(1)}, u32[]{:S(2)}) copy-start(f32[16,8,4,128]{3,2,1,0:T(4,128)S(1)} %collective-permute-done.4.refs_3_) | copy-start | bytes 786436
  65.4 0.7 copy-start.3
  71.3 18.2 %collective-permute-start.14 = (f32[1,40,8,128]{3,2,1,0:T(8,128)}, f32[1,40,8,128]{3,2,1,0:T(8,128)}, u32[]{:S(2)}, u32[]{:S(2)}) collective-permute-start(f32[1,40,8,128]{3,2,1,0:T(8,128)} %get-tuple-element.30), channel_id=1, source_target_pairs={{1,0},{2,1},{3,2},{5,4},{6,5},{7,6},{9,8},{10,9},{11,10},{13,12},{... | collective-permute-start | bytes 491528 | tf_op jit(solution)/shard_map/ppermute | solution.py:41
  72.6 16.9 %collective-permute-start.15 = (f32[1,40,8,128]{3,2,1,0:T(8,128)}, f32[1,40,8,128]{3,2,1,0:T(8,128)}, u32[]{:S(2)}, u32[]{:S(2)}) collective-permute-start(f32[1,40,8,128]{3,2,1,0:T(8,128)} %get-tuple-element.31), channel_id=1, source_target_pairs={{0,1},{1,2},{2,3},{4,5},{5,6},{6,7},{8,9},{9,10},{10,11},{12,13},{... | collective-permute-start | bytes 491528 | tf_op jit(solution)/shard_map/ppermute | solution.py:41
  84.4 52.1 %collective-permute-start.11 = (f32[1,40,8,128]{3,2,1,0:T(8,128)}, f32[1,40,8,128]{3,2,1,0:T(8,128)}, u32[]{:S(2)}, u32[]{:S(2)}) collective-permute-start(f32[1,40,8,128]{3,2,1,0:T(8,128)} %get-tuple-element.27), channel_id=1, source_target_pairs={{1,0},{2,1},{3,2},{5,4},{6,5},{7,6},{9,8},{10,9},{11,10},{13,12},{... | collective-permute-start | bytes 491528 | tf_op jit(solution)/shard_map/ppermute | solution.py:41
  85.7 50.8 %collective-permute-start.12 = (f32[1,40,8,128]{3,2,1,0:T(8,128)}, f32[1,40,8,128]{3,2,1,0:T(8,128)}, u32[]{:S(2)}, u32[]{:S(2)}) collective-permute-start(f32[1,40,8,128]{3,2,1,0:T(8,128)} %get-tuple-element.28), channel_id=1, source_target_pairs={{0,1},{1,2},{2,3},{4,5},{5,6},{6,7},{8,9},{9,10},{10,11},{12,13},{... | collective-permute-start | bytes 491528 | tf_op jit(solution)/shard_map/ppermute | solution.py:41
  124.6 122.0 %collective-permute-start.19 = (f32[16,2,64,128]{3,2,1,0:T(8,128)}, f32[16,2,64,128]{3,2,1,0:T(8,128)S(1)}, u32[]{:S(2)}, u32[]{:S(2)}) collective-permute-start(f32[16,2,64,128]{3,2,1,0:T(8,128)} %get-tuple-element.38), channel_id=1, source_target_pairs={{0,16},{16,0},{1,17},{17,1},{2,18},{18,2},{3,19},{19,3},{4,20},{20... | collective-permute-start | bytes 3145736 | tf_op jit(solution)/shard_map/ppermute | solution.py:46
  132.0 41.4 %collective-permute-start.7 = (f32[2,40,8,128]{3,2,1,0:T(8,128)}, f32[2,40,8,128]{3,2,1,0:T(8,128)S(1)}, u32[]{:S(2)}, u32[]{:S(2)}) collective-permute-start(f32[2,40,8,128]{3,2,1,0:T(8,128)} %get-tuple-element.24), channel_id=1, source_target_pairs={{1,0},{2,1},{3,2},{5,4},{6,5},{7,6},{9,8},{10,9},{11,10},{13,12},{... | collective-permute-start | bytes 983048 | tf_op jit(solution)/shard_map/ppermute | solution.py:41
  133.3 40.1 %collective-permute-start.8 = (f32[2,40,8,128]{3,2,1,0:T(8,128)}, f32[2,40,8,128]{3,2,1,0:T(8,128)S(1)}, u32[]{:S(2)}, u32[]{:S(2)}) collective-permute-start(f32[2,40,8,128]{3,2,1,0:T(8,128)} %get-tuple-element.25), channel_id=1, source_target_pairs={{0,1},{1,2},{2,3},{4,5},{5,6},{6,7},{8,9},{9,10},{10,11},{12,13},{... | collective-permute-start | bytes 983048 | tf_op jit(solution)/shard_map/ppermute | solution.py:41
  171.8 78.0 %collective-permute-start.18 = (f32[16,2,64,128]{3,2,1,0:T(8,128)}, f32[16,2,64,128]{3,2,1,0:T(8,128)S(1)}, u32[]{:S(2)}, u32[]{:S(2)}) collective-permute-start(f32[16,2,64,128]{3,2,1,0:T(8,128)} %get-tuple-element.37), channel_id=1, source_target_pairs={{0,16},{16,0},{1,17},{17,1},{2,18},{18,2},{3,19},{19,3},{4,20},{20... | collective-permute-start | bytes 3145736 | tf_op jit(solution)/shard_map/ppermute | solution.py:46
  173.3 0.7 copy-start.15
  173.4 0.8 copy-start.16
  209.4 44.5 %collective-permute-start.17 = (f32[16,2,64,128]{3,2,1,0:T(8,128)}, f32[16,2,64,128]{3,2,1,0:T(8,128)S(1)}, u32[]{:S(2)}, u32[]{:S(2)}) collective-permute-start(f32[16,2,64,128]{3,2,1,0:T(8,128)} %get-tuple-element.36), channel_id=1, source_target_pairs={{0,16},{16,0},{1,17},{17,1},{2,18},{18,2},{3,19},{19,3},{4,20},{20... | collective-permute-start | bytes 3145736 | tf_op jit(solution)/shard_map/ppermute | solution.py:46
  245.1 25.9 %collective-permute-start.16 = (f32[16,2,64,128]{3,2,1,0:T(8,128)}, f32[16,2,64,128]{3,2,1,0:T(8,128)}, u32[]{:S(2)}, u32[]{:S(2)}) collective-permute-start(f32[16,2,64,128]{3,2,1,0:T(8,128)} %get-tuple-element.35), channel_id=1, source_target_pairs={{0,16},{16,0},{1,17},{17,1},{2,18},{18,2},{3,19},{19,3},{4,20},{20... | collective-permute-start | bytes 3145736 | tf_op jit(solution)/shard_map/ppermute | solution.py:46
  246.6 1.0 copy-start.4
  249.9 3.3 %copy-start.7 = (f32[2,64,128]{2,1,0:T(8,128)S(1)}, f32[2,64,128]{2,1,0:T(8,128)}, u32[]{:S(2)}) copy-start(f32[2,64,128]{2,1,0:T(8,128)} %get-tuple-element.40) | copy-start | bytes 196612
  249.9 3.3 %copy-start.8 = (f32[2,64,128]{2,1,0:T(8,128)S(1)}, f32[2,64,128]{2,1,0:T(8,128)}, u32[]{:S(2)}) copy-start(f32[2,64,128]{2,1,0:T(8,128)} %get-tuple-element.41) | copy-start | bytes 196612
  249.9 3.3 %copy-start.9 = (f32[2,64,128]{2,1,0:T(8,128)S(1)}, f32[2,64,128]{2,1,0:T(8,128)}, u32[]{:S(2)}) copy-start(f32[2,64,128]{2,1,0:T(8,128)} %get-tuple-element.42) | copy-start | bytes 196612
  249.9 3.3 %copy-start.10 = (f32[2,64,128]{2,1,0:T(8,128)S(1)}, f32[2,64,128]{2,1,0:T(8,128)}, u32[]{:S(2)}) copy-start(f32[2,64,128]{2,1,0:T(8,128)} %get-tuple-element.43) | copy-start | bytes 196612
  249.9 1.0 copy-start.5
  253.9 1.0 copy-start.6

commit v4 on v3

--- a/solution.py
+++ b/solution.py
@@ -86,12 +86,12 @@
 
 def solve_kernel(
     groups, own, layers, parts, rows, columns,
-    chained, place_ref, image_ref, ahead_ref, behind_ref, code_ref, table_ref, fwd_ref, inv_ref, weight_ref, material_ref, sigma_ref,
+    chained, chunk, place_ref, image_ref, ahead_ref, behind_ref, code_ref, table_ref, fwd_ref, inv_ref, weight_ref, material_ref, sigma_ref,
     *refs,
 ):
     refs = refs[chained:]
     outs, heat_ref = refs[:groups], refs[groups]
-    pot, nu_all, nu_sat, gain, turn_gain, feed, samples_0, samples_1, products_0, products_1, last_row, back_x = refs[groups + 1 :]
+    pot, nu_all, nu_sat, gain, turn_gain, feed, samples_0, samples_1, products_0, products_1, last_row, back_x, arrived = refs[groups + 1 :]
     samples, products = (samples_0, samples_1), (products_0, products_1)
     span = rows // parts
     total = span + 2 * RIM
@@ -102,17 +102,25 @@
         chosen = jnp.concatenate([jnp.where(code == m, 1.0, 0.0) for m in (1.0, 2.0, 3.0)] * 3, axis=0)
         picked = lax.dot_general(
             chosen.astype(jnp.bfloat16), table_ref[...], (((0,), (0,)), ((), ())), preferred_element_type=jnp.float32)
-        edge = lax.broadcasted_iota(jnp.int32, (8, LANES), 0) < RIM
         for r in range(BLOCK):
             x = block * BLOCK + r
             for k, ref in enumerate((nu_all, nu_sat, gain, turn_gain, feed)):
                 ref[x] = picked[r * wide : (r + 1) * wide, k * LANES : (k + 1) * LANES]
-            pot[x, 0:columns, :] = image_ref[0, x]
-            pot[x, columns:wide, :] = jnp.where(edge, ahead_ref[0, x], behind_ref[0, x])
-            pot[x, wide : wide + 8, :] = image_ref[0, x, 0:8, :]
         return carry
 
+    def frame(x, carry):
+        edge = lax.broadcasted_iota(jnp.int32, (8, LANES), 0) < RIM
+        pot[x, columns:wide, :] = jnp.where(edge, ahead_ref[0, x], behind_ref[0, x])
+        pot[x, wide : wide + 8, :] = pot[x, 0:8, :]
+        return carry
+
+    fetch = pltpu.make_async_copy(
+        image_ref.at[chunk], pot.at[pl.ds(0, total), pl.ds(0, columns), :], arrived)
+    fetch.start()
+
     lax.fori_loop(0, total // BLOCK, load, 0, unroll=2)
+    fetch.wait()
+    lax.fori_loop(0, total, frame, 0, unroll=8)
     for k in range(SPARE):
         pot[total + k] = jnp.zeros((wide + 8, LANES), jnp.float32)
     tiles = [(8 * t, 16 * t) for t in range(wide // 8)]
@@ -347,12 +355,12 @@
         part = lambda i, s: (at, 0, 0, 0)
         whole = jax.ShapeDtypeStruct(potential_start.shape, jnp.float32)
         return pl.pallas_call(
-            functools.partial(solve_kernel, groups, own, layers, parts, rows, columns, int(chained)),
+            functools.partial(solve_kernel, groups, own, layers, parts, rows, columns, int(chained), at),
             grid_spec=pltpu.PrefetchScalarGridSpec(
                 num_scalar_prefetch=1,
                 grid=(1,),
                 in_specs=[
-                    pl.BlockSpec((1, total, columns, LANES), part),
+                    pl.BlockSpec(memory_space=pl.ANY),
                     pl.BlockSpec((1, total, 8, LANES), part),
                     pl.BlockSpec((1, total, 8, LANES), part),
                     pl.BlockSpec((1, total // BLOCK, 8, BLOCK * wide), lambda i, s: (k, 0, 0, 0)),
@@ -370,7 +378,7 @@
                 + [pltpu.VMEM((total + SPARE, wide, LANES), jnp.float32)] * 5
                 + [pltpu.VMEM((2 * STEP * wide, 2 * LANES), jnp.float32)] * 2
                 + [pltpu.VMEM((2 * STEP * wide, 4 * LANES), jnp.bfloat16)] * 2
-                + [pltpu.VMEM((wide, LANES), jnp.float32), pltpu.VMEM((wide + 8, LANES), jnp.float32)],
+                + [pltpu.VMEM((wide, LANES), jnp.float32), pltpu.VMEM((wide + 8, LANES), jnp.float32), pltpu.SemaphoreType.DMA(())],
             ),
             out_shape=[whole]
             + [jax.ShapeDtypeStruct((own, layers, rows, columns), jnp.float32)] * (groups - 1)

time: 276 us -> 273 us (0.989)
  Pallas kernels: 167 us -> 164 us
    pallas_call x4, Pallas kernels: 141 us -> 138 us  [solve(): pl.pallas_call(functools.partial(solve_kernel, groups, own, layers, parts...]
where the time goes in v4:
time: 273 us; the launch traced here: 270 us
  Pallas kernels  164 us (60%)
  waiting for transfers between devices  41 us (15%)
  starting transfers between devices  40.6 us (15%)
  local copies, waits for them, and re-layouts  16.3 us (6%)
  other arithmetic  7.34 us (3%)
    pallas_call x4, Pallas kernels, solve(): pl.pallas_call(functools.partial(solve_kernel, groups, own, layers, parts...  138 us
    ppermute x8, waiting for transfers between devices, turned(): lax.ppermute(value, 'harm', [(i, (i + by) % length) for i in range(length)])  32.1 us
    ppermute x8, starting transfers between devices, shifted(): lax.ppermute(value, axis, [(i, i + by) for i in range(length) if 0 <= i +...  19.6 us
    pallas_call x3, Pallas kernels, gather(): pl.pallas_call(functools.partial(gather_kernel, groups, own, layers, part...  17.3 us
    ppermute x4, starting transfers between devices, turned_and_shifted(): return lax.ppermute(value, ('harm', 'sx'), pairs)  11.5 us
    ppermute x8, starting transfers between devices, turned(): lax.ppermute(value, 'harm', [(i, (i + by) % length) for i in range(length)])  9.53 us
    pallas_call x4, Pallas kernels, place_into(): pl.pallas_call(place_kernel, grid_spec=pltpu.PrefetchScalarGridSpec(num_s...  9.05 us
    ppermute x4, waiting for transfers between devices, turned_and_shifted(): return lax.ppermute(value, ('harm', 'sx'), pairs)  8.9 us
  transfers between devices with their start and end apart: 20, of which 5 were waited for; matrix products, arithmetic and copies ran while one was open for 6% of the time, Pallas kernels for 60%

profile of v4, /device:TPU:16, one launch (start us, length us, event | category | flops | bytes accessed | tf_op | source)
XLA Modules:
  0.0 270.2 jit_solution(11204624619322857198)
XLA Ops:
  0.7 1.0 add_convert_fusion
  1.7 0.9 fusion.8
  2.5 1.3 collective-permute-start.1
  3.8 3.7 %collective-permute-start.2 = (f32[8,64,4]{2,1,0:T(8,128)}, f32[8,64,4]{2,1,0:T(8,128)}, u32[]{:S(2)}, u32[]{:S(2)}) collective-permute-start(f32[8,64,4]{2,1,0:T(8,128)} %get-tuple-element.59), channel_id=1, source_target_pairs={{0,1},{1,2},{2,3},{4,5},{5,6},{6,7},{8,9},{9,10},{10,11},{12,13},{... | collective-permute-start | bytes 24584 | tf_op jit(solution)/shard_map/ppermute | solution.py:41
  7.6 3.1 %constant_dynamic-slice_fusion.2 = (f32[16,2,64,128]{3,2,1,0:T(8,128)}, f32[16,2,64,128]{3,2,1,0:T(8,128)}) fusion(f32[16,16,64,128]{3,2,1,0:T(8,128)} %refs_0_.5, s32[]{:T(128)S(6)} %select_n.79, s32[]{:T(128)S(6)} %select_n.86), kind=kLoop, calls=%fused_computation.29 | loop fusion | bytes 4194312 | tf_op jit(solution)/shard_map/dynamic_slice | solution.py:295
  10.7 1.5 collective-permute-start.13
  12.2 2.6 constant_dynamic-slice_fusion.5
  14.8 3.4 %collective-permute-start.4 = (f32[16,8,4,128]{3,2,1,0:T(4,128)}, f32[16,8,4,128]{3,2,1,0:T(4,128)S(1)}, u32[]{:S(2)}, u32[]{:S(2)}) collective-permute-start(f32[16,8,4,128]{3,2,1,0:T(4,128)} %get-tuple-element.51), channel_id=1, source_target_pairs={{0,20},{4,24},{8,28},{16,4},{20,8},{24,12},{1,21},{5,25},{9,29},{1... | collective-permute-start | bytes 786440 | tf_op jit(solution)/shard_map/ppermute | solution.py:56
  18.9 1.5 collective-permute-start.9
  20.4 1.0 fusion.9
  21.5 1.7 constant_dynamic-slice_fusion.7
  23.9 18.3 %collective-permute-done.9 = f32[16]{0:T(128)S(1)} collective-permute-done((f32[16]{0:T(128)S(1)}, f32[16]{0:T(128)S(1)}, u32[]{:S(2)}, u32[]{:S(2)}) %collective-permute-start.9) | collective-permute-done | bytes 96 | tf_op jit(solution)/shard_map/ppermute | solution.py:46
  42.1 1.5 collective-permute-start.10
  44.1 1.1 fusion.5
  45.4 3.5 %collective-permute-start.3 = (f32[18,8,4,128]{3,2,1,0:T(4,128)S(1)}, f32[18,8,4,128]{3,2,1,0:T(4,128)S(1)}, u32[]{:S(2)}, u32[]{:S(2)}) collective-permute-start(f32[18,8,4,128]{3,2,1,0:T(4,128)S(1)} %get-tuple-element.57), channel_id=1, source_target_pairs={{0,4},{4,8},{8,12},{16,20},{20,24},{24,28},{1,5},{5,9},{9,13},{17,... | collective-permute-start | bytes 884744 | tf_op jit(solution)/shard_map/ppermute | solution.py:56
  48.9 2.4 collective-permute-start.5
  51.9 3.6 %collective-permute-done.3.refs_2_ = f32[18,8,4,128]{3,2,1,0:T(4,128)S(1)} collective-permute-done((f32[18,8,4,128]{3,2,1,0:T(4,128)S(1)}, f32[18,8,4,128]{3,2,1,0:T(4,128)S(1)}, u32[]{:S(2)}, u32[]{:S(2)}) %collective-permute-start.3) | collective-permute-done | bytes 294944 | tf_op jit(solution)/shard_map/ppermute | solution.py:56
  55.5 2.3 collective-permute-start.6
  57.8 0.9 collective-permute-done.5.refs_4_
  59.5 0.7 slice_bitcast_fusion
  60.2 0.7 slice_bitcast_fusion.1
  61.0 4.4 %collective-permute-done.6.refs_5_ = f32[16,8,4,128]{3,2,1,0:T(4,128)S(1)} collective-permute-done((f32[16,8,4,128]{3,2,1,0:T(4,128)}, f32[16,8,4,128]{3,2,1,0:T(4,128)S(1)}, u32[]{:S(2)}, u32[]{:S(2)}) %collective-permute-start.6) | collective-permute-done | bytes 262176 | tf_op jit(solution)/shard_map/ppermute | solution.py:56
  66.1 5.2 %shard_map.115 = (f32[1,40,128,128]{3,2,1,0:T(8,128)}, f32[1,40,8,128]{3,2,1,0:T(8,128)}, f32[1,40,8,128]{3,2,1,0:T(8,128)}) custom-call(s32[2]{0:T(128)} %pad_add_fusion.place_ref, f32[16,16,64,128]{3,2,1,0:T(8,128)} %refs_0_.5, f32[16,2,64,128]{3,2,1,0:T(8,128)} %collective-permute-done.13.refs_1_, f32[18,8,4,128]{3,2,1,0:T(4,128)} %copy-done, ...), custom_call_target="tpu_custom_call" | custom-call | bytes 5242880 | tf_op jit(solution)/shard_map/pallas_call | solution.py:326
  71.3 1.3 collective-permute-start.14
  72.6 3.7 %collective-permute-start.15 = (f32[1,40,8,128]{3,2,1,0:T(8,128)}, f32[1,40,8,128]{3,2,1,0:T(8,128)}, u32[]{:S(2)}, u32[]{:S(2)}) collective-permute-start(f32[1,40,8,128]{3,2,1,0:T(8,128)} %get-tuple-element.31), channel_id=1, source_target_pairs={{0,1},{1,2},{2,3},{4,5},{5,6},{6,7},{8,9},{9,10},{10,11},{12,13},{... | collective-permute-start | bytes 491528 | tf_op jit(solution)/shard_map/ppermute | solution.py:41
  76.3 1.2 fusion.1
  78.2 1.0 pad.9.code_ref
  79.2 5.3 %shard_map.114 = (f32[1,40,128,128]{3,2,1,0:T(8,128)}, f32[1,40,8,128]{3,2,1,0:T(8,128)}, f32[1,40,8,128]{3,2,1,0:T(8,128)}) custom-call(s32[2]{0:T(128)} %pad_add_fusion.place_ref, f32[16,16,64,128]{3,2,1,0:T(8,128)} %refs_0_.5, f32[16,2,64,128]{3,2,1,0:T(8,128)} %collective-permute-done.10.refs_1_, f32[18,8,4,128]{3,2,1,0:T(4,128)} %copy-done, ...), custom_call_target="tpu_custom_call" | custom-call | bytes 5242880 | tf_op jit(solution)/shard_map/pallas_call | solution.py:326
  84.4 1.3 collective-permute-start.11
  85.7 3.7 %collective-permute-start.12 = (f32[1,40,8,128]{3,2,1,0:T(8,128)}, f32[1,40,8,128]{3,2,1,0:T(8,128)}, u32[]{:S(2)}, u32[]{:S(2)}) collective-permute-start(f32[1,40,8,128]{3,2,1,0:T(8,128)} %get-tuple-element.28), channel_id=1, source_target_pairs={{0,1},{1,2},{2,3},{4,5},{5,6},{6,7},{8,9},{9,10},{10,11},{12,13},{... | collective-permute-start | bytes 491528 | tf_op jit(solution)/shard_map/ppermute | solution.py:41
  89.5 34.3 %shard_map.116 = (f32[16,16,64,128]{3,2,1,0:T(8,128)}, f32[16,2,64,128]{3,2,1,0:T(8,128)}, f32[2,64,128]{2,1,0:T(8,128)}) custom-call(s32[2]{0:T(128)} %pad_add_fusion.place_ref, f32[1,40,128,128]{3,2,1,0:T(8,128)} %get-tuple-element.29.image_ref, f32[1,40,8,128]{3,2,1,0:T(8,128)} %collective-permute-done.14.ahead_ref, ...), custom_call_target="tpu_custom_call" | custom-call | flops 17112760320 | bytes 11141120 | tf_op jit(solution)/shard_map/pallas_call | solution.py:357
  124.4 6.8 %shard_map.113 = (f32[2,40,128,128]{3,2,1,0:T(8,128)}, f32[2,40,8,128]{3,2,1,0:T(8,128)}, f32[2,40,8,128]{3,2,1,0:T(8,128)}) custom-call(s32[2]{0:T(128)} %pad_add_fusion.place_ref, f32[16,16,64,128]{3,2,1,0:T(8,128)} %refs_0_.5, f32[16,4,64,128]{3,2,1,0:T(8,128)} %collective-permute-done.refs_1_, f32[18,8,4,128]{3,2,1,0:T(4,128)} %copy-done, ...), custom_call_target="tpu_custom_call" | custom-call | bytes 10485760 | tf_op jit(solution)/shard_map/pallas_call | solution.py:326
  131.2 1.3 collective-permute-start.7
  132.5 3.3 %collective-permute-start.8 = (f32[2,40,8,128]{3,2,1,0:T(8,128)}, f32[2,40,8,128]{3,2,1,0:T(8,128)S(1)}, u32[]{:S(2)}, u32[]{:S(2)}) collective-permute-start(f32[2,40,8,128]{3,2,1,0:T(8,128)} %get-tuple-element.25), channel_id=1, source_target_pairs={{0,1},{1,2},{2,3},{4,5},{5,6},{6,7},{8,9},{9,10},{10,11},{12,13},{... | collective-permute-start | bytes 983048 | tf_op jit(solution)/shard_map/ppermute | solution.py:41
  135.8 34.5 %shard_map.117 = (f32[16,16,64,128]{3,2,1,0:T(8,128)}, f32[16,2,64,128]{3,2,1,0:T(8,128)}, f32[2,64,128]{2,1,0:T(8,128)}) custom-call(s32[2]{0:T(128)} %pad_add_fusion.place_ref, f32[1,40,128,128]{3,2,1,0:T(8,128)} %get-tuple-element.26.image_ref, f32[1,40,8,128]{3,2,1,0:T(8,128)} %collective-permute-done.11.ahead_ref, ...), custom_call_target="tpu_custom_call", output_to_operand_aliasing={{0}: (11, {})} | custom-call | flops 17112760320 | bytes 11141120 | tf_op jit(solution)/shard_map/pallas_call | solution.py:357
  170.3 1.5 collective-permute-start.18
  172.7 34.4 %shard_map.118 = (f32[16,16,64,128]{3,2,1,0:T(8,128)}, f32[16,2,64,128]{3,2,1,0:T(8,128)}, f32[2,64,128]{2,1,0:T(8,128)}) custom-call(s32[2]{0:T(128)} %pad_add_fusion.place_ref, f32[2,40,128,128]{3,2,1,0:T(8,128)} %get-tuple-element.23.image_ref, f32[2,40,8,128]{3,2,1,0:T(8,128)} %copy-done.15, ...), custom_call_target="tpu_custom_call", output_to_operand_aliasing={{0}: (11, {})} | custom-call | flops 17112760320 | bytes 11141120 | tf_op jit(solution)/shard_map/pallas_call | solution.py:357
  207.7 34.4 %shard_map.119 = (f32[16,16,64,128]{3,2,1,0:T(8,128)}, f32[16,2,64,128]{3,2,1,0:T(8,128)}, f32[2,64,128]{2,1,0:T(8,128)}) custom-call(s32[2]{0:T(128)} %pad_add_fusion.place_ref, f32[2,40,128,128]{3,2,1,0:T(8,128)} %get-tuple-element.23.image_ref, f32[2,40,8,128]{3,2,1,0:T(8,128)} %copy-done.15, ...), custom_call_target="tpu_custom_call", output_to_operand_aliasing={{0}: (11, {})} | custom-call | flops 17112760320 | bytes 11141120 | tf_op jit(solution)/shard_map/pallas_call | solution.py:357
  242.0 1.5 collective-permute-start.16
  243.6 1.0 copy-done.4
  244.6 2.3 shard_map.120.whole_ref
  246.9 1.0 copy-done.5
  247.9 2.3 shard_map.121.whole_ref
  250.2 0.7 pad_maximum_fusion.5
  250.9 1.0 copy-done.6
  251.9 2.3 shard_map.122.whole_ref
  254.2 13.8 %collective-permute-done.16.value_ref = f32[16,2,64,128]{3,2,1,0:T(8,128)} collective-permute-done((f32[16,2,64,128]{3,2,1,0:T(8,128)}, f32[16,2,64,128]{3,2,1,0:T(8,128)}, u32[]{:S(2)}, u32[]{:S(2)}) %collective-permute-start.16) | collective-permute-done | bytes 1048608 | tf_op jit(solution)/shard_map/ppermute | solution.py:46
  267.9 2.3 shard_map.123
  (74 shorter events, 6.8 us)
Async XLA Ops:
  0.6 20.8 %copy-start.14 = (f32[2,2,128]{2,1,0:T(2,128)S(1)}, f32[2,2,128]{2,1,0:T(2,128)}, u32[]{:S(2)}) copy-start(f32[2,2,128]{2,1,0:T(2,128)} %constant.98.clone) | copy-start | bytes 6148
  0.6 22.6 %copy-start.13 = (f32[3]{0:T(128)S(1)}, f32[3]{0:T(128)}, u32[]{:S(2)}) copy-start(f32[3]{0:T(128)} %param.13) | copy-start | bytes 40
  0.7 22.6 %copy-start.11 = (f32[3]{0:T(128)S(1)}, f32[3]{0:T(128)}, u32[]{:S(2)}) copy-start(f32[3]{0:T(128)} %param.14) | copy-start | bytes 40
  0.7 43.1 %copy-start.12 = (f32[3]{0:T(128)S(1)}, f32[3]{0:T(128)}, u32[]{:S(2)}) copy-start(f32[3]{0:T(128)} %sigma_ref.7) | copy-start | bytes 40
  2.5 41.6 %collective-permute-start.1 = (f32[8,64,4]{2,1,0:T(8,128)}, f32[8,64,4]{2,1,0:T(8,128)S(1)}, u32[]{:S(2)}, u32[]{:S(2)}) collective-permute-start(f32[8,64,4]{2,1,0:T(8,128)} %get-tuple-element.58), channel_id=1, source_target_pairs={{1,0},{2,1},{3,2},{5,4},{6,5},{7,6},{9,8},{10,9},{11,10},{13,12},{... | collective-permute-start | bytes 24584 | tf_op jit(solution)/shard_map/ppermute | solution.py:41
  3.8 40.3 %collective-permute-start.2 = (f32[8,64,4]{2,1,0:T(8,128)}, f32[8,64,4]{2,1,0:T(8,128)}, u32[]{:S(2)}, u32[]{:S(2)}) collective-permute-start(f32[8,64,4]{2,1,0:T(8,128)} %get-tuple-element.59), channel_id=1, source_target_pairs={{0,1},{1,2},{2,3},{4,5},{5,6},{6,7},{8,9},{9,10},{10,11},{12,13},{... | collective-permute-start | bytes 24584 | tf_op jit(solution)/shard_map/ppermute | solution.py:41
  10.7 54.7 %collective-permute-start.13 = (f32[16,2,64,128]{3,2,1,0:T(8,128)}, f32[16,2,64,128]{3,2,1,0:T(8,128)}, u32[]{:S(2)}, u32[]{:S(2)}) collective-permute-start(f32[16,2,64,128]{3,2,1,0:T(8,128)} %get-tuple-element.48), channel_id=1, source_target_pairs={{0,16},{16,0},{1,17},{17,1},{2,18},{18,2},{3,19},{19,3},{4,20},{20... | collective-permute-start | bytes 3145736 | tf_op jit(solution)/shard_map/ppermute | solution.py:46
  14.8 46.2 %collective-permute-start.4 = (f32[16,8,4,128]{3,2,1,0:T(4,128)}, f32[16,8,4,128]{3,2,1,0:T(4,128)S(1)}, u32[]{:S(2)}, u32[]{:S(2)}) collective-permute-start(f32[16,8,4,128]{3,2,1,0:T(4,128)} %get-tuple-element.51), channel_id=1, source_target_pairs={{0,20},{4,24},{8,28},{16,4},{20,8},{24,12},{1,21},{5,25},{9,29},{1... | collective-permute-start | bytes 786440 | tf_op jit(solution)/shard_map/ppermute | solution.py:56
  18.9 23.2 %collective-permute-start.9 = (f32[16]{0:T(128)S(1)}, f32[16]{0:T(128)S(1)}, u32[]{:S(2)}, u32[]{:S(2)}) collective-permute-start(f32[16]{0:T(128)S(1)} %get-tuple-element.66), channel_id=1, source_target_pairs={{0,16},{16,0},{1,17},{17,1},{2,18},{18,2},{3,19},{19,3},{4,20},{20... | collective-permute-start | bytes 200 | tf_op jit(solution)/shard_map/ppermute | solution.py:46
  42.1 37.0 %collective-permute-start.10 = (f32[16,2,64,128]{3,2,1,0:T(8,128)}, f32[16,2,64,128]{3,2,1,0:T(8,128)}, u32[]{:S(2)}, u32[]{:S(2)}) collective-permute-start(f32[16,2,64,128]{3,2,1,0:T(8,128)} %get-tuple-element.49), channel_id=1, source_target_pairs={{0,16},{16,0},{1,17},{17,1},{2,18},{18,2},{3,19},{19,3},{4,20},{20... | collective-permute-start | bytes 3145736 | tf_op jit(solution)/shard_map/ppermute | solution.py:46
  45.4 10.1 %collective-permute-start.3 = (f32[18,8,4,128]{3,2,1,0:T(4,128)S(1)}, f32[18,8,4,128]{3,2,1,0:T(4,128)S(1)}, u32[]{:S(2)}, u32[]{:S(2)}) collective-permute-start(f32[18,8,4,128]{3,2,1,0:T(4,128)S(1)} %get-tuple-element.57), channel_id=1, source_target_pairs={{0,4},{4,8},{8,12},{16,20},{20,24},{24,28},{1,5},{5,9},{9,13},{17,... | collective-permute-start | bytes 884744 | tf_op jit(solution)/shard_map/ppermute | solution.py:56
  48.9 9.9 %collective-permute-start.5 = (f32[18,8,4,128]{3,2,1,0:T(4,128)S(1)}, f32[18,8,4,128]{3,2,1,0:T(4,128)S(1)}, u32[]{:S(2)}, u32[]{:S(2)}) collective-permute-start(f32[18,8,4,128]{3,2,1,0:T(4,128)S(1)} %get-tuple-element.56), channel_id=1, source_target_pairs={{4,0},{8,4},{12,8},{20,16},{24,20},{28,24},{5,1},{9,5},{13,9},{21,... | collective-permute-start | bytes 884744 | tf_op jit(solution)/shard_map/ppermute | solution.py:56
  55.5 9.9 %copy-start = (f32[18,8,4,128]{3,2,1,0:T(4,128)}, f32[18,8,4,128]{3,2,1,0:T(4,128)S(1)}, u32[]{:S(2)}) copy-start(f32[18,8,4,128]{3,2,1,0:T(4,128)S(1)} %collective-permute-done.3.refs_2_) | copy-start | bytes 884740
  55.5 9.9 %collective-permute-start.6 = (f32[16,8,4,128]{3,2,1,0:T(4,128)}, f32[16,8,4,128]{3,2,1,0:T(4,128)S(1)}, u32[]{:S(2)}, u32[]{:S(2)}) collective-permute-start(f32[16,8,4,128]{3,2,1,0:T(4,128)} %get-tuple-element.50), channel_id=1, source_target_pairs={{4,16},{8,20},{12,24},{20,0},{24,4},{28,8},{5,17},{9,21},{13,25},{... | collective-permute-start | bytes 786440 | tf_op jit(solution)/shard_map/ppermute | solution.py:56
  58.7 6.7 %copy-start.1 = (f32[18,8,4,128]{3,2,1,0:T(4,128)}, f32[18,8,4,128]{3,2,1,0:T(4,128)S(1)}, u32[]{:S(2)}) copy-start(f32[18,8,4,128]{3,2,1,0:T(4,128)S(1)} %collective-permute-done.5.refs_4_) | copy-start | bytes 884740
  58.7 65.7 %collective-permute-start = (f32[16,4,64,128]{3,2,1,0:T(8,128)S(1)}, f32[16,4,64,128]{3,2,1,0:T(8,128)}, u32[]{:S(2)}, u32[]{:S(2)}) collective-permute-start(f32[16,4,64,128]{3,2,1,0:T(8,128)S(1)} %constant_dynamic-slice_fusion.7), channel_id=1, source_target_pairs={{0,16},{16,0},{1,17},{17,1},{2,18},{18,2},{3,19},{19,3},{4,20},{20... | collective-permute-start | bytes 6291464 | tf_op jit(solution)/shard_map/ppermute | solution.py:46
  61.0 4.4 %copy-start.2 = (f32[16,8,4,128]{3,2,1,0:T(4,128)}, f32[16,8,4,128]{3,2,1,0:T(4,128)S(1)}, u32[]{:S(2)}) copy-start(f32[16,8,4,128]{3,2,1,0:T(4,128)S(1)} %collective-permute-done.4.refs_3_) | copy-start | bytes 786436
  65.4 0.7 copy-start.3
  71.3 18.2 %collective-permute-start.14 = (f32[1,40,8,128]{3,2,1,0:T(8,128)}, f32[1,40,8,128]{3,2,1,0:T(8,128)}, u32[]{:S(2)}, u32[]{:S(2)}) collective-permute-start(f32[1,40,8,128]{3,2,1,0:T(8,128)} %get-tuple-element.30), channel_id=1, source_target_pairs={{1,0},{2,1},{3,2},{5,4},{6,5},{7,6},{9,8},{10,9},{11,10},{13,12},{... | collective-permute-start | bytes 491528 | tf_op jit(solution)/shard_map/ppermute | solution.py:41
  72.6 16.9 %collective-permute-start.15 = (f32[1,40,8,128]{3,2,1,0:T(8,128)}, f32[1,40,8,128]{3,2,1,0:T(8,128)}, u32[]{:S(2)}, u32[]{:S(2)}) collective-permute-start(f32[1,40,8,128]{3,2,1,0:T(8,128)} %get-tuple-element.31), channel_id=1, source_target_pairs={{0,1},{1,2},{2,3},{4,5},{5,6},{6,7},{8,9},{9,10},{10,11},{12,13},{... | collective-permute-start | bytes 491528 | tf_op jit(solution)/shard_map/ppermute | solution.py:41
  84.4 51.4 %collective-permute-start.11 = (f32[1,40,8,128]{3,2,1,0:T(8,128)}, f32[1,40,8,128]{3,2,1,0:T(8,128)}, u32[]{:S(2)}, u32[]{:S(2)}) collective-permute-start(f32[1,40,8,128]{3,2,1,0:T(8,128)} %get-tuple-element.27), channel_id=1, source_target_pairs={{1,0},{2,1},{3,2},{5,4},{6,5},{7,6},{9,8},{10,9},{11,10},{13,12},{... | collective-permute-start | bytes 491528 | tf_op jit(solution)/shard_map/ppermute | solution.py:41
  85.7 50.1 %collective-permute-start.12 = (f32[1,40,8,128]{3,2,1,0:T(8,128)}, f32[1,40,8,128]{3,2,1,0:T(8,128)}, u32[]{:S(2)}, u32[]{:S(2)}) collective-permute-start(f32[1,40,8,128]{3,2,1,0:T(8,128)} %get-tuple-element.28), channel_id=1, source_target_pairs={{0,1},{1,2},{2,3},{4,5},{5,6},{6,7},{8,9},{9,10},{10,11},{12,13},{... | collective-permute-start | bytes 491528 | tf_op jit(solution)/shard_map/ppermute | solution.py:41
  123.8 119.8 %collective-permute-start.19 = (f32[16,2,64,128]{3,2,1,0:T(8,128)}, f32[16,2,64,128]{3,2,1,0:T(8,128)S(1)}, u32[]{:S(2)}, u32[]{:S(2)}) collective-permute-start(f32[16,2,64,128]{3,2,1,0:T(8,128)} %get-tuple-element.38), channel_id=1, source_target_pairs={{0,16},{16,0},{1,17},{17,1},{2,18},{18,2},{3,19},{19,3},{4,20},{20... | collective-permute-start | bytes 3145736 | tf_op jit(solution)/shard_map/ppermute | solution.py:46
  131.2 40.6 %collective-permute-start.7 = (f32[2,40,8,128]{3,2,1,0:T(8,128)}, f32[2,40,8,128]{3,2,1,0:T(8,128)S(1)}, u32[]{:S(2)}, u32[]{:S(2)}) collective-permute-start(f32[2,40,8,128]{3,2,1,0:T(8,128)} %get-tuple-element.24), channel_id=1, source_target_pairs={{1,0},{2,1},{3,2},{5,4},{6,5},{7,6},{9,8},{10,9},{11,10},{13,12},{... | collective-permute-start | bytes 983048 | tf_op jit(solution)/shard_map/ppermute | solution.py:41
  132.5 39.3 %collective-permute-start.8 = (f32[2,40,8,128]{3,2,1,0:T(8,128)}, f32[2,40,8,128]{3,2,1,0:T(8,128)S(1)}, u32[]{:S(2)}, u32[]{:S(2)}) collective-permute-start(f32[2,40,8,128]{3,2,1,0:T(8,128)} %get-tuple-element.25), channel_id=1, source_target_pairs={{0,1},{1,2},{2,3},{4,5},{5,6},{6,7},{8,9},{9,10},{10,11},{12,13},{... | collective-permute-start | bytes 983048 | tf_op jit(solution)/shard_map/ppermute | solution.py:41
  170.3 76.5 %collective-permute-start.18 = (f32[16,2,64,128]{3,2,1,0:T(8,128)}, f32[16,2,64,128]{3,2,1,0:T(8,128)S(1)}, u32[]{:S(2)}, u32[]{:S(2)}) collective-permute-start(f32[16,2,64,128]{3,2,1,0:T(8,128)} %get-tuple-element.37), channel_id=1, source_target_pairs={{0,16},{16,0},{1,17},{17,1},{2,18},{18,2},{3,19},{19,3},{4,20},{20... | collective-permute-start | bytes 3145736 | tf_op jit(solution)/shard_map/ppermute | solution.py:46
  171.8 0.7 copy-start.15
  171.8 0.8 copy-start.16
  207.0 43.9 %collective-permute-start.17 = (f32[16,2,64,128]{3,2,1,0:T(8,128)}, f32[16,2,64,128]{3,2,1,0:T(8,128)S(1)}, u32[]{:S(2)}, u32[]{:S(2)}) collective-permute-start(f32[16,2,64,128]{3,2,1,0:T(8,128)} %get-tuple-element.36), channel_id=1, source_target_pairs={{0,16},{16,0},{1,17},{17,1},{2,18},{18,2},{3,19},{19,3},{4,20},{20... | collective-permute-start | bytes 3145736 | tf_op jit(solution)/shard_map/ppermute | solution.py:46
  242.0 25.9 %collective-permute-start.16 = (f32[16,2,64,128]{3,2,1,0:T(8,128)}, f32[16,2,64,128]{3,2,1,0:T(8,128)}, u32[]{:S(2)}, u32[]{:S(2)}) collective-permute-start(f32[16,2,64,128]{3,2,1,0:T(8,128)} %get-tuple-element.35), channel_id=1, source_target_pairs={{0,16},{16,0},{1,17},{17,1},{2,18},{18,2},{3,19},{19,3},{4,20},{20... | collective-permute-start | bytes 3145736 | tf_op jit(solution)/shard_map/ppermute | solution.py:46
  243.6 1.0 copy-start.4
  246.8 3.3 %copy-start.7 = (f32[2,64,128]{2,1,0:T(8,128)S(1)}, f32[2,64,128]{2,1,0:T(8,128)}, u32[]{:S(2)}) copy-start(f32[2,64,128]{2,1,0:T(8,128)} %get-tuple-element.40) | copy-start | bytes 196612
  246.8 3.3 %copy-start.8 = (f32[2,64,128]{2,1,0:T(8,128)S(1)}, f32[2,64,128]{2,1,0:T(8,128)}, u32[]{:S(2)}) copy-start(f32[2,64,128]{2,1,0:T(8,128)} %get-tuple-element.41) | copy-start | bytes 196612
  246.8 3.3 %copy-start.9 = (f32[2,64,128]{2,1,0:T(8,128)S(1)}, f32[2,64,128]{2,1,0:T(8,128)}, u32[]{:S(2)}) copy-start(f32[2,64,128]{2,1,0:T(8,128)} %get-tuple-element.42) | copy-start | bytes 196612
  246.8 3.3 %copy-start.10 = (f32[2,64,128]{2,1,0:T(8,128)S(1)}, f32[2,64,128]{2,1,0:T(8,128)}, u32[]{:S(2)}) copy-start(f32[2,64,128]{2,1,0:T(8,128)} %get-tuple-element.43) | copy-start | bytes 196612
  246.8 1.0 copy-start.5
  250.9 1.0 copy-start.6
